TPU v7x, 128 devices: a whole 4x4x4 slice. The times are simulated.
128 devices in a mesh: head: 4 (over y_hi, core), req: 32 (over z, x, y_lo).
Axes of the slice: x: 4, y: 4 (y_hi: 2, y_lo: 2; y = y_hi * 2 + y_lo), z: 4, core: 2. Of those that a mesh axis runs over, the one named last changes fastest.
Arguments:
- learner_acceptance_matrix: float32 [2048, 2048], P(('head', 'req')), may hold values from -0.125 to 0.125
- learner_address_matrix: float32 [2048, 2048], P(('head', 'req')), may hold values from -0.125 to 0.125
- learner_content_matrix: float32 [2048, 2048], P(('head', 'req')), may hold values from -0.125 to 0.125
- learner_gating_matrix: float32 [2048, 2048], P(('head', 'req')), may hold values from -0.125 to 0.125
- learner_result_matrix: float32 [2048, 2048], P(('head', 'req')), may hold values from -0.125 to 0.125
- fading_narrowing_matrix: bfloat16 [2048, 64], replicated, may hold values from -0.125 to 0.125
- fading_widening_matrix: bfloat16 [64, 2048], P(None, 'head'), may hold values from -0.75 to 0.75
- feature_fading_speed: float32 [2048], P('head'), may hold values from 0.001 to 0.5
- current_reward: float32 [2048], P('head'), may hold values from -1 to 1
- symbol_blending_factors: float32 [5, 2048], replicated, may hold values from 0 to 1
- group_scaling_factor: float32 [2048], P('head'), may hold values from 0.5 to 1.5
- group_scaling_offset: float32 [2048], P('head'), may hold values from -1.75 to 1.75
- request_hidden_entries: bfloat16 [64, 512, 2048], P('req', None, 'head'), may hold values from -6 to 6
- request_valid_count: int32 [64], P('req'), may hold values from 1 to 512, 24576 in all
- request_destination_place: int32 [64], P('req'), may hold values from 0 to 2047, as said below
- newest_symbol_hidden: bfloat16 [2048, 2048], P('req', 'head'), may hold values from -6 to 6
- preceding_hidden_entry: bfloat16 [2048, 2048], P('req', 'head'), may hold values from -6 to 6
- place_memory_matrix: float32 [2048, 32, 64, 64], P('req', 'head'), may hold values from -6 to 6
- place_newness_marks: int32 [2048], P('req'), may hold values 0 or 1
Outputs:
- prompt_hidden: bfloat16 [64, 512, 2048], P('req', None, 'head')
- decode_hidden: bfloat16 [2048, 2048], P('req', 'head')
- new_state: float32 [2048, 32, 64, 64], P('req', 'head')
- new_shift: bfloat16 [2048, 2048], P('req', 'head')
Inputs may be any that keep to these rules, and one draw needn't show every extreme that they name: Prompt p's slot is one of the 64 slots of the same index of req as prompt p, that is p // 2 == request_destination_place[p] // 64; the slots are distinct. `request_valid_count`: the longest prompt has exactly 512 live tokens.
All inputs are finite; a program needn't handle non-finite values. No bound on the sum of `request_valid_count` or of `place_newness_marks` on one device may be relied on, other than what follows from the above.
Results may differ from a plain program's by a relative error of at most 0.033.
Values may be sent and summed in bfloat16 or wider, within the bound.
No kernel may reach another device: no remote copies, remote signals or barrier semaphores. Data moves between devices by JAX's collectives and lax.ppermute only.
A program may use at most 256 MiB of HBM per device.

v0:
```python
import jax
import jax.numpy as jnp
from jax import lax
from jax.sharding import PartitionSpec as P

NORM_EPS = 0.00064


def project(left, right):
    return jnp.dot(left, right, preferred_element_type=jnp.float32)


def make_inputs(
    present,
    earlier,
    symbol_blending_factors,
    w_recept,
    w_key,
    w_value,
    w_gate,
    fading_narrowing_matrix,
    fading_widening_matrix,
    feature_fading_speed,
):
    current = present.astype(jnp.float32)
    previous = earlier.astype(jnp.float32)
    mixed_rows = [
        (current + (previous - current) * symbol_blending_factors[number]).astype(jnp.bfloat16)
        for number in range(5)
    ]
    acceptance_entries = project(mixed_rows[0], w_recept).astype(jnp.bfloat16)
    address_entry_tile = project(mixed_rows[1], w_key).astype(jnp.bfloat16)
    content_entries = project(mixed_rows[2], w_value).astype(jnp.bfloat16)
    lowrank = jnp.tanh(project(mixed_rows[3], fading_narrowing_matrix)).astype(jnp.bfloat16)
    fading_exponent_log = -feature_fading_speed * jnp.exp(project(lowrank, fading_widening_matrix))
    gate_rows = jax.nn.silu(project(mixed_rows[4], w_gate))
    return (
        acceptance_entries.astype(jnp.float32),
        address_entry_tile.astype(jnp.float32),
        content_entries.astype(jnp.float32),
        fading_exponent_log,
        gate_rows,
    )


def group_norm(outputs, group_scaling_factor, group_scaling_offset, gate_rows):
    center = outputs - jnp.mean(outputs, axis=-1, keepdims=True)
    spread = jnp.mean(center * center, axis=-1, keepdims=True)
    normed = (center / jnp.sqrt(spread + NORM_EPS)).reshape(outputs.shape[0], -1)
    return ((normed * group_scaling_factor + group_scaling_offset) * gate_rows).astype(jnp.bfloat16)


def span_recurrence(
    acceptance_entries,
    address_entry_tile,
    content_entries,
    fading_exponent_log,
    group_reward,
    segment_tile_extent,
):
    prompt_count, length, owned_groups, group_breadth = acceptance_entries.shape
    spans = length // segment_tile_extent

    def blocked(array):
        return array.reshape(
            prompt_count, spans, segment_tile_extent, owned_groups, group_breadth
        ).transpose(1, 0, 2, 3, 4)

    row_ids = lax.broadcasted_iota(jnp.int32, (segment_tile_extent, segment_tile_extent), 0)
    col_ids = lax.broadcasted_iota(jnp.int32, (segment_tile_extent, segment_tile_extent), 1)
    lower_mask = (row_ids > col_ids)[None, :, :, None, None]

    def advance(running_memory, inputs):
        acceptance_array, address_array, content_array, w = inputs
        inclusive = jnp.cumsum(w, axis=1)
        exclusive = inclusive - w
        carried_part = jnp.einsum(
            "pthd,phde->pthe",
            acceptance_array * jnp.exp(exclusive),
            running_memory,
            precision=lax.Precision.HIGHEST,
        )
        exponent = exclusive[:, :, None] - inclusive[:, None, :]
        weights = jnp.where(lower_mask, jnp.exp(jnp.where(lower_mask, exponent, 0.0)), 0.0)
        scores = jnp.einsum(
            "pthd,pjhd,ptjhd->phtj",
            acceptance_array,
            address_array,
            weights,
            precision=lax.Precision.HIGHEST,
        )
        local_part = jnp.einsum(
            "phtj,pjhe->pthe", scores, content_array, precision=lax.Precision.HIGHEST
        )
        diagonal_term = (
            jnp.sum(acceptance_array * group_reward * address_array, axis=-1, keepdims=True)
            * content_array
        )
        span_total = inclusive[:, -1]
        carried = address_array * jnp.exp(span_total[:, None] - inclusive)
        next_state = jnp.exp(span_total)[..., None] * running_memory + jnp.einsum(
            "pjhd,pjhe->phde", carried, content_array, precision=lax.Precision.HIGHEST
        )
        return (next_state, carried_part + local_part + diagonal_term)

    start_state = jnp.zeros((prompt_count, owned_groups, group_breadth, group_breadth), jnp.float32)
    final_state, outputs = lax.scan(
        advance,
        start_state,
        (
            blocked(acceptance_entries),
            blocked(address_entry_tile),
            blocked(content_entries),
            blocked(fading_exponent_log),
        ),
    )
    return (
        final_state,
        outputs.transpose(1, 0, 2, 3, 4).reshape(
            prompt_count * length, owned_groups, group_breadth
        ),
    )


def on_device(
    learner_acceptance_matrix,
    learner_address_matrix,
    learner_content_matrix,
    learner_gating_matrix,
    learner_result_matrix,
    fading_narrowing_matrix,
    fading_widening_matrix,
    feature_fading_speed,
    current_reward,
    symbol_blending_factors,
    group_scaling_factor,
    group_scaling_offset,
    request_hidden_entries,
    request_valid_count,
    request_destination_place,
    newest_symbol_hidden,
    preceding_hidden_entry,
    place_memory_matrix,
    place_newness_marks,
):
    model_width = symbol_blending_factors.shape[1]
    block_cols = feature_fading_speed.shape[0]
    owned_groups = place_memory_matrix.shape[1]
    group_breadth = place_memory_matrix.shape[2]
    slot_count = place_memory_matrix.shape[0]
    casted = (
        learner_acceptance_matrix.astype(jnp.bfloat16),
        learner_address_matrix.astype(jnp.bfloat16),
        learner_content_matrix.astype(jnp.bfloat16),
        learner_gating_matrix.astype(jnp.bfloat16),
    )
    whole_rows = (
        lax.all_gather(casted[0], ("head", "req"), axis=0, tiled=True),
        lax.all_gather(casted[1], ("head", "req"), axis=0, tiled=True),
        lax.all_gather(casted[2], ("head", "req"), axis=0, tiled=True),
        lax.all_gather(casted[3], ("head", "req"), axis=0, tiled=True),
    )
    column_start = lax.axis_index("head") * block_cols
    blocks = [
        lax.dynamic_slice_in_dim(matrix, column_start, block_cols, 1) for matrix in whole_rows
    ]
    w_recept, w_key, w_value, w_gate = blocks
    w_output = lax.all_gather(learner_result_matrix.astype(jnp.bfloat16), "req", axis=0, tiled=True)
    group_reward = current_reward.reshape(owned_groups, group_breadth)
    prompt_full, decode_full, shift_full = (
        lax.all_gather(request_hidden_entries, "head", axis=2, tiled=True),
        lax.all_gather(newest_symbol_hidden, "head", axis=1, tiled=True),
        lax.all_gather(preceding_hidden_entry, "head", axis=1, tiled=True),
    )
    prompt_count, length = (prompt_full.shape[0], prompt_full.shape[1])
    earlier = jnp.concatenate([jnp.zeros_like(prompt_full[:, :1]), prompt_full[:, :-1]], axis=1)
    acceptance_entries, address_entry_tile, content_entries, fading_exponent_log, gate_rows = (
        make_inputs(
            prompt_full.reshape(-1, model_width),
            earlier.reshape(-1, model_width),
            symbol_blending_factors,
            w_recept,
            w_key,
            w_value,
            w_gate,
            fading_narrowing_matrix,
            fading_widening_matrix,
            feature_fading_speed,
        )
    )
    positions = lax.broadcasted_iota(jnp.int32, (prompt_count, length), 1)
    live_mask = (positions < request_valid_count[:, None]).astype(jnp.float32).reshape(-1, 1)
    address_entry_tile = address_entry_tile * live_mask
    fading_exponent_log = fading_exponent_log * live_mask

    def heads_view(array):
        return array.reshape(prompt_count, length, owned_groups, group_breadth)

    final_state, outputs = span_recurrence(
        heads_view(acceptance_entries),
        heads_view(address_entry_tile),
        heads_view(content_entries),
        heads_view(fading_exponent_log),
        group_reward,
        min(32, length),
    )
    prompt_part = project(
        group_norm(outputs, group_scaling_factor, group_scaling_offset, gate_rows), w_output
    )
    fresh_mask = place_newness_marks == 1
    prior = jnp.where(fresh_mask[:, None], jnp.zeros_like(shift_full), shift_full)
    acceptance_each_group, address_each_group, value_per_head, decay_d, gate_d = make_inputs(
        decode_full,
        prior,
        symbol_blending_factors,
        w_recept,
        w_key,
        w_value,
        w_gate,
        fading_narrowing_matrix,
        fading_widening_matrix,
        feature_fading_speed,
    )
    acceptance_each_group = acceptance_each_group.reshape(-1, owned_groups, group_breadth)
    address_each_group = address_each_group.reshape(-1, owned_groups, group_breadth)
    value_per_head = value_per_head.reshape(-1, owned_groups, group_breadth)
    decay_d = decay_d.reshape(-1, owned_groups, group_breadth)
    begin_state = jnp.where(
        fresh_mask[:, None, None, None], jnp.zeros_like(place_memory_matrix), place_memory_matrix
    )
    decode_out = (
        jnp.einsum(
            "lkh,lkhs->lks", acceptance_each_group, begin_state, precision=lax.Precision.HIGHEST
        )
        + jnp.sum(acceptance_each_group * group_reward * address_each_group, axis=-1, keepdims=True)
        * value_per_head
    )
    next_state = (
        jnp.exp(decay_d)[..., None] * begin_state
        + address_each_group[..., :, None] * value_per_head[..., None, :]
    )
    decode_part = project(
        group_norm(decode_out, group_scaling_factor, group_scaling_offset, gate_d), w_output
    )
    prompt_sum, decode_sum = (
        lax.psum_scatter(
            prompt_part.reshape(prompt_count, length, model_width).astype(jnp.bfloat16),
            "head",
            scatter_dimension=2,
            tiled=True,
        ).astype(jnp.float32),
        lax.psum_scatter(
            decode_part.astype(jnp.bfloat16), "head", scatter_dimension=1, tiled=True
        ).astype(jnp.float32),
    )
    prompt_hidden = (prompt_sum * live_mask.reshape(prompt_count, length, 1)).astype(jnp.bfloat16)
    select = (positions == request_valid_count[:, None] - 1).astype(jnp.float32)
    last_tokens = jnp.sum(
        request_hidden_entries.astype(jnp.float32) * select[..., None], axis=1
    ).astype(jnp.bfloat16)
    first_slot = lax.axis_index("req") * slot_count
    offsets = request_destination_place - first_slot
    slot_ids = lax.broadcasted_iota(jnp.int32, (slot_count,), 0)
    new_state = next_state
    new_shift = newest_symbol_hidden
    prompt_taken = jnp.zeros((slot_count,), jnp.bool_)
    for prompt_index in range(prompt_count):
        slot_hit = slot_ids == offsets[prompt_index]
        new_state = jnp.where(slot_hit[:, None, None, None], final_state[prompt_index], new_state)
        new_shift = jnp.where(slot_hit[:, None], last_tokens[prompt_index], new_shift)
        prompt_taken = prompt_taken | slot_hit
    decode_hidden = jnp.where(prompt_taken[:, None], 0.0, decode_sum).astype(jnp.bfloat16)
    return (prompt_hidden, decode_hidden, new_state, new_shift)


def solution(mesh):
    in_specs = (
        P(("head", "req"), None),
        P(("head", "req"), None),
        P(("head", "req"), None),
        P(("head", "req"), None),
        P(("head", "req"), None),
        P(),
        P(None, "head"),
        P("head"),
        P("head"),
        P(),
        P("head"),
        P("head"),
        P("req", None, "head"),
        P("req"),
        P("req"),
        P("req", "head"),
        P("req", "head"),
        P("req", "head", None, None),
        P("req"),
    )
    out_specs = (
        P("req", None, "head"),
        P("req", "head"),
        P("req", "head", None, None),
        P("req", "head"),
    )
    return jax.shard_map(
        on_device, mesh=mesh, in_specs=in_specs, out_specs=out_specs, check_vma=False
    )
```

profile of v0, /device:TPU:1, one launch (start us, length us, event | category | flops | bytes accessed | tf_op | source)
XLA Modules:
  0.0 1562.1 jit_solution(9432620819879721345)
XLA Ops:
  20.6 10.3 all_gather.31
  30.9 9.5 all_gather.30
  40.4 13.7 all-gather.7.cloned.1.call-done
  73.8 294.9 %all-gather.9.cloned.1.call-done = bf16[2048,2048]{1,0:T(8,128)(2,1)} async-done(((bf16[16,2048]{1,0:T(8,128)(2,1)}), bf16[2048,2048]{1,0:T(8,128)(2,1)}) %all-gather.9.cloned.1.call-update) | async-done | bytes 8388624 | tf_op jit(solution)/shard_map/all_gather | solution.py:159
  368.7 6.4 convert_multiply_fusion
  377.6 305.9 %all-gather.13.cloned.1.call-done = bf16[2048,2048]{1,0:T(8,128)(2,1)} async-done(((bf16[16,2048]{1,0:T(8,128)(2,1)}), bf16[2048,2048]{1,0:T(8,128)(2,1)}) %all-gather.13.cloned.1.call-update) | async-done | bytes 8388624 | tf_op jit(solution)/shard_map/all_gather | solution.py:158
  683.5 6.4 fusion.81
  692.4 305.1 %all-gather.11.cloned.1.call-done = bf16[2048,2048]{1,0:T(8,128)(2,1)} async-done(((bf16[16,2048]{1,0:T(8,128)(2,1)}), bf16[2048,2048]{1,0:T(8,128)(2,1)}) %all-gather.11.cloned.1.call-update) | async-done | bytes 8388624 | tf_op jit(solution)/shard_map/all_gather | solution.py:160
  997.5 6.4 fusion.71
  1016.3 281.9 %while.14 = (s32[]{:T(128)}, f32[2,8,64,64]{3,2,1,0:T(8,128)S(1)}, f32[16,2,32,8,64]{4,2,3,1,0:T(8,128)}, f32[16,2,32,8,64]{4,3,2,1,0:T(8,128)}, f32[16,2,32,8,6...) while((s32[]{:T(128)}, f32[2,8,64,64]{3,2,1,0:T(8,128)S(1)}, ...), condition=%wide.region_3.4_spmd.clone.clone, body=%wide.region_0.3_spmd.clone.clone.sunk | while | flops 70795776 | bytes 13804680 | solution.py:107
  1024.7 7.0 fusion.205
  1042.3 7.0 fusion.205
  1059.9 7.0 fusion.205
  1077.5 7.0 fusion.205
  1095.1 7.0 fusion.205
  1112.6 7.0 fusion.205
  1130.2 7.0 fusion.205
  1147.8 7.0 fusion.205
  1165.3 7.0 fusion.205
  1182.9 7.0 fusion.205
  1200.5 7.0 fusion.205
  1218.1 7.0 fusion.205
  1235.6 7.0 fusion.205
  1253.2 7.0 fusion.205
  1270.8 7.0 fusion.205
  1288.4 7.0 fusion.205
  1305.2 11.3 fusion.28
  1327.1 139.9 %all-gather.15.cloned.1.call-done = bf16[2048,2048]{1,0:T(8,128)(2,1)} async-done(((bf16[16,2048]{1,0:T(8,128)(2,1)}), bf16[2048,2048]{1,0:T(8,128)(2,1)}) %all-gather.15.cloned.1.call-update) | async-done | bytes 8388624 | tf_op jit(solution)/shard_map/all_gather | solution.py:161
  1475.7 8.0 copy.67
  1488.6 13.0 convolution_convert_fusion
  1506.6 17.1 %select_select_fusion = f32[64,8,64,64]{3,2,1,0:T(8,128)} fusion(f32[64,8,64,64]{3,2,1,0:T(8,128)} %param.38, f32[64,8,64]{2,1,0:T(8,128)S(1)} %copy-done.10, f32[64,8,64]{2,1,0:T(8,128)S(1)} %copy-done.8, f32[64,8,64]{2,1,0:T(8,128)S(1)} %exp.45, f32[8,64,64]{2,1,0:T(8,128)S(1)} %get-tuple-element.135, f32[8,64,64]{2,1,0:T(8,128)S(1)} %get-tuple-element.134, ...), kind=kLoop, calls=%fused_computation.47 | loop fusion | flops 12582912 | bytes 17432768 | tf_op jit(solution)/shard_map/jit(_where)/select_n | solution.py:269
  1525.2 27.4 %reduce-scatter.3.cloned.1.call-done = bf16[2,512,512]{2,1,0:T(8,128)(2,1)} async-done(((bf16[2,512,2048]{2,1,0:T(8,128)(2,1)}), bf16[2,512,512]{2,1,0:T(8,128)(2,1)}) %reduce-scatter.3.cloned.1.call-update) | async-done | bytes 1048592 | tf_op jit(solution)/shard_map/reduce_scatter | solution.py:246
  (358 shorter events, 258.2 us)
Async XLA Ops:
  7.2 55.4 %copy-start = (bf16[2048,64]{0,1:T(8,128)(2,1)S(1)}, bf16[2048,64]{0,1:T(8,128)(2,1)}, u32[]{:S(2)}) copy-start(bf16[2048,64]{0,1:T(8,128)(2,1)} %param.26) | copy-start | bytes 786436
  7.2 46.9 %all-gather.7.cloned.1.call-start = ((), (), s32[]{:S(2)}) async-start(), calls=%async_computation.2 | async-start | bytes 5242880 | tf_op jit(solution)/shard_map/all_gather | solution.py:171
  7.9 360.8 %all-gather.9.cloned.1.call-start = ((), (), s32[]{:S(2)}) async-start(), calls=%async_computation.3 | async-start | bytes 8454144 | tf_op jit(solution)/shard_map/all_gather | solution.py:159
  9.5 673.9 %all-gather.13.cloned.1.call-start = ((), (), s32[]{:S(2)}) async-start(), calls=%async_computation.5 | async-start | bytes 8454144 | tf_op jit(solution)/shard_map/all_gather | solution.py:158
  11.1 986.3 %all-gather.11.cloned.1.call-start = ((), (), s32[]{:S(2)}) async-start(), calls=%async_computation.4 | async-start | bytes 8454144 | tf_op jit(solution)/shard_map/all_gather | solution.py:160
  12.8 1314.3 %all-gather.17.cloned.1.call-start = ((), (), s32[]{:S(2)}) async-start(), calls=%async_computation.7 | async-start | bytes 2162688 | tf_op jit(solution)/shard_map/all_gather | solution.py:168
  14.4 1452.7 %all-gather.15.cloned.1.call-start = ((), (), s32[]{:S(2)}) async-start(), calls=%async_computation.6 | async-start | bytes 8454144 | tf_op jit(solution)/shard_map/all_gather | solution.py:161
  16.0 1507.7 %reduce-scatter.5.cloned.1.call-start = ((), (), s32[]{:S(2)}) async-start(), calls=%async_computation.9 | async-start | bytes 327680 | tf_op jit(solution)/shard_map/reduce_scatter | solution.py:252
  16.7 1450.3 %copy-start.15 = (pred[64]{0:T(512)(128)(4,1)}, pred[64]{0:T(512)(128)(4,1)S(1)}, u32[]{:S(2)}) copy-start(pred[64]{0:T(512)(128)(4,1)S(1)} %broadcast_compare_fusion) | copy-start | bytes 196
  17.4 45.2 %copy-start.18 = (f32[512]{0:T(512)}, f32[512]{0:T(512)S(1)}, u32[]{:S(2)}) copy-start(f32[512]{0:T(512)S(1)} %neg.12) | copy-start | bytes 6148
  54.1 3.5 copy-start.2
  57.6 5.0 copy-start.3
  57.6 5.0 copy-start.14
  1006.2 5.3 copy-start.4
  1006.2 6.3 copy-start.5
  1012.5 3.8 copy-start.13
  1302.9 13.6 copy-start.7
  1305.2 11.3 copy-start.9
  1321.1 3.6 copy-start.1
  1321.1 146.0 %copy-start.20 = (f32[512]{0:T(512)S(1)}, f32[512]{0:T(512)}, u32[]{:S(2)}) copy-start(f32[512]{0:T(512)} %param.32) | copy-start | bytes 6148
  1321.1 146.0 %copy-start.22 = (f32[512]{0:T(512)S(1)}, f32[512]{0:T(512)}, u32[]{:S(2)}) copy-start(f32[512]{0:T(512)} %param.31) | copy-start | bytes 6148
  1471.0 81.6 %reduce-scatter.3.cloned.1.call-start = ((), (), s32[]{:S(2)}) async-start(), calls=%async_computation.8 | async-start | bytes 5242880 | tf_op jit(solution)/shard_map/reduce_scatter | solution.py:246
  1483.6 4.9 copy-start.11
  1483.6 4.9 copy-start.21
  1483.6 4.9 copy-start.23
  1501.5 1.3 copy-start.25
  1501.5 3.8 copy-start.24
  1501.5 3.9 copy-start.6
  1501.5 4.2 copy-start.12
  1501.6 5.0 copy-start.8
  1501.6 5.0 copy-start.10
  1506.6 46.0 %copy-start.17 = (f32[2,512]{1,0:T(2,128)S(1)}, f32[2,512]{1,0:T(2,128)}, u32[]{:S(2)}) copy-start(f32[2,512]{1,0:T(2,128)} %get-tuple-element.143) | copy-start | bytes 12292
  (2 other events, 1.3 us)
Sparse Core Ops, SparseCore 0:
  9.7 44.3 all-gather.6
  56.4 312.3 all-gather.8
  371.0 312.3 all-gather.12
  685.0 312.4 all-gather.10
  999.5 132.9 all-gather.16
  1134.1 332.8 all-gather.14
  1471.1 26.2 reduce-scatter.4
  1501.7 50.8 reduce-scatter.2
where the time goes:
time: 1570 us; the launch traced here: 1560 us
  waiting for transfers between devices  1090 us (69%)
  other arithmetic  227 us (14%)
  matrix products  140 us (9%)
  local copies, waits for them, and re-layouts  70.7 us (5%)
  blocking collectives  19.8 us (1%)
    all_gather x1, waiting for transfers between devices, on_device(): lax.all_gather(casted[0], ('head', 'req'), axis=0, tiled=True)  306 us
    all_gather x1, waiting for transfers between devices, on_device(): lax.all_gather(casted[2], ('head', 'req'), axis=0, tiled=True)  305 us
    all_gather x1, waiting for transfers between devices, on_device(): lax.all_gather(casted[1], ('head', 'req'), axis=0, tiled=True)  295 us
    all_gather x1, waiting for transfers between devices, on_device(): lax.all_gather(casted[3], ('head', 'req'), axis=0, tiled=True)  140 us
    dot_general x16, other arithmetic, advance(): jnp.einsum('pthd,pjhd,ptjhd->phtj', acceptance_array, address_array, weig...  112 us
    dot_general x10, matrix products, project(): return jnp.dot(left, right, preferred_element_type=jnp.float32)  47 us
    dot_general x16, matrix products, advance(): jnp.einsum('phtj,pjhe->pthe', scores, content_array, precision=lax.Precis...  38 us
    dot_general x16, matrix products, advance(): jnp.einsum('pjhd,pjhe->phde', carried, content_array, precision=lax.Preci...  33.8 us
  transfers between devices with their start and end apart: 8, of which 6 were waited for; matrix products, arithmetic and copies ran while one was open for 27% of the time, Pallas kernels for 0%

commit v1 on v0

v1 whole, which is shorter than its diff:
```python
import functools

import jax
import jax.numpy as jnp
import numpy as np
from jax import lax
from jax.experimental import pallas as pl
from jax.experimental.pallas import tpu as pltpu
from jax.sharding import Mesh
from jax.sharding import PartitionSpec as P

NORM_EPS = 0.00064
N_HEAD = 4
CH = 64
BF = jnp.bfloat16
F32 = jnp.float32


STEPS = (("x", 1), ("z", 1), ("x", 3), ("z", 3))


def swap(a, axes, bits):
    sizes = {"x": 4, "z": 4, "yl": 2, "head": 4}
    names = ("yh", "core") if axes == "head" else axes
    return lax.ppermute(a, names, [(i, i ^ bits) for i in range(sizes[axes])])


def order_of(part):
    return [STEPS[(part + n) % 4] for n in range(4)]


def after(value, other):
    return lax.optimization_barrier((value, other))[0]


def column_blocks(matrices, h):
    stacked = jnp.stack([m.astype(BF) for m in matrices])
    width = stacked.shape[2] // N_HEAD
    parts = [lax.dynamic_slice_in_dim(stacked, (h ^ d) * width, width, 2) for d in range(4)]
    return [parts[0]] + [swap(parts[d], "head", d) for d in (1, 2, 3)]


def with_neighbour(own, yl):
    other = swap(own, "yl", 1)
    first = yl == 0
    return jnp.concatenate(
        [jnp.where(first, own, other), jnp.where(first, other, own)], axis=-2
    )


ANY = pl.BlockSpec(memory_space=pl.ANY)


def cost(flops, nbytes, trans=0):
    return pl.CostEstimate(flops=flops, bytes_accessed=nbytes, transcendentals=trans)


def params(axes):
    return pltpu.CompilerParams(
        dimension_semantics=("arbitrary",) * axes, vmem_limit_bytes=48 << 20
    )


def axis_dim(axis):
    return 0 if axis == "z" else 1


def places(p, n, place_ref):
    axis, bits = order_of(p)[n]
    pos = place_ref[1] if axis == "z" else place_ref[2]
    seen = [b for name, b in order_of(p)[:n] if name == axis]
    offsets = [0] + seen
    return [pos ^ o for o in offsets], [pos ^ bits ^ o for o in offsets]


def part_of(ref, dim, i, lot):
    return ref.at[i, :, lot] if dim == 0 else ref.at[:, i, lot]


def pack_kernel(place_ref, *refs, n, lot):
    owns, recvs, outs, sem = refs[:4], refs[4:8], refs[8:12], refs[12]
    copies = []
    for p in range(4):
        dim = axis_dim(order_of(p)[n][0])
        own_at, recv_at = places(p, n, place_ref)
        if len(own_at) == 1:
            own_at, recv_at = [0], [1]
        for src, at in ((owns[p], own_at), (recvs[p], recv_at)):
            for i, j in enumerate(at):
                source = part_of(src, dim, i, lot)
                target = part_of(outs[p], dim, j, slice(None))
                copies.append(pltpu.make_async_copy(source, target, sem.at[len(copies)]))
    for copy in copies:
        copy.start()
    for copy in copies:
        copy.wait()


def pack(place, owns, recvs, n, lot):
    shapes = []
    for p in range(4):
        shape = list(owns[p].shape)
        shape[axis_dim(order_of(p)[n][0])] *= 2
        shape[2] = lot.stop - lot.start
        shapes.append(jax.ShapeDtypeStruct(tuple(shape), BF))
    return pl.pallas_call(
        functools.partial(pack_kernel, n=n, lot=lot),
        out_shape=shapes,
        grid_spec=pltpu.PrefetchScalarGridSpec(
            num_scalar_prefetch=1,
            grid=(1,),
            in_specs=[ANY] * 8,
            out_specs=[pl.BlockSpec(a.shape, lambda i, s: (0, 0, 0, 0, 0)) for a in shapes],
            scratch_shapes=[pltpu.SemaphoreType.DMA((16,))],
        ),
        compiler_params=params(1),
        cost_estimate=cost(0, 8 << 20),
        name="pack",
    )(place, *owns, *recvs)


def swap_all(owns, n):
    return [swap(owns[p], *order_of(p)[n]) for p in range(4)]


def copy_weights(pieces, m, place_ref, buf, sem):
    for p in range(4):
        dim = axis_dim(order_of(p)[3][0])
        own_at, recv_at = places(p, 3, place_ref)
        for src, at in ((pieces[p], own_at), (pieces[p + 4], recv_at)):
            for i, j in enumerate(at):
                target = buf.at[p * 4 + j] if dim == 0 else buf.at[pl.ds(p * 4, 4), j]
                pltpu.make_async_copy(part_of(src, dim, i, m), target, sem).start()


def wait_weights(buf, sem):
    pltpu.make_async_copy(buf, buf, sem).wait()


def mix_kernel(place_ref, count_ref, *refs, d, length):
    hid_ref, mu_ref, narrow_ref = refs[:3]
    refs = refs[3:]
    if d > 0:
        low_in, refs = refs[0], refs[2:]
    if d == 3:
        widen_ref, speed_ref, refs = refs[0], refs[1], refs[2:]
    x_ref, low_ref, cur_ref, step_ref = refs
    i = pl.program_id(0)
    rows = cur_ref.shape[0]
    slots = hid_ref.shape[0] - rows
    tokens = rows - slots

    @pl.when(i == 0)
    def _():
        cur = hid_ref[:rows].astype(F32)
        cur_ref[...] = cur
        seq = cur[:tokens]
        at = lax.broadcasted_iota(jnp.int32, seq.shape, 0)
        before = jnp.where((at & (length - 1)) == 0, 0.0, pltpu.roll(seq, 1, 0))
        step_ref[:tokens] = before - seq
        step_ref[tokens:] = hid_ref[rows:].astype(F32) - cur[tokens:]

    mixed = (cur_ref[...] + step_ref[...] * mu_ref[pl.ds(i, 1), :]).astype(BF)
    x_ref[0] = mixed

    @pl.when(i == 3)
    def _():
        low = jnp.dot(mixed, narrow_ref[...], preferred_element_type=F32)
        if d > 0:
            low = low + low_in[...]
        if d < 3:
            low_ref[...] = low
        else:
            lowrank = jnp.tanh(low).astype(BF)
            rate = jnp.exp(jnp.dot(lowrank, widen_ref[...], preferred_element_type=F32))
            log_decay = -speed_ref[...] * rate
            at = lax.broadcasted_iota(jnp.int32, (rows, 512), 0)
            limit = jnp.where(
                at < length,
                count_ref[0],
                jnp.where(at < 2 * length, count_ref[1] + length, rows),
            )
            low_ref[...] = jnp.where(at < limit, log_decay, 0.0)


def mix(place, counts, hidden, d, mu, narrow, low, held, widen, speed, slots, length):
    rows = hidden.shape[0] - slots
    once = lambda i, s, c: (0, 0)
    args = [hidden, mu, narrow]
    specs = [
        pl.BlockSpec(hidden.shape, once),
        pl.BlockSpec((5, 512), lambda i, s, c: (0, s[0] ^ d)),
        pl.BlockSpec((512, 64), lambda i, s, c: (s[0] ^ d, 0)),
    ]
    alias = {}
    if d > 0:
        args += [low, held]
        specs += [pl.BlockSpec(low.shape, once), ANY]
        alias = {6: 0}
    wide = 64
    if d == 3:
        args += [widen, speed]
        specs += [pl.BlockSpec(widen.shape, once), pl.BlockSpec(speed.shape, once)]
        wide = 512
    return pl.pallas_call(
        functools.partial(mix_kernel, d=d, length=length),
        out_shape=(
            jax.ShapeDtypeStruct((5, rows, 2048), BF),
            jax.ShapeDtypeStruct((rows, wide), F32),
        ),
        grid_spec=pltpu.PrefetchScalarGridSpec(
            num_scalar_prefetch=2,
            grid=(5,),
            in_specs=specs,
            out_specs=(
                pl.BlockSpec((1, rows, 512), lambda i, s, c: (i, 0, d)),
                pl.BlockSpec((rows, wide), once),
            ),
            scratch_shapes=[pltpu.VMEM((rows, 512), F32), pltpu.VMEM((rows, 512), F32)],
        ),
        input_output_aliases=alias,
        compiler_params=params(1),
        cost_estimate=cost(20 * rows * 512, 12 * rows * 512),
        name="mix",
    )(place, counts, *args)


def rkv_kernel(place_ref, x_ref, *refs):
    pieces = refs[:8]
    out_ref, buf, sem = refs[8:]
    i, j = pl.program_id(0), pl.program_id(1)
    slot = lax.rem(i, 2)

    @pl.when(jnp.logical_and(i == 0, j == 0))
    def _():
        copy_weights(pieces, 0, place_ref, buf.at[0], sem.at[0])

    @pl.when(j == 0)
    def _():
        @pl.when(i < 2)
        def _():
            copy_weights(pieces, i + 1, place_ref, buf.at[1 - slot], sem.at[1 - slot])

        wait_weights(buf.at[slot], sem.at[slot])

    w = buf[slot].reshape(2048, 512)
    out_ref[0] = jnp.dot(x_ref[0], w, preferred_element_type=F32).astype(out_ref.dtype)


def project_rkv(place, mixed, pieces, tile):
    rows = mixed.shape[1]
    return pl.pallas_call(
        rkv_kernel,
        out_shape=jax.ShapeDtypeStruct((3, rows, 512), BF),
        grid_spec=pltpu.PrefetchScalarGridSpec(
            num_scalar_prefetch=1,
            grid=(3, rows // tile),
            in_specs=[pl.BlockSpec((1, tile, 2048), lambda i, j, s: (i, j, 0))] + [ANY] * 8,
            out_specs=pl.BlockSpec((1, tile, 512), lambda i, j, s: (i, j, 0)),
            scratch_shapes=[
                pltpu.VMEM((2, 16, 4, 32, 512), BF),
                pltpu.SemaphoreType.DMA((2,)),
            ],
        ),
        compiler_params=params(2),
        cost_estimate=cost(6 * rows * 2048 * 512, 24 << 20),
        name="project_rkv",
    )(place, mixed, *pieces)


def gate_kernel(place_ref, x_ref, *refs):
    pieces = refs[:8]
    out_ref, buf, sem = refs[8:]

    @pl.when(pl.program_id(0) == 0)
    def _():
        copy_weights(pieces, 0, place_ref, buf, sem)
        wait_weights(buf, sem)

    total = jnp.dot(x_ref[0], buf[...].reshape(2048, 512), preferred_element_type=F32)
    out_ref[...] = (total / (1.0 + jnp.exp(-total))).astype(out_ref.dtype)


def project_gate(place, mixed, pieces, tile):
    rows = mixed.shape[1]
    return pl.pallas_call(
        gate_kernel,
        out_shape=jax.ShapeDtypeStruct((rows, 512), BF),
        grid_spec=pltpu.PrefetchScalarGridSpec(
            num_scalar_prefetch=1,
            grid=(rows // tile,),
            in_specs=[pl.BlockSpec((1, tile, 2048), lambda j, s: (4, j, 0))] + [ANY] * 8,
            out_specs=pl.BlockSpec((tile, 512), lambda j, s: (j, 0)),
            scratch_shapes=[pltpu.VMEM((16, 4, 32, 512), BF), pltpu.SemaphoreType.DMA(())],
        ),
        compiler_params=params(1),
        cost_estimate=cost(2 * rows * 2048 * 512, 8 << 20),
        name="project_gate",
    )(place, mixed, *pieces)


def result_kernel(place_ref, count_ref, *refs, spans, t0, decode, chained):
    lots = len(spans)
    xs, pieces = refs[: 4 * lots], refs[4 * lots : 4 * lots + 8]
    rest = refs[4 * lots + 8 + (1 if chained else 0) :]
    out_ref, rest = rest[0], rest[1:]
    if decode:
        decode_ref, rest = rest[0], rest[1:]
    buf, sem = rest
    copy_weights(pieces, 1, place_ref, buf, sem)
    wait_weights(buf, sem)
    start = 0
    for lot, span in enumerate(spans):
        total = None
        for d in range(4):
            w = buf[4 * d : 4 * d + 4].reshape(512, 512)
            term = jnp.dot(xs[4 * lot + d][...], w, preferred_element_type=F32)
            total = term if total is None else total + term
        at = lax.broadcasted_iota(jnp.int32, (span, 512), 0) + (t0 + start)
        for p in range(2):
            own = jnp.where(at < count_ref[p], total[p * span : (p + 1) * span], 0.0)
            out_ref[p, start : start + span] = own.astype(out_ref.dtype)
        start += span
        if decode:
            decode_ref[...] = total[2 * span :].astype(decode_ref.dtype)


def project_result(place, counts, xs, pieces, spans, t0, decode, earlier, length):
    rows = xs[0].shape[0]
    span = sum(spans)
    once = lambda i, s, c: (0, 0)
    out_shape = [jax.ShapeDtypeStruct((2, length, 512), BF)]
    out_specs = [pl.BlockSpec((2, span, 512), lambda i, s, c: (0, t0 // span, 0))]
    if decode:
        out_shape.append(jax.ShapeDtypeStruct((rows - 2 * span, 512), BF))
        out_specs.append(pl.BlockSpec((rows - 2 * span, 512), once))
    chained = earlier is not None
    return pl.pallas_call(
        functools.partial(result_kernel, spans=spans, t0=t0, decode=decode, chained=chained),
        out_shape=out_shape,
        grid_spec=pltpu.PrefetchScalarGridSpec(
            num_scalar_prefetch=2,
            grid=(1,),
            in_specs=[pl.BlockSpec(a.shape, once) for a in xs] + [ANY] * (9 if chained else 8),
            out_specs=out_specs,
            scratch_shapes=[pltpu.VMEM((16, 4, 32, 512), BF), pltpu.SemaphoreType.DMA(())],
        ),
        input_output_aliases={2 + len(xs) + 8: 0} if chained else {},
        compiler_params=params(1),
        cost_estimate=cost(4 * span * 2048 * 512, 8 << 20),
        name="project_result",
    )(place, counts, *xs, *pieces, *([earlier] if chained else []))


SLOT_BLOCK = 16


def head_mask(value):
    row = lax.broadcasted_iota(jnp.int32, (128, 128), 0) < 64
    col = lax.broadcasted_iota(jnp.int32, (128, 128), 1) < 64
    return jnp.where(row == col, value, 0.0).astype(BF)


def in_two(a):
    hi = a.astype(BF)
    return jnp.concatenate([hi, (a - hi.astype(F32)).astype(BF)], axis=1)


def decode_kernel(
    keep_ref, s_ref, r_ref, k_ref, v_ref, w_ref, g_ref, vec_ref,
    state_ref, out_ref, rt_ref, kt_ref, dt_ref, y_ref,
):
    g = pl.program_id(0)

    @pl.when(g == 0)
    def _():
        r = r_ref[0].astype(F32)
        k = k_ref[0].astype(F32)
        decay = jnp.exp(w_ref[...])
        for q in range(4):
            cols = slice(128 * q, 128 * q + 128)

            def turned(a):
                t = jnp.transpose(a[:, cols])
                return jnp.concatenate([t[:64], t[64:]], axis=1)

            rt_ref[q] = turned(r).astype(BF)
            kt_ref[q] = turned(k).astype(BF)
            dt_ref[q] = in_two(turned(decay))

    here = pl.ds(pl.multiple_of(g * SLOT_BLOCK, SLOT_BLOCK), SLOT_BLOCK)
    v = v_ref[0, here].astype(F32)
    row = lax.broadcasted_iota(jnp.int32, (128, 128), 0)
    low = lax.broadcasted_iota(jnp.int32, (128, 128), 1) < 64
    for s in range(SLOT_BLOCK):
        slot = g * SLOT_BLOCK + s
        hit = row == jnp.where(low, slot, slot + 64)
        pick = jnp.where(hit, 1.0, 0.0).astype(BF)
        kept = jnp.where(hit, keep_ref[slot].astype(F32), 0.0).astype(BF)
        r_b = jnp.dot(rt_ref[...].reshape(256, 128), kept, preferred_element_type=F32)
        k_b = jnp.dot(kt_ref[...].reshape(256, 128), pick, preferred_element_type=F32)
        d_b = jnp.dot(
            dt_ref[...].reshape(256, 256),
            jnp.concatenate([kept, kept], axis=0),
            preferred_element_type=F32,
        )
        for q in range(4):
            span = slice(64 * q, 64 * q + 64)
            cols = slice(128 * q, 128 * q + 128)
            state = jnp.concatenate([s_ref[s, 2 * q], s_ref[s, 2 * q + 1]], axis=1)
            after_it = d_b[span] * state + k_b[span] * v[s : s + 1, cols]
            state_ref[s, 2 * q] = after_it[:, :64]
            state_ref[s, 2 * q + 1] = after_it[:, 64:]
            y_ref[s : s + 1, cols] = jnp.sum(r_b[span] * state, axis=0, keepdims=True)
    r = r_ref[0, here].astype(F32)
    k = k_ref[0, here].astype(F32)
    reward, scale, offset = vec_ref[0:1], vec_ref[1:2], vec_ref[2:3]
    own = r * reward * k
    ones = jnp.concatenate([head_mask(1.0)] * 2, axis=0)
    mean_of = jnp.concatenate([head_mask(1.0 / 64)] * 2, axis=0)
    for q in range(4):
        cols = slice(128 * q, 128 * q + 128)
        total = jnp.dot(in_two(own[:, cols]), ones, preferred_element_type=F32)
        y = y_ref[:, cols] + total * v[:, cols]
        center = y - jnp.dot(in_two(y), mean_of, preferred_element_type=F32)
        spread = jnp.dot(in_two(center * center), mean_of, preferred_element_type=F32)
        normed = center * lax.rsqrt(spread + NORM_EPS) * scale[:, cols] + offset[:, cols]
        out_ref[:, cols] = (normed * g_ref[here, cols].astype(F32)).astype(out_ref.dtype)


def decode_step(states, keep, rkv, log_decay, gate, vectors):
    slots = states.shape[0]
    at = rkv.shape[1] // slots - 1

    def part(n):
        return pl.BlockSpec((1, slots, 512), lambda g, s: (n, at, 0))

    flat = pl.BlockSpec((slots, 512), lambda g, s: (at, 0))
    big = pl.BlockSpec((SLOT_BLOCK, 8, 64, 64), lambda g, s: (g, 0, 0, 0))
    return pl.pallas_call(
        decode_kernel,
        out_shape=(
            jax.ShapeDtypeStruct(states.shape, F32),
            jax.ShapeDtypeStruct((slots, 512), BF),
        ),
        grid_spec=pltpu.PrefetchScalarGridSpec(
            num_scalar_prefetch=1,
            grid=(slots // SLOT_BLOCK,),
            in_specs=[big, part(0), part(1), part(2), flat, flat]
            + [pl.BlockSpec((8, 512), lambda g, s: (0, 0))],
            out_specs=(big, pl.BlockSpec((SLOT_BLOCK, 512), lambda g, s: (g, 0))),
            scratch_shapes=[
                pltpu.VMEM((4, 64, 128), BF),
                pltpu.VMEM((4, 64, 128), BF),
                pltpu.VMEM((4, 64, 256), BF),
                pltpu.VMEM((SLOT_BLOCK, 512), F32),
            ],
        ),
        compiler_params=params(1),
        cost_estimate=cost(1 << 27, 36 << 20),
        name="decode_step",
    )(keep, states, rkv, rkv, rkv, log_decay, gate, vectors)


def span_tables():
    t = np.arange(CH)
    blocks = []
    size = 4
    while size <= CH:
        start = (t // size) * size
        mid = start + size // 2
        m = np.zeros((CH, CH), np.float32)
        for i in range(CH):
            if i >= mid[i]:
                m[i, mid[i] : i] = 1.0
            else:
                m[i, i + 1 : mid[i]] = 1.0
        blocks.append(m)
        size *= 2
    before = (t[None, :] < t[:, None]).astype(np.float32)
    after = (t[None, :] > t[:, None]).astype(np.float32)
    whole = np.ones((8, CH), np.float32)
    table = np.concatenate(blocks + [before, after, whole])
    return np.concatenate([table, table], axis=1)


LEVELS = int(np.log2(CH))


def wkv_kernel(
    count_ref, table_ref, r_ref, k_ref, v_ref, w_ref, g_ref, vec_ref, start_ref, *outs, t0, last
):
    c, p = pl.program_id(0), pl.program_id(1)
    out_ref, state_ref = outs[0], outs[1]

    @pl.when(c == 0)
    def _():
        state_ref[p] = start_ref[p]

    table = table_ref[...]
    row = lax.broadcasted_iota(jnp.int32, (CH, 512), 0)
    lane = lax.broadcasted_iota(jnp.int32, (CH, 128), 1)
    low = lane < 64
    arow = lax.broadcasted_iota(jnp.int32, (CH, 2 * CH), 0)
    acol = lax.broadcasted_iota(jnp.int32, (CH, 2 * CH), 1) & (CH - 1)
    diff = arow ^ acol
    causal = arow > acol
    srow = lax.broadcasted_iota(jnp.int32, (128, 128), 0) < 64
    scol = lax.broadcasted_iota(jnp.int32, (128, 128), 1) < 64
    same_head = srow == scol
    mean_of = jnp.where(same_head, 1.0 / 64, 0.0).astype(BF)
    mean_two = jnp.concatenate([mean_of, mean_of], axis=0)
    reward, scale, offset = vec_ref[0:1], vec_ref[1:2], vec_ref[2:3]
    contract_lanes = (((1,), (1,)), ((), ()))
    contract_rows = (((0,), (0,)), ((), ()))

    def both_heads(a):
        zero = jnp.zeros_like(a)
        return jnp.concatenate([jnp.where(low, a, zero), jnp.where(low, zero, a)], axis=0)

    live = (row + (c * CH + t0)) < count_ref[p]
    r = r_ref[0].astype(F32)
    k = jnp.where(live, k_ref[0].astype(F32), 0.0)
    v = v_ref[0]
    w = w_ref[...]
    w_hi = w.astype(BF)
    w_lo = (w - w_hi.astype(F32)).astype(BF)
    sums = jnp.dot(table, jnp.concatenate([w_hi, w_lo], axis=0), preferred_element_type=F32)
    factors = jnp.exp(sums)
    r_dec = (r * factors[(LEVELS - 1) * CH : LEVELS * CH]).astype(BF)
    k_dec = (k * factors[LEVELS * CH : (LEVELS + 1) * CH]).astype(BF)
    whole = factors[(LEVELS + 1) * CH : (LEVELS + 1) * CH + 1]
    r_own = r * reward
    r_hi = r_own.astype(BF)
    r_lo = (r_own - r_hi.astype(F32)).astype(BF)
    k_bf = k.astype(BF)
    mixed = [jnp.where((row & 1) == 1, r, k).astype(BF)]
    for level in range(1, LEVELS):
        pick = jnp.where((row & (1 << level)) != 0, r, k)
        mixed.append((pick * factors[(level - 1) * CH : level * CH]).astype(BF))
    for q in range(4):
        cols = slice(128 * q, 128 * q + 128)
        keys = both_heads(k_bf[:, cols])
        scores = lax.dot_general(
            jnp.concatenate([r_hi[:, cols], r_lo[:, cols]], axis=1),
            jnp.concatenate([keys, keys], axis=1),
            contract_lanes,
            preferred_element_type=F32,
        )
        scores = jnp.where(diff == 0, scores, 0.0)
        for level in range(LEVELS):
            a = mixed[level][:, cols]
            s = lax.dot_general(a, both_heads(a), contract_lanes, preferred_element_type=F32)
            here = jnp.logical_and(causal, (diff >> level) == 1)
            scores = jnp.where(here, s, scores)
        vq = v[:, cols]
        state = state_ref[p, q]
        y = jnp.dot(scores.astype(BF), both_heads(vq), preferred_element_type=F32)
        y = y + lax.dot_general(
            r_dec[:, cols], state.astype(BF), contract_lanes, preferred_element_type=F32
        )
        added = lax.dot_general(vq, k_dec[:, cols], contract_rows, preferred_element_type=F32)
        state_ref[p, q] = state * whole[:, cols] + jnp.where(same_head, added, 0.0)
        y_hi = y.astype(BF)
        y_lo = (y - y_hi.astype(F32)).astype(BF)
        mean = jnp.dot(
            jnp.concatenate([y_hi, y_lo], axis=1), mean_two, preferred_element_type=F32
        )
        center = y - mean
        spread = jnp.dot((center * center).astype(BF), mean_of, preferred_element_type=F32)
        normed = center * lax.rsqrt(spread + NORM_EPS)
        gate = g_ref[:, cols].astype(F32)
        out_ref[0, :, cols] = ((normed * scale[:, cols] + offset[:, cols]) * gate).astype(
            out_ref.dtype
        )

    if last:
        final_ref = outs[2]

        @pl.when(c == pl.num_programs(0) - 1)
        def _():
            for q in range(4):
                turned = jnp.transpose(state_ref[p, q])
                final_ref[0, 2 * q] = turned[:64, :64]
                final_ref[0, 2 * q + 1] = turned[64:, 64:]


def wkv(counts, rkv, log_decay, gate, vectors, start, t0, t1, length):
    prompts = start.shape[0]
    table = jnp.asarray(span_tables(), BF)
    c0, per = t0 // CH, length // CH
    last = t1 == length

    def part(n):
        return pl.BlockSpec((1, CH, 512), lambda c, p, s: (n, p * per + c + c0, 0))

    flat = pl.BlockSpec((CH, 512), lambda c, p, s: (p * per + c + c0, 0))
    held = pl.BlockSpec((prompts, 4, 128, 128), lambda c, p, s: (0, 0, 0, 0))
    out_shape = [
        jax.ShapeDtypeStruct((prompts, t1 - t0, 512), BF),
        jax.ShapeDtypeStruct((prompts, 4, 128, 128), F32),
    ]
    out_specs = [pl.BlockSpec((1, CH, 512), lambda c, p, s: (p, c, 0)), held]
    if last:
        out_shape.append(jax.ShapeDtypeStruct((prompts, 8, 64, 64), F32))
        out_specs.append(pl.BlockSpec((1, 8, 64, 64), lambda c, p, s: (p, 0, 0, 0)))
    return pl.pallas_call(
        functools.partial(wkv_kernel, t0=t0, last=last),
        out_shape=out_shape,
        grid_spec=pltpu.PrefetchScalarGridSpec(
            num_scalar_prefetch=1,
            grid=((t1 - t0) // CH, prompts),
            in_specs=[
                pl.BlockSpec(table.shape, lambda c, p, s: (0, 0)),
                part(0),
                part(1),
                part(2),
                flat,
                flat,
                pl.BlockSpec((8, 512), lambda c, p, s: (0, 0)),
                held,
            ],
            out_specs=out_specs,
        ),
        compiler_params=params(2),
        cost_estimate=cost((t1 - t0) * 80_000_000, (t1 - t0) << 17),
        name="wkv",
    )(counts, table, rkv, rkv, rkv, log_decay, gate, vectors, start)


def on_device(
    learner_acceptance_matrix,
    learner_address_matrix,
    learner_content_matrix,
    learner_gating_matrix,
    learner_result_matrix,
    fading_narrowing_matrix,
    fading_widening_matrix,
    feature_fading_speed,
    current_reward,
    symbol_blending_factors,
    group_scaling_factor,
    group_scaling_offset,
    request_hidden_entries,
    request_valid_count,
    request_destination_place,
    newest_symbol_hidden,
    preceding_hidden_entry,
    place_memory_matrix,
    place_newness_marks,
):
    h = lax.axis_index("yh") * 2 + lax.axis_index("core")
    z, x, yl = lax.axis_index("z"), lax.axis_index("x"), lax.axis_index("yl")
    req = z * 8 + x * 2 + yl
    place = jnp.stack([h, z, x, yl]).astype(jnp.int32)
    prompts, length, width = request_hidden_entries.shape
    slots, groups, breadth = place_memory_matrix.shape[:3]
    tokens = prompts * length
    rows = tokens + slots
    keep = place_newness_marks != 1
    counts = request_valid_count

    blocks = column_blocks(
        [
            learner_acceptance_matrix,
            learner_address_matrix,
            learner_content_matrix,
            learner_gating_matrix,
            learner_result_matrix,
        ],
        h,
    )
    hidden = request_hidden_entries.reshape(tokens, width)
    prior = jnp.where(keep[:, None], preceding_hidden_entry, jnp.zeros((), BF))
    hidden, newest, prior = after((hidden, newest_symbol_hidden, prior), blocks[1])
    own = jnp.concatenate([hidden, newest, prior], axis=0)
    by_row = with_neighbour(jnp.stack(blocks), yl)
    side = swap(own, "head", 1)
    far = swap(own, "head", 2)
    far_side = swap(far, "head", 1)

    def mixes(piece, d, mixed, low):
        return mix(
            place,
            counts,
            piece,
            d,
            symbol_blending_factors,
            fading_narrowing_matrix,
            low,
            mixed,
            fading_widening_matrix,
            feature_fading_speed[None],
            slots,
            length,
        )

    every, first, second = slice(0, 5), slice(0, 3), slice(3, 5)
    held = [by_row[p][None, None] for p in range(4)]
    recv = swap_all(held, 0)
    mixed, low = mixes(own, 0, None, None)
    held = pack(place, held, after(recv, low), 0, every)
    recv = swap_all(held, 1)
    mixed, low = mixes(side, 1, mixed, low)
    held = pack(place, held, after(recv, low), 1, every)
    recv = swap_all(held, 2)
    mixed, low = mixes(far, 2, mixed, low)
    recv = after(recv, low)
    early = pack(place, held, recv, 2, first)
    early_recv = swap_all(early, 3)
    late = pack(place, held, recv, 2, second)
    mixed, log_decay = mixes(far_side, 3, mixed, low)
    early_recv = after(early_recv, log_decay)
    late_recv = swap_all(after(late, early_recv), 3)
    early = list(early) + early_recv
    late = list(late) + late_recv

    rkv = project_rkv(place, mixed, early, rows // 2)
    gate = project_gate(place, mixed, late, rows // 2)
    small = jnp.stack([current_reward, group_scaling_factor, group_scaling_offset])
    vectors = jnp.concatenate([small, jnp.zeros((5, width), F32)])
    new_state, normed_d = decode_step(
        place_memory_matrix, keep.astype(jnp.int32), rkv, log_decay, gate, vectors
    )
    state = jnp.zeros((prompts, groups // 2, 128, 128), F32)
    sent = []
    t0 = 0
    for t1 in (256, 384, 512):
        out = wkv(counts, rkv, log_decay, gate, vectors, state, t0, t1, length)
        state = out[1]
        normed = out[0].reshape(prompts * (t1 - t0), width)
        if t0 == 0:
            normed = jnp.concatenate([normed, normed_d], axis=0)
        n_side = swap(normed, "head", 1)
        n_far = swap(normed, "head", 2)
        n_far_side = swap(n_far, "head", 1)
        sent.append([normed, n_side, n_far, n_far_side])
        t0 = t1
    result, decode_all = project_result(
        place, counts, sent[0], late, (256,), 0, True, None, length
    )
    (result,) = project_result(
        place, counts, sent[1] + sent[2], late, (128, 128), 256, False, result, length
    )
    prompt_hidden = result
    final_state = out[2]

    offsets = request_destination_place - req * slots
    slot_ids = lax.broadcasted_iota(jnp.int32, (slots,), 0)
    new_shift = newest_symbol_hidden
    taken = jnp.zeros((slots,), jnp.bool_)
    for n in range(prompts):
        new_state = lax.dynamic_update_slice(
            new_state, final_state[n : n + 1], (offsets[n], 0, 0, 0)
        )
        last_token = lax.dynamic_slice(
            request_hidden_entries, (n, counts[n] - 1, 0), (1, 1, width)
        )[0]
        new_shift = lax.dynamic_update_slice(new_shift, last_token, (offsets[n], 0))
        taken = taken | (slot_ids == offsets[n])
    decode_hidden = jnp.where(taken[:, None], jnp.zeros((), BF), decode_all)
    return (prompt_hidden, decode_hidden, new_state, new_shift)


def solution(mesh):
    split = Mesh(mesh.devices.reshape(2, 2, 4, 4, 2), ("yh", "core", "z", "x", "yl"))
    head = ("yh", "core")
    req = ("z", "x", "yl")
    row_shard = P(head + req, None)
    in_specs = (
        row_shard,
        row_shard,
        row_shard,
        row_shard,
        row_shard,
        P(),
        P(None, head),
        P(head),
        P(head),
        P(),
        P(head),
        P(head),
        P(req, None, head),
        P(req),
        P(req),
        P(req, head),
        P(req, head),
        P(req, head, None, None),
        P(req),
    )
    out_specs = (
        P(req, None, head),
        P(req, head),
        P(req, head, None, None),
        P(req, head),
    )
    return jax.shard_map(
        on_device, mesh=split, in_specs=in_specs, out_specs=out_specs, check_vma=False
    )
```

time: 1570 us -> 213 us (0.14)
  waiting for transfers between devices: 1090 us -> 14.6 us
  other arithmetic: 227 us -> 8.69 us
  matrix products: 140 us -> 0 us
  Pallas kernels: 0 us -> 118 us
  local copies, waits for them, and re-layouts: 70.7 us -> 11.8 us
  starting transfers between devices: 0.33 us -> 50.9 us
  blocking collectives: 19.8 us -> 0 us
    all_gather x6 -> x0, waiting for transfers between devices: 1060 us -> none  [the longest x1 306 us: on_device(): lax.all_gather(casted[0], ('head', 'req'), axis=0, tiled=True)]
    dot_general x59 -> x0, matrix products: 140 us -> none  [the longest x10 47 us: project(): return jnp.dot(left, right, preferred_element_type=jnp.float32)]
    pallas_call x0 -> x16, Pallas kernels: none -> 118 us  [the longest x3 40.7 us: wkv(): pl.pallas_call(functools.partial(wkv_kernel, t0=t0, last=last), out_shape...]
    dot_general x16 -> x0, other arithmetic: 112 us -> none  [advance(): jnp.einsum('pthd,pjhd,ptjhd->phtj', acceptance_array, address_array, weig...]
    ppermute x0 -> x36, starting transfers between devices: none -> 50.9 us  [swap(): return lax.ppermute(a, names, [(i, i ^ bits) for i in range(sizes[axes])])]
    while x16 -> x0, other arithmetic: 28.5 us -> none
    reduce_scatter x2 -> x0, waiting for transfers between devices: 27.4 us -> none  [the longest x1 27.4 us: on_device(): lax.psum_scatter(prompt_part.reshape(prompt_count, length, model_width).a...]
    reduce_sum x20 -> x0, other arithmetic: 27 us -> none  [the longest x16 20.6 us: advance(): jnp.sum(acceptance_array * group_reward * address_array, axis=-1, keepdim...]
  transfers between devices with their start and end apart: 8 -> 36, of which waited for: 6 -> 5; matrix products, arithmetic and copies ran while one was open for 27% -> 4% of each run, Pallas kernels for 0% -> 34%
where the time goes in v1:
time: 213 us; the launch traced here: 212 us
  Pallas kernels  118 us (55%)
  starting transfers between devices  50.9 us (24%)
  waiting for transfers between devices  14.6 us (7%)
  local copies, waits for them, and re-layouts  11.8 us (6%)
  other arithmetic  8.69 us (4%)
  between operations  7.84 us (4%)
    ppermute x36, starting transfers between devices, swap(): return lax.ppermute(a, names, [(i, i ^ bits) for i in range(sizes[axes])])  50.9 us
    pallas_call x3, Pallas kernels, wkv(): pl.pallas_call(functools.partial(wkv_kernel, t0=t0, last=last), out_shape...  40.7 us
    pallas_call x4, Pallas kernels, mix(): pl.pallas_call(functools.partial(mix_kernel, d=d, length=length), out_sha...  21.3 us
    pallas_call x1, Pallas kernels, decode_step(): pl.pallas_call(decode_kernel, out_shape=(jax.ShapeDtypeStruct(states.shap...  15.9 us
    ppermute x36, waiting for transfers between devices, swap(): return lax.ppermute(a, names, [(i, i ^ bits) for i in range(sizes[axes])])  14.6 us
    pallas_call x1, Pallas kernels, project_rkv(): pl.pallas_call(rkv_kernel, out_shape=jax.ShapeDtypeStruct((3, rows, 512),...  13.8 us
    pallas_call x4, Pallas kernels, pack(): pl.pallas_call(functools.partial(pack_kernel, n=n, lot=lot), out_shape=sh...  11.6 us
    pallas_call x2, Pallas kernels, project_result(): pl.pallas_call(functools.partial(result_kernel, spans=spans, t0=t0, decod...  8.65 us
  transfers between devices with their start and end apart: 36, of which 5 were waited for; matrix products, arithmetic and copies ran while one was open for 4% of the time, Pallas kernels for 34%

profile of v1, /device:TPU:1, one launch (start us, length us, event | category | flops | bytes accessed | tf_op | source)
XLA Modules:
  0.0 211.5 jit_solution(17120775997613716858)
XLA Ops:
  7.7 3.0 %collective-permute-start.5 = (bf16[5,16,512]{2,1,0:T(8,128)(2,1)S(1)}, bf16[5,16,512]{2,1,0:T(8,128)(2,1)S(1)}, u32[]{:S(2)}, u32[]{:S(2)}) collective-permute-start(bf16[5,16,512]{2,1,0:T(8,128)(2,1)S(1)} %get-tuple-element.127), channel_id=1, source_target_pairs={{0,96},{32,64},{64,32},{96,0},{1,97},{33,65},{65,33},{97,1},{2,98}... | collective-permute-start | bytes 245768 | tf_op jit(solution)/shard_map/ppermute | solution.py:25
  11.7 1.7 collective-permute-done.5
  13.4 2.1 collective-permute-done.4
  16.0 3.0 %collective-permute-start.1 = (bf16[1152,512]{1,0:T(8,128)(2,1)S(1)}, bf16[1152,512]{1,0:T(8,128)(2,1)}, u32[]{:S(2)}, u32[]{:S(2)}) collective-permute-start(bf16[1152,512]{1,0:T(8,128)(2,1)S(1)} %constant_dynamic-update-slice_fusion.refs_0_), channel_id=1, source_target_pairs={{0,64},{32,96},{64,0},{96,32},{1,65},{33,97},{65,1},{97,33},{2,66}... | collective-permute-start | bytes 3538952 | tf_op jit(solution)/shard_map/ppermute | solution.py:25
  19.0 4.4 %collective-permute-done.6 = bf16[4,5,16,512]{3,2,1,0:T(8,128)(2,1)} collective-permute-done((bf16[4,5,16,512]{3,2,1,0:T(8,128)(2,1)S(1)}, bf16[4,5,16,512]{3,2,1,0:T(8,128)(2,1)}, u32[]{:S(2)}, u32[]{:S(2)}) %collective-permute-start.6) | collective-permute-done | bytes 327712 | tf_op jit(solution)/shard_map/ppermute | solution.py:25
  28.0 1.8 collective-permute-start.9
  30.5 3.7 %collective-permute-start.10 = (bf16[1,1,5,32,512]{4,3,2,1,0:T(8,128)(2,1)S(1)}, bf16[1,1,5,32,512]{4,3,2,1,0:T(8,128)(2,1)}, u32[]{:S(2)}, u32[]{:S(2)}) collective-permute-start(bf16[1,1,5,32,512]{4,3,2,1,0:T(8,128)(2,1)S(1)} %get-tuple-element.120.refs_3_), channel_id=1, source_target_pairs={{0,24},{8,16},{16,8},{24,0},{1,25},{9,17},{17,9},{25,1},{2,26},{10... | collective-permute-start | bytes 491528 | tf_op jit(solution)/shard_map/ppermute | solution.py:25
  35.5 4.8 %mix.4 = (bf16[5,1088,2048]{2,1,0:T(8,128)(2,1)}, f32[1088,64]{1,0:T(8,128)S(1)}) custom-call(s32[4]{0:T(128)S(1)} %pad_add_fusion.place_ref, s32[2]{0:T(128)S(1)} %copy-done.14, bf16[1152,512]{1,0:T(8,128)(2,1)S(1)} %constant_dynamic-update-slice_fusion.refs_0_, f32[5,2048]{1,0:T(8,128)S(1)} %copy-done.3, bf16[2048,64]{1,0:T(8,128)(2,1)S(1)} %copy.33.refs_2_), custom_call_target="tpu_custom_call" | custom-call | flops 11141120 | bytes 6684672 | tf_op jit(solution)/shard_map/mix/pallas_call | solution.py:205
  40.3 2.4 %pack.4 = (bf16[1,2,5,32,512]{4,3,2,1,0:T(8,128)(2,1)S(1)}, bf16[2,1,5,32,512]{4,3,2,1,0:T(8,128)(2,1)S(1)}, bf16[1,2,5,32,512]{4,3,2,1,0:T(8,128)(2,1)S(1)}, bf16[2,1,5,32,512]{4,3,2,1,0:T(8,128)(2,1)S(1)}) custom-call(s32[4]{0:T(128)S(1)} %pad_add_fusion.place_ref, bf16[1,1,5,32,512]{4,3,2,1,0:T(8,128)(2,1)S(1)} %get-tuple-element.121.refs_0_, ...), custom_call_target="tpu_custom_call" | custom-call | bytes 8388608 | tf_op jit(solution)/shard_map/pack/pallas_call | solution.py:106
  42.8 2.6 %collective-permute-start.12 = (bf16[2,1,5,32,512]{4,3,2,1,0:T(8,128)(2,1)S(1)}, bf16[2,1,5,32,512]{4,3,2,1,0:T(8,128)(2,1)S(1)}, u32[]{:S(2)}, u32[]{:S(2)}) collective-permute-start(bf16[2,1,5,32,512]{4,3,2,1,0:T(8,128)(2,1)S(1)} %get-tuple-element.76.refs_1_), channel_id=1, source_target_pairs={{0,6},{2,4},{4,2},{6,0},{1,7},{3,5},{5,3},{7,1},{8,14},{10,12},{12... | collective-permute-start | bytes 983048 | tf_op jit(solution)/shard_map/ppermute | solution.py:25
  45.4 4.8 %mix.5 = (bf16[5,1088,2048]{2,1,0:T(8,128)(2,1)}, f32[1088,64]{1,0:T(8,128)S(1)}) custom-call(s32[4]{0:T(128)S(1)} %pad_add_fusion.place_ref, s32[2]{0:T(128)S(1)} %copy-done.14, bf16[1152,512]{1,0:T(8,128)(2,1)S(1)} %collective-permute-done.3.refs_0_, f32[5,2048]{1,0:T(8,128)S(1)} %copy-done.3, ...), custom_call_target="tpu_custom_call", output_to_operand_aliasing={{0}: (6, {})} | custom-call | flops 11141120 | bytes 6684672 | tf_op jit(solution)/shard_map/mix/pallas_call | solution.py:205
  52.6 2.4 %pack.5 = (bf16[2,2,5,32,512]{4,3,2,1,0:T(8,128)(2,1)S(1)}, bf16[2,2,5,32,512]{4,3,2,1,0:T(8,128)(2,1)S(1)}, bf16[2,2,5,32,512]{4,3,2,1,0:T(8,128)(2,1)}, bf16[2,2,5,32,512]{4,3,2,1,0:T(8,128)(2,1)}) custom-call(s32[4]{0:T(128)S(1)} %pad_add_fusion.place_ref, bf16[1,2,5,32,512]{4,3,2,1,0:T(8,128)(2,1)S(1)} %get-tuple-element.75.refs_0_, ...), custom_call_target="tpu_custom_call" | custom-call | bytes 8388608 | tf_op jit(solution)/shard_map/pack/pallas_call | solution.py:106
  58.0 7.6 %collective-permute-start.2 = (bf16[1152,512]{1,0:T(8,128)(2,1)}, bf16[1152,512]{1,0:T(8,128)(2,1)S(1)}, u32[]{:S(2)}, u32[]{:S(2)}) collective-permute-start(bf16[1152,512]{1,0:T(8,128)(2,1)} %collective-permute-done.1.refs_0_), channel_id=1, source_target_pairs={{0,32},{32,0},{64,96},{96,64},{1,33},{33,1},{65,97},{97,65},{2,34}... | collective-permute-start | bytes 3538952 | tf_op jit(solution)/shard_map/ppermute | solution.py:25
  66.6 6.1 %mix.6 = (bf16[5,1088,2048]{2,1,0:T(8,128)(2,1)}, f32[1088,64]{1,0:T(8,128)S(1)}) custom-call(s32[4]{0:T(128)S(1)} %pad_add_fusion.place_ref, s32[2]{0:T(128)S(1)} %copy-done.14, bf16[1152,512]{1,0:T(8,128)(2,1)} %collective-permute-done.1.refs_0_, f32[5,2048]{1,0:T(8,128)S(1)} %copy-done.3, ...), custom_call_target="tpu_custom_call", output_to_operand_aliasing={{0}: (6, {})} | custom-call | flops 11141120 | bytes 6684672 | tf_op jit(solution)/shard_map/mix/pallas_call | solution.py:205
  72.9 4.4 %pack.6 = (bf16[2,4,3,32,512]{4,3,2,1,0:T(8,128)(2,1)}, bf16[4,2,3,32,512]{4,3,2,1,0:T(8,128)(2,1)}, bf16[2,4,3,32,512]{4,3,2,1,0:T(8,128)(2,1)}, bf16[4,2,3,32,512]{4,3,2,1,0:T(8,128)(2,1)}) custom-call(s32[4]{0:T(128)S(1)} %pad_add_fusion.place_ref, bf16[2,2,5,32,512]{4,3,2,1,0:T(8,128)(2,1)S(1)} %get-tuple-element.83.refs_0_, ...), custom_call_target="tpu_custom_call" | custom-call | bytes 8388608 | tf_op jit(solution)/shard_map/pack/pallas_call | solution.py:106
  78.2 1.7 collective-permute-start.20
  80.2 2.5 %collective-permute-start.22 = (bf16[4,2,3,32,512]{4,3,2,1,0:T(8,128)(2,1)}, bf16[4,2,3,32,512]{4,3,2,1,0:T(8,128)(2,1)}, u32[]{:S(2)}, u32[]{:S(2)}) collective-permute-start(bf16[4,2,3,32,512]{4,3,2,1,0:T(8,128)(2,1)} %get-tuple-element.94.refs_3_), channel_id=1, source_target_pairs={{0,6},{2,4},{4,2},{6,0},{1,7},{3,5},{5,3},{7,1},{8,14},{10,12},{12... | collective-permute-start | bytes 2359304 | tf_op jit(solution)/shard_map/ppermute | solution.py:25
  93.0 2.4 %pack.7 = (bf16[2,4,2,32,512]{4,3,2,1,0:T(8,128)(2,1)S(1)}, bf16[4,2,2,32,512]{4,3,2,1,0:T(8,128)(2,1)S(1)}, bf16[2,4,2,32,512]{4,3,2,1,0:T(8,128)(2,1)S(1)}, bf16[4,2,2,32,512]{4,3,2,1,0:T(8,128)(2,1)S(1)}) custom-call(s32[4]{0:T(128)S(1)} %pad_add_fusion.place_ref, bf16[2,2,5,32,512]{4,3,2,1,0:T(8,128)(2,1)S(1)} %get-tuple-element.83.refs_0_, ...), custom_call_target="tpu_custom_call" | custom-call | bytes 8388608 | tf_op jit(solution)/shard_map/pack/pallas_call | solution.py:106
  97.7 5.5 %mix.7 = (bf16[5,1088,2048]{2,1,0:T(8,128)(2,1)}, f32[1088,512]{1,0:T(8,128)S(1)}) custom-call(s32[4]{0:T(128)S(1)} %pad_add_fusion.place_ref, s32[2]{0:T(128)S(1)} %copy-done.14, bf16[1152,512]{1,0:T(8,128)(2,1)S(1)} %copy-done.2, f32[5,2048]{1,0:T(8,128)S(1)} %copy-done.3, bf16[2048,64]{1,0:T(8,128)(2,1)S(1)} %copy.33.refs_2_, ...), custom_call_target="tpu_custom_call", output_to_operand_aliasing={{0}: (6, {})} | custom-call | flops 11141120 | bytes 6684672 | tf_op jit(solution)/shard_map/mix/pallas_call | solution.py:205
  103.1 1.8 collective-permute-start.23
  105.6 13.8 %project_rkv.1.r_ref.k_ref.v_ref = bf16[3,1088,512]{2,1,0:T(8,128)(2,1)} custom-call(s32[4]{0:T(128)S(1)} %pad_add_fusion.place_ref, bf16[5,1088,2048]{2,1,0:T(8,128)(2,1)} %get-tuple-element.70.x_ref, bf16[2,4,3,32,512]{4,3,2,1,0:T(8,128)(2,1)} %get-tuple-element.91.refs_0_, bf16[4,2,3,32,512]{4,3,2,1,0:T(8,128)(2,1)S(1)} %copy-done.4, ...), custom_call_target="tpu_custom_call" | custom-call | flops 6845104128 | bytes 25165824 | tf_op jit(solution)/shard_map/project_rkv/pallas_call | solution.py:252
  119.5 5.9 %project_gate.1.g_ref = bf16[1088,512]{1,0:T(8,128)(2,1)S(1)} custom-call(s32[4]{0:T(128)S(1)} %pad_add_fusion.place_ref, bf16[5,1088,2048]{2,1,0:T(8,128)(2,1)} %get-tuple-element.70.x_ref, bf16[2,4,2,32,512]{4,3,2,1,0:T(8,128)(2,1)S(1)} %get-tuple-element.104.refs_0_.refs_4_.refs_8_, ...), custom_call_target="tpu_custom_call" | custom-call | flops 2281701376 | bytes 8388608 | tf_op jit(solution)/shard_map/project_gate/pallas_call | solution.py:286
  125.4 19.0 %wkv.3 = (bf16[2,256,512]{2,1,0:T(8,128)(2,1)S(1)}, f32[2,4,128,128]{3,2,1,0:T(8,128)S(1)}) custom-call(s32[2]{0:T(128)S(1)} %copy-done.14, bf16[456,128]{1,0:T(8,128)(2,1)S(1)} %copy-done.16, bf16[3,1088,512]{2,1,0:T(8,128)(2,1)} %project_rkv.1.r_ref.k_ref.v_ref, bf16[3,1088,512]{2,1,0:T(8,128)(2,1)} %project_rkv.1.r_ref.k_ref.v_ref, ...), custom_call_target="tpu_custom_call" | custom-call | flops 20480000000 | bytes 33554432 | tf_op jit(solution)/shard_map/wkv/pallas_call | solution.py:607
  144.4 15.9 %decode_step.1 = (f32[64,8,64,64]{3,2,1,0:T(8,128)}, bf16[64,512]{1,0:T(8,128)(2,1)S(1)}) custom-call(s32[64]{0:T(128)S(1)} %get-tuple-element.134.keep_ref, f32[64,8,64,64]{3,2,1,0:T(8,128)} %s_ref.1, bf16[3,1088,512]{2,1,0:T(8,128)(2,1)} %project_rkv.1.r_ref.k_ref.v_ref, bf16[3,1088,512]{2,1,0:T(8,128)(2,1)} %project_rkv.1.r_ref.k_ref.v_ref, ...), custom_call_target="tpu_custom_call" | custom-call | flops 134217728 | bytes 37748736 | tf_op jit(solution)/shard_map/decode_step/pallas_call | solution.py:440
  160.4 1.8 collective-permute-start.34
  162.2 10.3 %wkv.4 = (bf16[2,128,512]{2,1,0:T(8,128)(2,1)S(1)}, f32[2,4,128,128]{3,2,1,0:T(8,128)S(1)}) custom-call(s32[2]{0:T(128)S(1)} %copy-done.14, bf16[456,128]{1,0:T(8,128)(2,1)S(1)} %copy-done.16, bf16[3,1088,512]{2,1,0:T(8,128)(2,1)} %project_rkv.1.r_ref.k_ref.v_ref, bf16[3,1088,512]{2,1,0:T(8,128)(2,1)} %project_rkv.1.r_ref.k_ref.v_ref, ...), custom_call_target="tpu_custom_call" | custom-call | flops 10240000000 | bytes 16777216 | tf_op jit(solution)/shard_map/wkv/pallas_call | solution.py:607
  172.4 5.7 %collective-permute-start.27 = (bf16[256,512]{1,0:T(8,128)(2,1)S(1)}, bf16[256,512]{1,0:T(8,128)(2,1)S(1)}, u32[]{:S(2)}, u32[]{:S(2)}) collective-permute-start(bf16[256,512]{1,0:T(8,128)(2,1)S(1)} %bitcast.46), channel_id=1, source_target_pairs={{0,32},{32,0},{64,96},{96,64},{1,33},{33,1},{65,97},{97,65},{2,34}... | collective-permute-start | bytes 786440 | tf_op jit(solution)/shard_map/ppermute | solution.py:25
  179.4 11.5 %wkv.5 = (bf16[2,128,512]{2,1,0:T(8,128)(2,1)S(1)}, f32[2,4,128,128]{3,2,1,0:T(8,128)}, f32[2,8,64,64]{3,2,1,0:T(8,128)S(1)}) custom-call(s32[2]{0:T(128)S(1)} %copy-done.14, bf16[456,128]{1,0:T(8,128)(2,1)S(1)} %copy-done.16, bf16[3,1088,512]{2,1,0:T(8,128)(2,1)} %project_rkv.1.r_ref.k_ref.v_ref, bf16[3,1088,512]{2,1,0:T(8,128)(2,1)} %project_rkv.1.r_ref.k_ref.v_ref, ...), custom_call_target="tpu_custom_call" | custom-call | flops 10240000000 | bytes 16777216 | tf_op jit(solution)/shard_map/wkv/pallas_call | solution.py:607
  190.9 2.2 %collective-permute-start.31 = (bf16[256,512]{1,0:T(8,128)(2,1)S(1)}, bf16[256,512]{1,0:T(8,128)(2,1)S(1)}, u32[]{:S(2)}, u32[]{:S(2)}) collective-permute-start(bf16[256,512]{1,0:T(8,128)(2,1)S(1)} %bitcast.49), channel_id=1, source_target_pairs={{0,64},{32,96},{64,0},{96,32},{1,65},{33,97},{65,1},{97,33},{2,66}... | collective-permute-start | bytes 786440 | tf_op jit(solution)/shard_map/ppermute | solution.py:25
  195.1 4.8 %collective-permute-done.31.refs_6_ = bf16[256,512]{1,0:T(8,128)(2,1)S(1)} collective-permute-done((bf16[256,512]{1,0:T(8,128)(2,1)S(1)}, bf16[256,512]{1,0:T(8,128)(2,1)S(1)}, u32[]{:S(2)}, u32[]{:S(2)}) %collective-permute-start.31) | collective-permute-done | bytes 262176 | tf_op jit(solution)/shard_map/ppermute | solution.py:25
  202.0 4.5 %project_result.2 = (bf16[2,512,512]{2,1,0:T(8,128)(2,1)}, bf16[64,512]{1,0:T(8,128)(2,1)S(1)}) custom-call(s32[4]{0:T(128)S(1)} %pad_add_fusion.place_ref, s32[2]{0:T(128)S(1)} %copy-done.14, bf16[576,512]{1,0:T(8,128)(2,1)S(1)} %pad_maximum_fusion.refs_0_, bf16[576,512]{1,0:T(8,128)(2,1)S(1)} %collective-permute-done.33.refs_1_, ...), custom_call_target="tpu_custom_call" | custom-call | flops 1073741824 | bytes 8388608 | tf_op jit(solution)/shard_map/project_result/pallas_call | solution.py:338
  207.2 4.2 %project_result.3 = bf16[2,512,512]{2,1,0:T(8,128)(2,1)} custom-call(s32[4]{0:T(128)S(1)} %pad_add_fusion.place_ref, s32[2]{0:T(128)S(1)} %copy-done.14, bf16[256,512]{1,0:T(8,128)(2,1)S(1)} %bitcast.48, bf16[256,512]{1,0:T(8,128)(2,1)S(1)} %collective-permute-done.27.refs_1_, ...), custom_call_target="tpu_custom_call", output_to_operand_aliasing={{}: (18, {})} | custom-call | flops 1073741824 | bytes 8388608 | tf_op jit(solution)/shard_map/project_result/pallas_call | solution.py:338
  (140 shorter events, 35.7 us)
Async XLA Ops:
  11.0 34.5 %collective-permute-start.3 = (bf16[1152,512]{1,0:T(8,128)(2,1)S(1)}, bf16[1152,512]{1,0:T(8,128)(2,1)S(1)}, u32[]{:S(2)}, u32[]{:S(2)}) collective-permute-start(bf16[1152,512]{1,0:T(8,128)(2,1)S(1)} %constant_dynamic-update-slice_fusion.refs_0_), channel_id=1, source_target_pairs={{0,32},{32,0},{64,96},{96,64},{1,33},{33,1},{65,97},{97,65},{2,34}... | collective-permute-start | bytes 3538952 | tf_op jit(solution)/shard_map/ppermute | solution.py:25
  15.5 7.8 %collective-permute-start.6 = (bf16[4,5,16,512]{3,2,1,0:T(8,128)(2,1)S(1)}, bf16[4,5,16,512]{3,2,1,0:T(8,128)(2,1)}, u32[]{:S(2)}, u32[]{:S(2)}) collective-permute-start(bf16[4,5,16,512]{3,2,1,0:T(8,128)(2,1)S(1)} %pad_maximum_fusion.1), channel_id=1, source_target_pairs={{0,1},{1,0},{2,3},{3,2},{4,5},{5,4},{6,7},{7,6},{8,9},{9,8},{10,11... | collective-permute-start | bytes 983048 | tf_op jit(solution)/shard_map/ppermute | solution.py:25
  16.0 42.0 %collective-permute-start.1 = (bf16[1152,512]{1,0:T(8,128)(2,1)S(1)}, bf16[1152,512]{1,0:T(8,128)(2,1)}, u32[]{:S(2)}, u32[]{:S(2)}) collective-permute-start(bf16[1152,512]{1,0:T(8,128)(2,1)S(1)} %constant_dynamic-update-slice_fusion.refs_0_), channel_id=1, source_target_pairs={{0,64},{32,96},{64,0},{96,32},{1,65},{33,97},{65,1},{97,33},{2,66}... | collective-permute-start | bytes 3538952 | tf_op jit(solution)/shard_map/ppermute | solution.py:25
  26.4 13.9 %collective-permute-start.8 = (bf16[1,1,5,32,512]{4,3,2,1,0:T(8,128)(2,1)}, bf16[1,1,5,32,512]{4,3,2,1,0:T(8,128)(2,1)}, u32[]{:S(2)}, u32[]{:S(2)}) collective-permute-start(bf16[1,1,5,32,512]{4,3,2,1,0:T(8,128)(2,1)} %get-tuple-element.122.refs_1_), channel_id=1, source_target_pairs={{0,8},{8,0},{16,24},{24,16},{1,9},{9,1},{17,25},{25,17},{2,10},{10... | collective-permute-start | bytes 491528 | tf_op jit(solution)/shard_map/ppermute | solution.py:25
  28.0 12.3 %collective-permute-start.9 = (bf16[1,1,5,32,512]{4,3,2,1,0:T(8,128)(2,1)}, bf16[1,1,5,32,512]{4,3,2,1,0:T(8,128)(2,1)}, u32[]{:S(2)}, u32[]{:S(2)}) collective-permute-start(bf16[1,1,5,32,512]{4,3,2,1,0:T(8,128)(2,1)} %get-tuple-element.123.refs_2_), channel_id=1, source_target_pairs={{0,6},{2,4},{4,2},{6,0},{1,7},{3,5},{5,3},{7,1},{8,14},{10,12},{12... | collective-permute-start | bytes 491528 | tf_op jit(solution)/shard_map/ppermute | solution.py:25
  30.5 9.8 %collective-permute-start.10 = (bf16[1,1,5,32,512]{4,3,2,1,0:T(8,128)(2,1)S(1)}, bf16[1,1,5,32,512]{4,3,2,1,0:T(8,128)(2,1)}, u32[]{:S(2)}, u32[]{:S(2)}) collective-permute-start(bf16[1,1,5,32,512]{4,3,2,1,0:T(8,128)(2,1)S(1)} %get-tuple-element.120.refs_3_), channel_id=1, source_target_pairs={{0,24},{8,16},{16,8},{24,0},{1,25},{9,17},{17,9},{25,1},{2,26},{10... | collective-permute-start | bytes 491528 | tf_op jit(solution)/shard_map/ppermute | solution.py:25
  42.7 8.3 %collective-permute-start.11 = (bf16[1,2,5,32,512]{4,3,2,1,0:T(8,128)(2,1)S(1)}, bf16[1,2,5,32,512]{4,3,2,1,0:T(8,128)(2,1)S(1)}, u32[]{:S(2)}, u32[]{:S(2)}) collective-permute-start(bf16[1,2,5,32,512]{4,3,2,1,0:T(8,128)(2,1)S(1)} %get-tuple-element.75.refs_0_), channel_id=1, source_target_pairs={{0,8},{8,0},{16,24},{24,16},{1,9},{9,1},{17,25},{25,17},{2,10},{10... | collective-permute-start | bytes 983048 | tf_op jit(solution)/shard_map/ppermute | solution.py:25
  42.8 8.2 %collective-permute-start.12 = (bf16[2,1,5,32,512]{4,3,2,1,0:T(8,128)(2,1)S(1)}, bf16[2,1,5,32,512]{4,3,2,1,0:T(8,128)(2,1)S(1)}, u32[]{:S(2)}, u32[]{:S(2)}) collective-permute-start(bf16[2,1,5,32,512]{4,3,2,1,0:T(8,128)(2,1)S(1)} %get-tuple-element.76.refs_1_), channel_id=1, source_target_pairs={{0,6},{2,4},{4,2},{6,0},{1,7},{3,5},{5,3},{7,1},{8,14},{10,12},{12... | collective-permute-start | bytes 983048 | tf_op jit(solution)/shard_map/ppermute | solution.py:25
  45.4 7.2 %collective-permute-start.13 = (bf16[1,2,5,32,512]{4,3,2,1,0:T(8,128)(2,1)S(1)}, bf16[1,2,5,32,512]{4,3,2,1,0:T(8,128)(2,1)S(1)}, u32[]{:S(2)}, u32[]{:S(2)}) collective-permute-start(bf16[1,2,5,32,512]{4,3,2,1,0:T(8,128)(2,1)S(1)} %get-tuple-element.77.refs_2_), channel_id=1, source_target_pairs={{0,24},{8,16},{16,8},{24,0},{1,25},{9,17},{17,9},{25,1},{2,26},{10... | collective-permute-start | bytes 983048 | tf_op jit(solution)/shard_map/ppermute | solution.py:25
  45.4 7.2 %collective-permute-start.14 = (bf16[2,1,5,32,512]{4,3,2,1,0:T(8,128)(2,1)S(1)}, bf16[2,1,5,32,512]{4,3,2,1,0:T(8,128)(2,1)S(1)}, u32[]{:S(2)}, u32[]{:S(2)}) collective-permute-start(bf16[2,1,5,32,512]{4,3,2,1,0:T(8,128)(2,1)S(1)} %get-tuple-element.78.refs_3_), channel_id=1, source_target_pairs={{0,2},{2,0},{4,6},{6,4},{1,3},{3,1},{5,7},{7,5},{8,10},{10,8},{12,... | collective-permute-start | bytes 983048 | tf_op jit(solution)/shard_map/ppermute | solution.py:25
  55.0 17.8 %collective-permute-start.15 = (bf16[2,2,5,32,512]{4,3,2,1,0:T(8,128)(2,1)S(1)}, bf16[2,2,5,32,512]{4,3,2,1,0:T(8,128)(2,1)}, u32[]{:S(2)}, u32[]{:S(2)}) collective-permute-start(bf16[2,2,5,32,512]{4,3,2,1,0:T(8,128)(2,1)S(1)} %get-tuple-element.83.refs_0_), channel_id=1, source_target_pairs={{0,6},{2,4},{4,2},{6,0},{1,7},{3,5},{5,3},{7,1},{8,14},{10,12},{12... | collective-permute-start | bytes 1966088 | tf_op jit(solution)/shard_map/ppermute | solution.py:25
  55.6 17.2 %collective-permute-start.16 = (bf16[2,2,5,32,512]{4,3,2,1,0:T(8,128)(2,1)S(1)}, bf16[2,2,5,32,512]{4,3,2,1,0:T(8,128)(2,1)}, u32[]{:S(2)}, u32[]{:S(2)}) collective-permute-start(bf16[2,2,5,32,512]{4,3,2,1,0:T(8,128)(2,1)S(1)} %get-tuple-element.84.refs_1_), channel_id=1, source_target_pairs={{0,24},{8,16},{16,8},{24,0},{1,25},{9,17},{17,9},{25,1},{2,26},{10... | collective-permute-start | bytes 1966088 | tf_op jit(solution)/shard_map/ppermute | solution.py:25
  57.1 15.7 %collective-permute-start.17 = (bf16[2,2,5,32,512]{4,3,2,1,0:T(8,128)(2,1)}, bf16[2,2,5,32,512]{4,3,2,1,0:T(8,128)(2,1)}, u32[]{:S(2)}, u32[]{:S(2)}) collective-permute-start(bf16[2,2,5,32,512]{4,3,2,1,0:T(8,128)(2,1)} %get-tuple-element.85.refs_2_), channel_id=1, source_target_pairs={{0,2},{2,0},{4,6},{6,4},{1,3},{3,1},{5,7},{7,5},{8,10},{10,8},{12,... | collective-permute-start | bytes 1966088 | tf_op jit(solution)/shard_map/ppermute | solution.py:25
  57.8 15.0 %collective-permute-start.18 = (bf16[2,2,5,32,512]{4,3,2,1,0:T(8,128)(2,1)}, bf16[2,2,5,32,512]{4,3,2,1,0:T(8,128)(2,1)}, u32[]{:S(2)}, u32[]{:S(2)}) collective-permute-start(bf16[2,2,5,32,512]{4,3,2,1,0:T(8,128)(2,1)} %get-tuple-element.86.refs_3_), channel_id=1, source_target_pairs={{0,8},{8,0},{16,24},{24,16},{1,9},{9,1},{17,25},{25,17},{2,10},{10... | collective-permute-start | bytes 1966088 | tf_op jit(solution)/shard_map/ppermute | solution.py:25
  58.0 37.4 %collective-permute-start.2 = (bf16[1152,512]{1,0:T(8,128)(2,1)}, bf16[1152,512]{1,0:T(8,128)(2,1)S(1)}, u32[]{:S(2)}, u32[]{:S(2)}) collective-permute-start(bf16[1152,512]{1,0:T(8,128)(2,1)} %collective-permute-done.1.refs_0_), channel_id=1, source_target_pairs={{0,32},{32,0},{64,96},{96,64},{1,33},{33,1},{65,97},{97,65},{2,34}... | collective-permute-start | bytes 3538952 | tf_op jit(solution)/shard_map/ppermute | solution.py:25
  77.3 25.8 %collective-permute-start.19 = (bf16[2,4,3,32,512]{4,3,2,1,0:T(8,128)(2,1)}, bf16[2,4,3,32,512]{4,3,2,1,0:T(8,128)(2,1)}, u32[]{:S(2)}, u32[]{:S(2)}) collective-permute-start(bf16[2,4,3,32,512]{4,3,2,1,0:T(8,128)(2,1)} %get-tuple-element.91.refs_0_), channel_id=1, source_target_pairs={{0,24},{8,16},{16,8},{24,0},{1,25},{9,17},{17,9},{25,1},{2,26},{10... | collective-permute-start | bytes 2359304 | tf_op jit(solution)/shard_map/ppermute | solution.py:25
  78.2 25.0 %collective-permute-start.20 = (bf16[4,2,3,32,512]{4,3,2,1,0:T(8,128)(2,1)}, bf16[4,2,3,32,512]{4,3,2,1,0:T(8,128)(2,1)}, u32[]{:S(2)}, u32[]{:S(2)}) collective-permute-start(bf16[4,2,3,32,512]{4,3,2,1,0:T(8,128)(2,1)} %get-tuple-element.92.refs_1_), channel_id=1, source_target_pairs={{0,2},{2,0},{4,6},{6,4},{1,3},{3,1},{5,7},{7,5},{8,10},{10,8},{12,... | collective-permute-start | bytes 2359304 | tf_op jit(solution)/shard_map/ppermute | solution.py:25
  79.9 23.2 %collective-permute-start.21 = (bf16[2,4,3,32,512]{4,3,2,1,0:T(8,128)(2,1)}, bf16[2,4,3,32,512]{4,3,2,1,0:T(8,128)(2,1)}, u32[]{:S(2)}, u32[]{:S(2)}) collective-permute-start(bf16[2,4,3,32,512]{4,3,2,1,0:T(8,128)(2,1)} %get-tuple-element.93.refs_2_), channel_id=1, source_target_pairs={{0,8},{8,0},{16,24},{24,16},{1,9},{9,1},{17,25},{25,17},{2,10},{10... | collective-permute-start | bytes 2359304 | tf_op jit(solution)/shard_map/ppermute | solution.py:25
  80.2 22.9 %collective-permute-start.22 = (bf16[4,2,3,32,512]{4,3,2,1,0:T(8,128)(2,1)}, bf16[4,2,3,32,512]{4,3,2,1,0:T(8,128)(2,1)}, u32[]{:S(2)}, u32[]{:S(2)}) collective-permute-start(bf16[4,2,3,32,512]{4,3,2,1,0:T(8,128)(2,1)} %get-tuple-element.94.refs_3_), channel_id=1, source_target_pairs={{0,6},{2,4},{4,2},{6,0},{1,7},{3,5},{5,3},{7,1},{8,14},{10,12},{12... | collective-permute-start | bytes 2359304 | tf_op jit(solution)/shard_map/ppermute | solution.py:25
  103.1 16.3 %collective-permute-start.23 = (bf16[2,4,2,32,512]{4,3,2,1,0:T(8,128)(2,1)S(1)}, bf16[2,4,2,32,512]{4,3,2,1,0:T(8,128)(2,1)S(1)}, u32[]{:S(2)}, u32[]{:S(2)}) collective-permute-start(bf16[2,4,2,32,512]{4,3,2,1,0:T(8,128)(2,1)S(1)} %get-tuple-element.104.refs_0_.refs_4_.refs_8_), channel_id=1, source_target_pairs={{0,24},{8,16},{16,8},{24,0},{1,25},{9,17},{17,9},{25,1},{2,26},{10... | collective-permute-start | bytes 1572872 | tf_op jit(solution)/shard_map/ppermute | solution.py:25
  105.0 14.5 %collective-permute-start.24 = (bf16[4,2,2,32,512]{4,3,2,1,0:T(8,128)(2,1)S(1)}, bf16[4,2,2,32,512]{4,3,2,1,0:T(8,128)(2,1)S(1)}, u32[]{:S(2)}, u32[]{:S(2)}) collective-permute-start(bf16[4,2,2,32,512]{4,3,2,1,0:T(8,128)(2,1)S(1)} %get-tuple-element.105.refs_1_.refs_5_.refs_9_), channel_id=1, source_target_pairs={{0,2},{2,0},{4,6},{6,4},{1,3},{3,1},{5,7},{7,5},{8,10},{10,8},{12,... | collective-permute-start | bytes 1572872 | tf_op jit(solution)/shard_map/ppermute | solution.py:25
  105.0 14.5 %collective-permute-start.25 = (bf16[2,4,2,32,512]{4,3,2,1,0:T(8,128)(2,1)S(1)}, bf16[2,4,2,32,512]{4,3,2,1,0:T(8,128)(2,1)S(1)}, u32[]{:S(2)}, u32[]{:S(2)}) collective-permute-start(bf16[2,4,2,32,512]{4,3,2,1,0:T(8,128)(2,1)S(1)} %get-tuple-element.106.refs_2_.refs_6_.refs_10_), channel_id=1, source_target_pairs={{0,8},{8,0},{16,24},{24,16},{1,9},{9,1},{17,25},{25,17},{2,10},{10... | collective-permute-start | bytes 1572872 | tf_op jit(solution)/shard_map/ppermute | solution.py:25
  105.5 13.9 %collective-permute-start.26 = (bf16[4,2,2,32,512]{4,3,2,1,0:T(8,128)(2,1)S(1)}, bf16[4,2,2,32,512]{4,3,2,1,0:T(8,128)(2,1)S(1)}, u32[]{:S(2)}, u32[]{:S(2)}) collective-permute-start(bf16[4,2,2,32,512]{4,3,2,1,0:T(8,128)(2,1)S(1)} %get-tuple-element.107.refs_3_.refs_7_.refs_11_), channel_id=1, source_target_pairs={{0,6},{2,4},{4,2},{6,0},{1,7},{3,5},{5,3},{7,1},{8,14},{10,12},{12... | collective-permute-start | bytes 1572872 | tf_op jit(solution)/shard_map/ppermute | solution.py:25
  160.4 18.9 %collective-permute-start.34 = (bf16[576,512]{1,0:T(8,128)(2,1)S(1)}, bf16[576,512]{1,0:T(8,128)(2,1)S(1)}, u32[]{:S(2)}, u32[]{:S(2)}) collective-permute-start(bf16[576,512]{1,0:T(8,128)(2,1)S(1)} %pad_maximum_fusion.refs_0_), channel_id=1, source_target_pairs={{0,64},{32,96},{64,0},{96,32},{1,65},{33,97},{65,1},{97,33},{2,66}... | collective-permute-start | bytes 1769480 | tf_op jit(solution)/shard_map/ppermute | solution.py:25
  172.4 34.7 %collective-permute-start.27 = (bf16[256,512]{1,0:T(8,128)(2,1)S(1)}, bf16[256,512]{1,0:T(8,128)(2,1)S(1)}, u32[]{:S(2)}, u32[]{:S(2)}) collective-permute-start(bf16[256,512]{1,0:T(8,128)(2,1)S(1)} %bitcast.46), channel_id=1, source_target_pairs={{0,32},{32,0},{64,96},{96,64},{1,33},{33,1},{65,97},{97,65},{2,34}... | collective-permute-start | bytes 786440 | tf_op jit(solution)/shard_map/ppermute | solution.py:25
  178.1 16.4 %collective-permute-start.28 = (bf16[256,512]{1,0:T(8,128)(2,1)S(1)}, bf16[256,512]{1,0:T(8,128)(2,1)S(1)}, u32[]{:S(2)}, u32[]{:S(2)}) collective-permute-start(bf16[256,512]{1,0:T(8,128)(2,1)S(1)} %bitcast.47), channel_id=1, source_target_pairs={{0,64},{32,96},{64,0},{96,32},{1,65},{33,97},{65,1},{97,33},{2,66}... | collective-permute-start | bytes 786440 | tf_op jit(solution)/shard_map/ppermute | solution.py:25
  178.9 22.2 %collective-permute-start.33 = (bf16[576,512]{1,0:T(8,128)(2,1)S(1)}, bf16[576,512]{1,0:T(8,128)(2,1)S(1)}, u32[]{:S(2)}, u32[]{:S(2)}) collective-permute-start(bf16[576,512]{1,0:T(8,128)(2,1)S(1)} %pad_maximum_fusion.refs_0_), channel_id=1, source_target_pairs={{0,32},{32,0},{64,96},{96,64},{1,33},{33,1},{65,97},{97,65},{2,34}... | collective-permute-start | bytes 1769480 | tf_op jit(solution)/shard_map/ppermute | solution.py:25
  179.3 21.8 %collective-permute-start.35 = (bf16[576,512]{1,0:T(8,128)(2,1)S(1)}, bf16[576,512]{1,0:T(8,128)(2,1)S(1)}, u32[]{:S(2)}, u32[]{:S(2)}) collective-permute-start(bf16[576,512]{1,0:T(8,128)(2,1)S(1)} %collective-permute-done.34.refs_2_), channel_id=1, source_target_pairs={{0,32},{32,0},{64,96},{96,64},{1,33},{33,1},{65,97},{97,65},{2,34}... | collective-permute-start | bytes 1769480 | tf_op jit(solution)/shard_map/ppermute | solution.py:25
  190.9 9.0 %collective-permute-start.31 = (bf16[256,512]{1,0:T(8,128)(2,1)S(1)}, bf16[256,512]{1,0:T(8,128)(2,1)S(1)}, u32[]{:S(2)}, u32[]{:S(2)}) collective-permute-start(bf16[256,512]{1,0:T(8,128)(2,1)S(1)} %bitcast.49), channel_id=1, source_target_pairs={{0,64},{32,96},{64,0},{96,32},{1,65},{33,97},{65,1},{97,33},{2,66}... | collective-permute-start | bytes 786440 | tf_op jit(solution)/shard_map/ppermute | solution.py:25
  194.5 12.7 %collective-permute-start.30 = (bf16[256,512]{1,0:T(8,128)(2,1)S(1)}, bf16[256,512]{1,0:T(8,128)(2,1)S(1)}, u32[]{:S(2)}, u32[]{:S(2)}) collective-permute-start(bf16[256,512]{1,0:T(8,128)(2,1)S(1)} %bitcast.50), channel_id=1, source_target_pairs={{0,32},{32,0},{64,96},{96,64},{1,33},{33,1},{65,97},{97,65},{2,34}... | collective-permute-start | bytes 786440 | tf_op jit(solution)/shard_map/ppermute | solution.py:25
  199.9 7.2 %collective-permute-start.29 = (bf16[256,512]{1,0:T(8,128)(2,1)S(1)}, bf16[256,512]{1,0:T(8,128)(2,1)S(1)}, u32[]{:S(2)}, u32[]{:S(2)}) collective-permute-start(bf16[256,512]{1,0:T(8,128)(2,1)S(1)} %collective-permute-done.28.refs_2_), channel_id=1, source_target_pairs={{0,32},{32,0},{64,96},{96,64},{1,33},{33,1},{65,97},{97,65},{2,34}... | collective-permute-start | bytes 786440 | tf_op jit(solution)/shard_map/ppermute | solution.py:25
  201.1 6.1 %collective-permute-start.32 = (bf16[256,512]{1,0:T(8,128)(2,1)S(1)}, bf16[256,512]{1,0:T(8,128)(2,1)S(1)}, u32[]{:S(2)}, u32[]{:S(2)}) collective-permute-start(bf16[256,512]{1,0:T(8,128)(2,1)S(1)} %collective-permute-done.31.refs_6_), channel_id=1, source_target_pairs={{0,32},{32,0},{64,96},{96,64},{1,33},{33,1},{65,97},{97,65},{2,34}... | collective-permute-start | bytes 786440 | tf_op jit(solution)/shard_map/ppermute | solution.py:25
  (30 other events, 280.8 us)

commit v2 on v1

v2 whole, which is shorter than its diff:
```python
import functools

import jax
import jax.numpy as jnp
import numpy as np
from jax import lax
from jax.experimental import pallas as pl
from jax.experimental.pallas import tpu as pltpu
from jax.sharding import Mesh
from jax.sharding import PartitionSpec as P

NORM_EPS = 0.00064
N_HEAD = 4
CH = 64
BF = jnp.bfloat16
F32 = jnp.float32


STEPS = (("x", 1), ("z", 1), ("x", 3), ("z", 3))


def swap(a, axes, bits):
    sizes = {"x": 4, "z": 4, "yl": 2, "head": 4}
    names = ("yh", "core") if axes == "head" else axes
    return lax.ppermute(a, names, [(i, i ^ bits) for i in range(sizes[axes])])


def order_of(part):
    return [STEPS[(part + n) % 4] for n in range(4)]


def after(value, other):
    return lax.optimization_barrier((value, other))[0]


ANY = pl.BlockSpec(memory_space=pl.ANY)


def in_hbm(*arrays):
    return [pltpu.with_memory_space_constraint(a, pltpu.HBM) for a in arrays]


def cost(flops, nbytes, trans=0):
    return pl.CostEstimate(flops=flops, bytes_accessed=nbytes, transcendentals=trans)


def params(axes):
    return pltpu.CompilerParams(
        dimension_semantics=("arbitrary",) * axes, vmem_limit_bytes=48 << 20
    )


def split_kernel(place_ref, keep_ref, count_ref, spot_ref, *refs):
    mats, hid, newest, prior = refs[:5], refs[5], refs[6], refs[7]
    outs, own_ref, shift_ref = refs[8:12], refs[12], refs[13]
    buf, old, sem = refs[14:]
    tokens, slots = hid.shape[0], newest.shape[0]
    copies = [pltpu.make_async_copy(mats[m], buf.at[m], sem.at[m]) for m in range(5)]
    copies += [
        pltpu.make_async_copy(prior, old, sem.at[5]),
        pltpu.make_async_copy(newest, own_ref.at[pl.ds(tokens, slots)], sem.at[6]),
        pltpu.make_async_copy(hid, own_ref.at[pl.ds(0, tokens)], sem.at[7]),
    ]
    for copy in copies:
        copy.start()
    row = lax.broadcasted_iota(jnp.int32, (slots, 512), 0)
    keep = jnp.zeros((slots, 512), F32)
    for n in range(slots):
        keep = jnp.where(row == n, keep_ref[n].astype(F32), keep)
    for m in range(5):
        copies[m].wait()
    for d in range(4):
        at = pl.multiple_of((place_ref[0] ^ d) * 512, 512)
        for m in range(5):
            outs[d][m] = buf[m, :, pl.ds(at, 512)].astype(BF)
    copies[5].wait()
    kept = jnp.where(keep > 0.5, old[...].astype(F32), 0.0)
    own_ref[tokens + slots :] = kept.astype(BF)
    copies[6].wait()
    copies[7].wait()
    shift = own_ref[tokens : tokens + slots].astype(F32)
    few = lax.broadcasted_iota(jnp.int32, (16, 512), 0)
    for p in range(2):
        at = p * (tokens // 2) + count_ref[p] - 1
        base = pl.multiple_of((at >> 4) << 4, 16)
        near = own_ref[pl.ds(base, 16)].astype(F32)
        last = jnp.sum(jnp.where(few == (at & 15), near, 0.0), axis=0, keepdims=True)
        shift = jnp.where(row == spot_ref[p], last, shift)
    shift_ref[...] = shift.astype(BF)


def split(place, keep, counts, spots, matrices, hidden, newest, prior):
    rows, width = matrices[0].shape[0], matrices[0].shape[1] // N_HEAD
    shape = (len(matrices), rows, width)
    total = hidden.shape[0] + 2 * newest.shape[0]
    hbm = pl.BlockSpec(memory_space=pltpu.HBM)
    out = pl.pallas_call(
        split_kernel,
        out_shape=[jax.ShapeDtypeStruct(shape, BF)] * 4
        + [jax.ShapeDtypeStruct((total, width), BF), jax.ShapeDtypeStruct(newest.shape, BF)],
        grid_spec=pltpu.PrefetchScalarGridSpec(
            num_scalar_prefetch=4,
            grid=(1,),
            in_specs=[hbm] * 8,
            out_specs=[pl.BlockSpec(shape, lambda i, *s: (0, 0, 0))] * 4
            + [
                pl.BlockSpec((total, width), lambda i, *s: (0, 0)),
                pl.BlockSpec(newest.shape, lambda i, *s: (0, 0)),
            ],
            scratch_shapes=[
                pltpu.VMEM((5,) + matrices[0].shape, F32),
                pltpu.VMEM(newest.shape, BF),
                pltpu.SemaphoreType.DMA((8,)),
            ],
        ),
        compiler_params=params(1),
        name="split",
    )(place, keep, counts, spots, *in_hbm(*matrices, hidden, newest, prior))
    return out[:4], out[4], out[5]


def in_order(own, other, yl):
    first = yl == 0
    return jnp.concatenate(
        [jnp.where(first, own, other), jnp.where(first, other, own)], axis=-2
    )


def axis_dim(axis):
    return 0 if axis == "z" else 1


def places(p, n, place_ref):
    axis, bits = order_of(p)[n]
    pos = place_ref[1] if axis == "z" else place_ref[2]
    seen = [b for name, b in order_of(p)[:n] if name == axis]
    offsets = [0] + seen
    return [pos ^ o for o in offsets], [pos ^ bits ^ o for o in offsets]


def part_of(ref, dim, i, lot):
    return ref.at[i, :, lot] if dim == 0 else ref.at[:, i, lot]


def pack_kernel(place_ref, *refs, n, lot):
    owns, recvs, outs, sem = refs[:4], refs[4:8], refs[8:12], refs[12]
    copies = []
    for p in range(4):
        dim = axis_dim(order_of(p)[n][0])
        own_at, recv_at = places(p, n, place_ref)
        if len(own_at) == 1:
            own_at, recv_at = [0], [1]
        for src, at in ((owns[p], own_at), (recvs[p], recv_at)):
            for i, j in enumerate(at):
                source = part_of(src, dim, i, lot)
                target = part_of(outs[p], dim, j, slice(None))
                copies.append(pltpu.make_async_copy(source, target, sem.at[len(copies)]))
    for copy in copies:
        copy.start()
    for copy in copies:
        copy.wait()


def pack(place, owns, recvs, n, lot):
    shapes = []
    for p in range(4):
        shape = list(owns[p].shape)
        shape[axis_dim(order_of(p)[n][0])] *= 2
        shape[2] = lot.stop - lot.start
        shapes.append(jax.ShapeDtypeStruct(tuple(shape), BF))
    return pl.pallas_call(
        functools.partial(pack_kernel, n=n, lot=lot),
        out_shape=shapes,
        grid_spec=pltpu.PrefetchScalarGridSpec(
            num_scalar_prefetch=1,
            grid=(1,),
            in_specs=[ANY] * 8,
            out_specs=[pl.BlockSpec(a.shape, lambda i, s: (0, 0, 0, 0, 0)) for a in shapes],
            scratch_shapes=[pltpu.SemaphoreType.DMA((16,))],
        ),
        compiler_params=params(1),
        cost_estimate=cost(0, 8 << 20),
        name="pack",
    )(place, *in_hbm(*owns, *recvs))


def swap_all(owns, n):
    return [swap(owns[p], *order_of(p)[n]) for p in range(4)]


def copy_weights(pieces, m, place_ref, buf, sem):
    for p in range(4):
        dim = axis_dim(order_of(p)[3][0])
        own_at, recv_at = places(p, 3, place_ref)
        for src, at in ((pieces[p], own_at), (pieces[p + 4], recv_at)):
            for i, j in enumerate(at):
                target = buf.at[p * 4 + j] if dim == 0 else buf.at[pl.ds(p * 4, 4), j]
                pltpu.make_async_copy(part_of(src, dim, i, m), target, sem).start()


def wait_weights(buf, sem):
    pltpu.make_async_copy(buf, buf, sem).wait()


def mix_kernel(place_ref, count_ref, *refs, d, length):
    hid_ref, mu_ref, narrow_ref = refs[:3]
    refs = refs[3:]
    if d > 0:
        low_in, refs = refs[0], refs[2:]
    if d == 3:
        widen_ref, speed_ref, refs = refs[0], refs[1], refs[2:]
    x_ref, low_ref, cur_ref, step_ref = refs
    i = pl.program_id(0)
    rows = cur_ref.shape[0]
    slots = hid_ref.shape[0] - rows
    tokens = rows - slots

    @pl.when(i == 0)
    def _():
        cur = hid_ref[:rows].astype(F32)
        cur_ref[...] = cur
        seq = cur[:tokens]
        at = lax.broadcasted_iota(jnp.int32, seq.shape, 0)
        before = jnp.where((at & (length - 1)) == 0, 0.0, pltpu.roll(seq, 1, 0))
        step_ref[:tokens] = before - seq
        step_ref[tokens:] = hid_ref[rows:].astype(F32) - cur[tokens:]

    mixed = (cur_ref[...] + step_ref[...] * mu_ref[pl.ds(i, 1), :]).astype(BF)
    x_ref[0] = mixed

    @pl.when(i == 3)
    def _():
        low = lax.dot_general(
            mixed, narrow_ref[...], (((1,), (1,)), ((), ())), preferred_element_type=F32
        )
        if d > 0:
            low = low + low_in[...]
        if d < 3:
            low_ref[...] = low
        else:
            lowrank = jnp.tanh(low).astype(BF)
            rate = jnp.exp(jnp.dot(lowrank, widen_ref[...], preferred_element_type=F32))
            log_decay = -speed_ref[...] * rate
            at = lax.broadcasted_iota(jnp.int32, (rows, 512), 0)
            limit = jnp.where(
                at < length,
                count_ref[0],
                jnp.where(at < 2 * length, count_ref[1] + length, rows),
            )
            low_ref[...] = jnp.where(at < limit, log_decay, 0.0)


def mix(place, counts, hidden, d, mu, narrow, low, held, widen, speed, slots, length):
    rows = hidden.shape[0] - slots
    once = lambda i, s, c: (0, 0)
    args = in_hbm(hidden, mu, narrow)
    specs = [
        pl.BlockSpec(hidden.shape, once),
        pl.BlockSpec((5, 512), lambda i, s, c: (0, s[0] ^ d)),
        pl.BlockSpec((64, 512), lambda i, s, c: (0, s[0] ^ d)),
    ]
    alias = {}
    if d > 0:
        args += in_hbm(low, held)
        specs += [pl.BlockSpec(low.shape, once), ANY]
        alias = {6: 0}
    wide = 64
    if d == 3:
        args += in_hbm(widen, speed)
        specs += [pl.BlockSpec(widen.shape, once), pl.BlockSpec(speed.shape, once)]
        wide = 512
    return pl.pallas_call(
        functools.partial(mix_kernel, d=d, length=length),
        out_shape=(
            jax.ShapeDtypeStruct((5, rows, 2048), BF),
            jax.ShapeDtypeStruct((rows, wide), F32),
        ),
        grid_spec=pltpu.PrefetchScalarGridSpec(
            num_scalar_prefetch=2,
            grid=(5,),
            in_specs=specs,
            out_specs=(
                pl.BlockSpec((1, rows, 512), lambda i, s, c: (i, 0, d)),
                pl.BlockSpec((rows, wide), once),
            ),
            scratch_shapes=[pltpu.VMEM((rows, 512), F32), pltpu.VMEM((rows, 512), F32)],
        ),
        input_output_aliases=alias,
        compiler_params=params(1),
        cost_estimate=cost(20 * rows * 512, 12 * rows * 512),
        name="mix",
    )(place, counts, *args)


def rkv_kernel(place_ref, x_ref, *refs):
    pieces = refs[:8]
    out_ref, buf, sem = refs[8:]
    i, j = pl.program_id(0), pl.program_id(1)
    slot = lax.rem(i, 2)

    @pl.when(jnp.logical_and(i == 0, j == 0))
    def _():
        copy_weights(pieces, 0, place_ref, buf.at[0], sem.at[0])

    @pl.when(j == 0)
    def _():
        @pl.when(i < 2)
        def _():
            copy_weights(pieces, i + 1, place_ref, buf.at[1 - slot], sem.at[1 - slot])

        wait_weights(buf.at[slot], sem.at[slot])

    w = buf[slot].reshape(2048, 512)
    out_ref[0] = jnp.dot(x_ref[0], w, preferred_element_type=F32).astype(out_ref.dtype)


def project_rkv(place, mixed, pieces, tile):
    rows = mixed.shape[1]
    return pl.pallas_call(
        rkv_kernel,
        out_shape=jax.ShapeDtypeStruct((3, rows, 512), BF),
        grid_spec=pltpu.PrefetchScalarGridSpec(
            num_scalar_prefetch=1,
            grid=(3, rows // tile),
            in_specs=[pl.BlockSpec((1, tile, 2048), lambda i, j, s: (i, j, 0))] + [ANY] * 8,
            out_specs=pl.BlockSpec((1, tile, 512), lambda i, j, s: (i, j, 0)),
            scratch_shapes=[
                pltpu.VMEM((2, 16, 4, 32, 512), BF),
                pltpu.SemaphoreType.DMA((2,)),
            ],
        ),
        compiler_params=params(2),
        cost_estimate=cost(6 * rows * 2048 * 512, 24 << 20),
        name="project_rkv",
    )(place, mixed, *pieces)


def gate_kernel(place_ref, x_ref, *refs):
    pieces = refs[:8]
    out_ref, buf, sem = refs[8:]

    @pl.when(pl.program_id(0) == 0)
    def _():
        copy_weights(pieces, 0, place_ref, buf, sem)
        wait_weights(buf, sem)

    total = jnp.dot(x_ref[0], buf[...].reshape(2048, 512), preferred_element_type=F32)
    out_ref[...] = (total / (1.0 + jnp.exp(-total))).astype(out_ref.dtype)


def project_gate(place, mixed, pieces, tile):
    rows = mixed.shape[1]
    return pl.pallas_call(
        gate_kernel,
        out_shape=jax.ShapeDtypeStruct((rows, 512), BF),
        grid_spec=pltpu.PrefetchScalarGridSpec(
            num_scalar_prefetch=1,
            grid=(rows // tile,),
            in_specs=[pl.BlockSpec((1, tile, 2048), lambda j, s: (4, j, 0))] + [ANY] * 8,
            out_specs=pl.BlockSpec((tile, 512), lambda j, s: (j, 0)),
            scratch_shapes=[pltpu.VMEM((16, 4, 32, 512), BF), pltpu.SemaphoreType.DMA(())],
        ),
        compiler_params=params(1),
        cost_estimate=cost(2 * rows * 2048 * 512, 8 << 20),
        name="project_gate",
    )(place, mixed, *pieces)


def result_kernel(place_ref, count_ref, spot_ref, *refs, spans, t0, slot0, chained):
    lots = len(spans)
    xs, pieces = refs[: 4 * lots], refs[4 * lots : 4 * lots + 8]
    rest = refs[4 * lots + 8 + (2 if chained else 0) :]
    out_ref, slot_ref, buf, sem = rest
    copy_weights(pieces, 1, place_ref, buf, sem)
    wait_weights(buf, sem)
    start = slot = 0
    for lot, span in enumerate(spans):
        total = None
        for d in range(4):
            w = buf[4 * d : 4 * d + 4].reshape(512, 512)
            term = jnp.dot(xs[4 * lot + d][...], w, preferred_element_type=F32)
            total = term if total is None else total + term
        at = lax.broadcasted_iota(jnp.int32, (span, 512), 0) + (t0 + start)
        for p in range(2):
            own = jnp.where(at < count_ref[p], total[p * span : (p + 1) * span], 0.0)
            out_ref[p, start : start + span] = own.astype(out_ref.dtype)
        start += span
        more = total.shape[0] - 2 * span
        which = lax.broadcasted_iota(jnp.int32, (more, 512), 0) + (slot0 + slot)
        taken = jnp.logical_or(which == spot_ref[0], which == spot_ref[1])
        own = jnp.where(taken, 0.0, total[2 * span :])
        slot_ref[slot : slot + more] = own.astype(slot_ref.dtype)
        slot += more


def project_result(place, counts, spots, xs, pieces, spans, t0, earlier, length, all_slots):
    span = sum(spans)
    slots = sum(xs[4 * n].shape[0] - 2 * spans[n] for n in range(len(spans)))
    once = lambda i, *s: (0, 0)
    chained = earlier is not None
    block = t0 // span
    return pl.pallas_call(
        functools.partial(
            result_kernel, spans=spans, t0=t0, slot0=block * slots, chained=chained
        ),
        out_shape=[
            jax.ShapeDtypeStruct((2, length, 512), BF),
            jax.ShapeDtypeStruct((all_slots, 512), BF),
        ],
        grid_spec=pltpu.PrefetchScalarGridSpec(
            num_scalar_prefetch=3,
            grid=(1,),
            in_specs=[pl.BlockSpec(a.shape, once) for a in xs] + [ANY] * (10 if chained else 8),
            out_specs=[
                pl.BlockSpec((2, span, 512), lambda i, *s: (0, block, 0)),
                pl.BlockSpec((slots, 512), lambda i, *s: (block, 0)),
            ],
            scratch_shapes=[pltpu.VMEM((16, 4, 32, 512), BF), pltpu.SemaphoreType.DMA(())],
        ),
        input_output_aliases={3 + len(xs) + 8: 0, 3 + len(xs) + 9: 1} if chained else {},
        compiler_params=params(1),
        cost_estimate=cost(4 * span * 2048 * 512, 8 << 20),
        name="project_result",
    )(place, counts, spots, *xs, *pieces, *(earlier if chained else []))


SLOT_BLOCK = 8


def head_mask(value):
    row = lax.broadcasted_iota(jnp.int32, (128, 128), 0) < 64
    col = lax.broadcasted_iota(jnp.int32, (128, 128), 1) < 64
    return jnp.where(row == col, value, 0.0).astype(BF)


def in_two(a):
    hi = a.astype(BF)
    return jnp.concatenate([hi, (a - hi.astype(F32)).astype(BF)], axis=1)


def turn_decode(r_ref, k_ref, w_ref, rt_ref, kt_ref, dt_ref):
    r = r_ref[0].astype(F32)
    k = k_ref[0].astype(F32)
    decay = jnp.exp(w_ref[...])
    for q in range(4):
        cols = slice(128 * q, 128 * q + 128)

        def turned(a):
            t = jnp.transpose(a[:, cols])
            return jnp.concatenate([t[:64], t[64:]], axis=1)

        rt_ref[q] = turned(r).astype(BF)
        kt_ref[q] = turned(k).astype(BF)
        dt_ref[q] = in_two(turned(decay))


def decode_slots(
    first, keep_ref, s_ref, r_ref, k_ref, v_ref, g_ref, vec_ref, next_ref, rt_ref, kt_ref, dt_ref,
    y_ref,
):
    here = pl.ds(pl.multiple_of(first, SLOT_BLOCK), SLOT_BLOCK)
    v = v_ref[0, here].astype(F32)
    row = lax.broadcasted_iota(jnp.int32, (128, 128), 0)
    low = lax.broadcasted_iota(jnp.int32, (128, 128), 1) < 64
    for s in range(SLOT_BLOCK):
        slot = first + s
        hit = row == jnp.where(low, slot, slot + 64)
        pick = jnp.where(hit, 1.0, 0.0).astype(BF)
        kept = jnp.where(hit, keep_ref[slot].astype(F32), 0.0).astype(BF)
        r_b = jnp.dot(rt_ref[...].reshape(256, 128), kept, preferred_element_type=F32)
        k_b = jnp.dot(kt_ref[...].reshape(256, 128), pick, preferred_element_type=F32)
        d_b = jnp.dot(
            dt_ref[...].reshape(256, 256),
            jnp.concatenate([kept, kept], axis=0),
            preferred_element_type=F32,
        )
        for q in range(4):
            span = slice(64 * q, 64 * q + 64)
            cols = slice(128 * q, 128 * q + 128)
            state = jnp.concatenate([s_ref[s, 2 * q], s_ref[s, 2 * q + 1]], axis=1)
            after_it = d_b[span] * state + k_b[span] * v[s : s + 1, cols]
            next_ref[s, 2 * q] = after_it[:, :64]
            next_ref[s, 2 * q + 1] = after_it[:, 64:]
            y_ref[s : s + 1, cols] = jnp.sum(r_b[span] * state, axis=0, keepdims=True)
    r = r_ref[0, here].astype(F32)
    k = k_ref[0, here].astype(F32)
    reward, scale, offset = vec_ref[0:1], vec_ref[1:2], vec_ref[2:3]
    own = r * reward * k
    ones = jnp.concatenate([head_mask(1.0)] * 2, axis=0)
    mean_of = jnp.concatenate([head_mask(1.0 / 64)] * 2, axis=0)
    out = []
    for q in range(4):
        cols = slice(128 * q, 128 * q + 128)
        total = jnp.dot(in_two(own[:, cols]), ones, preferred_element_type=F32)
        y = y_ref[:, cols] + total * v[:, cols]
        center = y - jnp.dot(in_two(y), mean_of, preferred_element_type=F32)
        spread = jnp.dot(in_two(center * center), mean_of, preferred_element_type=F32)
        normed = center * lax.rsqrt(spread + NORM_EPS) * scale[:, cols] + offset[:, cols]
        out.append((normed * g_ref[here, cols].astype(F32)).astype(BF))
    return jnp.concatenate(out, axis=1)


def span_tables():
    t = np.arange(CH)
    blocks = []
    size = 4
    while size <= CH:
        start = (t // size) * size
        mid = start + size // 2
        m = np.zeros((CH, CH), np.float32)
        for i in range(CH):
            if i >= mid[i]:
                m[i, mid[i] : i] = 1.0
            else:
                m[i, i + 1 : mid[i]] = 1.0
        blocks.append(m)
        size *= 2
    before = (t[None, :] < t[:, None]).astype(np.float32)
    after = (t[None, :] > t[:, None]).astype(np.float32)
    whole = np.ones((8, CH), np.float32)
    table = np.concatenate(blocks + [before, after, whole])
    return np.concatenate([table, table], axis=1)


LEVELS = int(np.log2(CH))


def wkv_kernel(
    count_ref, keep_ref, table_ref, *refs, t0, span, slot0, last, chained, prompts
):
    ins, refs = refs[: 5 * prompts], refs[5 * prompts :]
    vec_ref, start_ref, slots_ref, rd_ref, kd_ref, vd_ref, wd_ref, gd_ref = refs[:8]
    refs = refs[9:] if chained else refs[8:]
    out_ref, state_ref, next_ref = refs[:3]
    turned = refs[-4:-1]
    y_ref = refs[-1]
    c = pl.program_id(0)

    @pl.when(c == 0)
    def _():
        state_ref[...] = start_ref[...]
        turn_decode(rd_ref, kd_ref, wd_ref, *turned)

    table = table_ref[...]
    row = lax.broadcasted_iota(jnp.int32, (CH, 512), 0)
    low = lax.broadcasted_iota(jnp.int32, (CH, 128), 1) < 64
    arow = lax.broadcasted_iota(jnp.int32, (CH, 2 * CH), 0)
    acol = lax.broadcasted_iota(jnp.int32, (CH, 2 * CH), 1) & (CH - 1)
    diff = arow ^ acol
    causal = arow > acol
    same_head = (lax.broadcasted_iota(jnp.int32, (128, 128), 0) < 64) == (
        lax.broadcasted_iota(jnp.int32, (128, 128), 1) < 64
    )
    mean_of = head_mask(1.0 / 64)
    mean_two = jnp.concatenate([mean_of, mean_of], axis=0)
    reward, scale, offset = vec_ref[0:1], vec_ref[1:2], vec_ref[2:3]
    contract_lanes = (((1,), (1,)), ((), ()))
    contract_rows = (((0,), (0,)), ((), ()))

    def both_heads(a):
        zero = jnp.zeros_like(a)
        return jnp.concatenate([jnp.where(low, a, zero), jnp.where(low, zero, a)], axis=0)

    def lanes_dot(a, b):
        return lax.dot_general(a, b, contract_lanes, preferred_element_type=F32)

    def dot(a, b):
        return jnp.dot(a, b, preferred_element_type=F32)

    streams = [(p, q) for p in range(prompts) for q in range(4)]
    cols = [slice(128 * q, 128 * q + 128) for q in range(4)]
    keys, own, mixed, r_dec, k_dec, whole, values = {}, {}, {}, {}, {}, {}, {}
    for p in range(prompts):
        r_ref, k_ref, v_ref, w_ref, g_ref = ins[5 * p : 5 * p + 5]
        live = (row + (c * CH + t0)) < count_ref[p]
        r = r_ref[0].astype(F32)
        k = jnp.where(live, k_ref[0].astype(F32), 0.0)
        values[p] = v_ref[0]
        w = w_ref[...]
        w_hi = w.astype(BF)
        w_lo = (w - w_hi.astype(F32)).astype(BF)
        factors = jnp.exp(dot(table, jnp.concatenate([w_hi, w_lo], axis=0)))
        r_dec[p] = (r * factors[(LEVELS - 1) * CH : LEVELS * CH]).astype(BF)
        k_dec[p] = (k * factors[LEVELS * CH : (LEVELS + 1) * CH]).astype(BF)
        whole[p] = factors[(LEVELS + 1) * CH : (LEVELS + 1) * CH + 1]
        weighted = r * reward
        hi = weighted.astype(BF)
        own[p] = (hi, (weighted - hi.astype(F32)).astype(BF))
        keys[p] = k.astype(BF)
        mixed[p] = [jnp.where((row & 1) == 1, r, k).astype(BF)]
        for level in range(1, LEVELS):
            pick = jnp.where((row & (1 << level)) != 0, r, k)
            mixed[p].append((pick * factors[(level - 1) * CH : level * CH]).astype(BF))
    scores = {}
    for p, q in streams:
        key = both_heads(keys[p][:, cols[q]])
        s = lanes_dot(
            jnp.concatenate([half[:, cols[q]] for half in own[p]], axis=1),
            jnp.concatenate([key, key], axis=1),
        )
        scores[p, q] = jnp.where(diff == 0, s, 0.0)
    for level in range(LEVELS):
        here = jnp.logical_and(causal, (diff >> level) == 1)
        for p, q in streams:
            a = mixed[p][level][:, cols[q]]
            scores[p, q] = jnp.where(here, lanes_dot(a, both_heads(a)), scores[p, q])
    y = {}
    for p, q in streams:
        v = values[p][:, cols[q]]
        state = state_ref[p, q]
        y[p, q] = dot(scores[p, q].astype(BF), both_heads(v)) + lanes_dot(
            r_dec[p][:, cols[q]], state.astype(BF)
        )
        added = lax.dot_general(v, k_dec[p][:, cols[q]], contract_rows, preferred_element_type=F32)
        state_ref[p, q] = state * whole[p][:, cols[q]] + jnp.where(same_head, added, 0.0)
    center = {n: y[n] - dot(in_two(y[n]), mean_two) for n in streams}
    spread = {n: dot((center[n] * center[n]).astype(BF), mean_of) for n in streams}
    for p, q in streams:
        normed = center[p, q] * lax.rsqrt(spread[p, q] + NORM_EPS)
        gate = ins[5 * p + 4][:, cols[q]].astype(F32)
        at = pl.multiple_of(p * span + c * CH, CH)
        out_ref[pl.ds(at, CH), cols[q]] = (
            (normed * scale[:, cols[q]] + offset[:, cols[q]]) * gate
        ).astype(out_ref.dtype)

    done = decode_slots(
        slot0 + c * SLOT_BLOCK, keep_ref, slots_ref, rd_ref, kd_ref, vd_ref, gd_ref, vec_ref,
        next_ref, *turned, y_ref,
    )
    at = pl.multiple_of(prompts * span + c * SLOT_BLOCK, SLOT_BLOCK)
    out_ref[pl.ds(at, SLOT_BLOCK), :] = done

    if last:
        final_ref = refs[3]

        @pl.when(c == pl.num_programs(0) - 1)
        def _():
            for p, q in streams:
                whole_state = jnp.transpose(state_ref[p, q])
                final_ref[p, 2 * q] = whole_state[:64, :64]
                final_ref[p, 2 * q + 1] = whole_state[64:, 64:]


def wkv(counts, keep, rkv, log_decay, gate, vectors, start, states, earlier, t0, t1, length):
    prompts, slots = start.shape[0], states.shape[0]
    table = jnp.asarray(span_tables(), BF)
    c0, per, span = t0 // CH, length // CH, t1 - t0
    chunks = span // CH
    last, chained = t1 == length, earlier is not None
    at = prompts * length // slots

    def part(n, p):
        return pl.BlockSpec((1, CH, 512), lambda c, s, k: (n, p * per + c + c0, 0))

    def flat(p):
        return pl.BlockSpec((CH, 512), lambda c, s, k: (p * per + c + c0, 0))

    def slot_part(n):
        return pl.BlockSpec((1, slots, 512), lambda c, s, k: (n, at, 0))

    slot_flat = pl.BlockSpec((slots, 512), lambda c, s, k: (at, 0))
    big = pl.BlockSpec((SLOT_BLOCK, 8, 64, 64), lambda c, s, k: (c + c0, 0, 0, 0))
    held = pl.BlockSpec((prompts, 4, 128, 128), lambda c, s, k: (0, 0, 0, 0))
    rows = prompts * span + chunks * SLOT_BLOCK
    out_shape = [
        jax.ShapeDtypeStruct((rows, 512), BF),
        jax.ShapeDtypeStruct((prompts, 4, 128, 128), F32),
        jax.ShapeDtypeStruct(states.shape, F32),
    ]
    out_specs = [pl.BlockSpec((rows, 512), lambda c, s, k: (0, 0)), held, big]
    if last:
        out_shape.append(jax.ShapeDtypeStruct((prompts, 8, 64, 64), F32))
        out_specs.append(pl.BlockSpec((prompts, 8, 64, 64), lambda c, s, k: (0, 0, 0, 0)))
    ins, specs = [], []
    for p in range(prompts):
        ins += [rkv, rkv, rkv, log_decay, gate]
        specs += [part(0, p), part(1, p), part(2, p), flat(p), flat(p)]
    ins += [vectors, start, states, rkv, rkv, rkv, log_decay, gate]
    specs += [pl.BlockSpec((8, 512), lambda c, s, k: (0, 0)), held, big]
    specs += [slot_part(0), slot_part(1), slot_part(2), slot_flat, slot_flat]
    alias = {}
    if chained:
        ins.append(earlier)
        specs.append(ANY)
        alias = {2 + len(ins): 2}
    return pl.pallas_call(
        functools.partial(
            wkv_kernel,
            t0=t0,
            span=span,
            slot0=c0 * SLOT_BLOCK,
            last=last,
            chained=chained,
            prompts=prompts,
        ),
        out_shape=out_shape,
        grid_spec=pltpu.PrefetchScalarGridSpec(
            num_scalar_prefetch=2,
            grid=(chunks,),
            in_specs=[pl.BlockSpec(table.shape, lambda c, s, k: (0, 0))] + specs,
            out_specs=out_specs,
            scratch_shapes=[
                pltpu.VMEM((4, 64, 128), BF),
                pltpu.VMEM((4, 64, 128), BF),
                pltpu.VMEM((4, 64, 256), BF),
                pltpu.VMEM((SLOT_BLOCK, 512), F32),
            ],
        ),
        input_output_aliases=alias,
        compiler_params=params(1),
        cost_estimate=cost(span * 80_000_000, span << 17),
        name="wkv",
    )(counts, keep, table, *ins)


def on_device(
    learner_acceptance_matrix,
    learner_address_matrix,
    learner_content_matrix,
    learner_gating_matrix,
    learner_result_matrix,
    fading_narrowing_matrix,
    fading_widening_matrix,
    feature_fading_speed,
    current_reward,
    symbol_blending_factors,
    group_scaling_factor,
    group_scaling_offset,
    request_hidden_entries,
    request_valid_count,
    request_destination_place,
    newest_symbol_hidden,
    preceding_hidden_entry,
    place_memory_matrix,
    place_newness_marks,
):
    h = lax.axis_index("yh") * 2 + lax.axis_index("core")
    z, x, yl = lax.axis_index("z"), lax.axis_index("x"), lax.axis_index("yl")
    req = z * 8 + x * 2 + yl
    place = jnp.stack([h, z, x, yl]).astype(jnp.int32)
    prompts, length, width = request_hidden_entries.shape
    slots, groups, breadth = place_memory_matrix.shape[:3]
    tokens = prompts * length
    rows = tokens + slots
    keep = place_newness_marks != 1
    counts = request_valid_count

    spots = request_destination_place - req * slots
    parts, own, new_shift = split(
        place,
        keep.astype(jnp.int32),
        counts,
        spots,
        [
            learner_acceptance_matrix,
            learner_address_matrix,
            learner_content_matrix,
            learner_gating_matrix,
            learner_result_matrix,
        ],
        request_hidden_entries.reshape(tokens, width),
        newest_symbol_hidden,
        preceding_hidden_entry,
    )
    blocks = [parts[0]] + [swap(parts[d], "head", d) for d in (1, 2, 3)]
    side = swap(own, "head", 1)
    far = swap(after(own, blocks[3]), "head", 2)
    stacked = jnp.stack(blocks)
    neighbour = swap(stacked, "yl", 1)
    far_side = swap(far, "head", 1)

    def mixes(piece, d, mixed, low):
        return mix(
            place,
            counts,
            piece,
            d,
            symbol_blending_factors,
            fading_narrowing_matrix.T,
            low,
            mixed,
            fading_widening_matrix,
            feature_fading_speed[None],
            slots,
            length,
        )

    every, first, second = slice(0, 5), slice(0, 3), slice(3, 5)
    mixed, low = mixes(own, 0, None, None)
    neighbour, side, low = lax.optimization_barrier((neighbour, side, low))
    by_row = in_order(stacked, neighbour, yl)
    held = [by_row[p][None, None] for p in range(4)]
    recv = swap_all(held, 0)
    held = pack(place, held, recv, 0, every)
    recv = swap_all(held, 1)
    mixed, low = mixes(side, 1, mixed, low)
    held = pack(place, held, after(recv, low), 1, every)
    recv = swap_all(held, 2)
    mixed, low = mixes(far, 2, mixed, low)
    recv = after(recv, low)
    early = pack(place, held, recv, 2, first)
    early_recv = swap_all(early, 3)
    mixed, log_decay = mixes(far_side, 3, mixed, low)
    late = pack(place, held, after(recv, log_decay), 2, second)
    early_recv = after(early_recv, log_decay)
    late_recv = swap_all(after(late, early_recv), 3)
    early = list(early) + early_recv
    late = list(late) + late_recv

    rkv = project_rkv(place, mixed, early, rows)
    gate = project_gate(place, mixed, late, rows // 2)
    small = jnp.stack([current_reward, group_scaling_factor, group_scaling_offset])
    vectors = jnp.concatenate([small, jnp.zeros((5, width), F32)])
    state = jnp.zeros((prompts, groups // 2, 128, 128), F32)
    sent = []
    t0 = 0
    new_state = None
    kept = keep.astype(jnp.int32)
    for t1 in (256, 384, 512):
        out = wkv(
            counts,
            kept,
            rkv,
            log_decay,
            gate,
            vectors,
            state,
            place_memory_matrix,
            new_state,
            t0,
            t1,
            length,
        )
        normed, state, new_state = out[:3]
        n_side = swap(normed, "head", 1)
        n_far = swap(normed, "head", 2)
        if t1 == length:
            result = project_result(
                place, counts, spots, sent[0], late, (256,), 0, None, length, slots
            )
            n_far = after(n_far, result[1])
        n_far_side = swap(n_far, "head", 1)
        sent.append([normed, n_side, n_far, n_far_side])
        t0 = t1
    prompt_hidden, decode_hidden = project_result(
        place, counts, spots, sent[1] + sent[2], late, (128, 128), 256, result, length, slots
    )
    final_state = out[3]
    for n in range(prompts):
        new_state = lax.dynamic_update_slice(new_state, final_state[n : n + 1], (spots[n], 0, 0, 0))
    return (prompt_hidden, decode_hidden, new_state, new_shift)


def solution(mesh):
    split = Mesh(mesh.devices.reshape(2, 2, 4, 4, 2), ("yh", "core", "z", "x", "yl"))
    head = ("yh", "core")
    req = ("z", "x", "yl")
    row_shard = P(head + req, None)
    in_specs = (
        row_shard,
        row_shard,
        row_shard,
        row_shard,
        row_shard,
        P(),
        P(None, head),
        P(head),
        P(head),
        P(),
        P(head),
        P(head),
        P(req, None, head),
        P(req),
        P(req),
        P(req, head),
        P(req, head),
        P(req, head, None, None),
        P(req),
    )
    out_specs = (
        P(req, None, head),
        P(req, head),
        P(req, head, None, None),
        P(req, head),
    )
    return jax.shard_map(
        on_device, mesh=split, in_specs=in_specs, out_specs=out_specs, check_vma=False
    )
```

time: 213 us -> 190 us (0.89)
  Pallas kernels: 118 us -> 107 us
  other arithmetic: 8.69 us -> 1.62 us
  starting transfers between devices: 50.9 us -> 48.1 us
  between operations: 7.84 us -> 5.33 us
    pallas_call x6, Pallas kernels: 65.3 us -> 52.5 us  [the longest x3 39.3 us: wkv(): pl.pallas_call(functools.partial(wkv_kernel, t0=t0, span=span, slot0=c0 *...]
    pallas_call x4, Pallas kernels: 21.3 us -> 25.8 us  [mix(): pl.pallas_call(functools.partial(mix_kernel, d=d, length=length), out_sha...]
    unnamed x4 -> x0, other arithmetic: 3.65 us -> none
    ppermute x36, starting transfers between devices: 50.9 us -> 48.1 us  [swap(): return lax.ppermute(a, names, [(i, i ^ bits) for i in range(sizes[axes])])]
    pallas_call x4, Pallas kernels: 11.6 us -> 9.3 us  [pack(): pl.pallas_call(functools.partial(pack_kernel, n=n, lot=lot), out_shape=sh...]
    unnamed x55 -> x86, local copies, waits for them, and re-layouts: 7.04 us -> 9.18 us
  transfers between devices with their start and end apart: 36 -> 36, of which waited for: 5 -> 8; matrix products, arithmetic and copies ran while one was open for 4% -> 2% of each run, Pallas kernels for 34% -> 40%
where the time goes in v2:
time: 190 us
  Pallas kernels  107 us (56%)
  starting transfers between devices  48.1 us (25%)
  waiting for transfers between devices  14.3 us (8%)
  local copies, waits for them, and re-layouts  13.2 us (7%)
  between operations  5.33 us (3%)
    ppermute x36, starting transfers between devices, swap(): return lax.ppermute(a, names, [(i, i ^ bits) for i in range(sizes[axes])])  48.1 us
    pallas_call x3, Pallas kernels, wkv(): pl.pallas_call(functools.partial(wkv_kernel, t0=t0, span=span, slot0=c0 *...  39.3 us
    pallas_call x4, Pallas kernels, mix(): pl.pallas_call(functools.partial(mix_kernel, d=d, length=length), out_sha...  25.8 us
    ppermute x36, waiting for transfers between devices, swap(): return lax.ppermute(a, names, [(i, i ^ bits) for i in range(sizes[axes])])  14.3 us
    pallas_call x1, Pallas kernels, project_rkv(): pl.pallas_call(rkv_kernel, out_shape=jax.ShapeDtypeStruct((3, rows, 512),...  13.7 us
    pallas_call x2, Pallas kernels, project_result(): pl.pallas_call(functools.partial(result_kernel, spans=spans, t0=t0, slot0...  10.3 us
    pallas_call x4, Pallas kernels, pack(): pl.pallas_call(functools.partial(pack_kernel, n=n, lot=lot), out_shape=sh...  9.3 us
    unnamed x86, local copies, waits for them, and re-layouts  9.18 us
  transfers between devices with their start and end apart: 36, of which 8 were waited for; matrix products, arithmetic and copies ran while one was open for 2% of the time, Pallas kernels for 40%

profile of v2, /device:TPU:1, one launch (start us, length us, event | category | flops | bytes accessed | tf_op | source)
XLA Modules:
  0.0 189.7 jit_solution(14175722678276129084)
XLA Ops:
  2.7 2.9 %split.1 = (bf16[5,16,512]{2,1,0:T(8,128)(2,1)S(1)}, bf16[5,16,512]{2,1,0:T(8,128)(2,1)S(1)}, bf16[5,16,512]{2,1,0:T(8,128)(2,1)S(1)}, bf16[5,16,512]{2,1,0:T(8,...) custom-call(s32[4]{0:T(128)S(1)} %pad_add_fusion.place_ref, s32[64]{0:T(128)S(1)} %compare_convert_fusion.keep_ref, ...), custom_call_target="tpu_custom_call" | custom-call | tf_op jit(solution)/shard_map/split/pallas_call | solution.py:97
  7.1 3.0 %collective-permute-start = (bf16[5,16,512]{2,1,0:T(8,128)(2,1)S(1)}, bf16[5,16,512]{2,1,0:T(8,128)(2,1)S(1)}, u32[]{:S(2)}, u32[]{:S(2)}) collective-permute-start(bf16[5,16,512]{2,1,0:T(8,128)(2,1)S(1)} %get-tuple-element.73), channel_id=1, source_target_pairs={{0,96},{32,64},{64,32},{96,0},{1,97},{33,65},{65,33},{97,1},{2,98}... | collective-permute-start | bytes 245768 | tf_op jit(solution)/shard_map/ppermute | solution.py:25
  10.7 2.0 %collective-permute-done = bf16[5,16,512]{2,1,0:T(8,128)(2,1)S(1)} collective-permute-done((bf16[5,16,512]{2,1,0:T(8,128)(2,1)S(1)}, bf16[5,16,512]{2,1,0:T(8,128)(2,1)S(1)}, u32[]{:S(2)}, u32[]{:S(2)}) %collective-permute-start) | collective-permute-done | bytes 81952 | tf_op jit(solution)/shard_map/ppermute | solution.py:25
  12.8 2.1 %collective-permute-done.4 = bf16[5,16,512]{2,1,0:T(8,128)(2,1)S(1)} collective-permute-done((bf16[5,16,512]{2,1,0:T(8,128)(2,1)S(1)}, bf16[5,16,512]{2,1,0:T(8,128)(2,1)S(1)}, u32[]{:S(2)}, u32[]{:S(2)}) %collective-permute-start.4) | collective-permute-done | bytes 81952 | tf_op jit(solution)/shard_map/ppermute | solution.py:25
  15.4 3.0 %collective-permute-start.1 = (bf16[1152,512]{1,0:T(8,128)(2,1)S(1)}, bf16[1152,512]{1,0:T(8,128)(2,1)S(1)}, u32[]{:S(2)}, u32[]{:S(2)}) collective-permute-start(bf16[1152,512]{1,0:T(8,128)(2,1)S(1)} %get-tuple-element.74.refs_0_), channel_id=1, source_target_pairs={{0,64},{32,96},{64,0},{96,32},{1,65},{33,97},{65,1},{97,33},{2,66}... | collective-permute-start | bytes 3538952 | tf_op jit(solution)/shard_map/ppermute | solution.py:25
  19.0 6.2 %mix.4 = (bf16[5,1088,2048]{2,1,0:T(8,128)(2,1)}, f32[1088,64]{1,0:T(8,128)S(1)}) custom-call(s32[4]{0:T(128)S(1)} %pad_add_fusion.place_ref, s32[2]{0:T(128)S(1)} %copy-done.19, bf16[1152,512]{1,0:T(8,128)(2,1)} %copy-done.8, f32[5,2048]{1,0:T(8,128)} %refs_1_.9, bf16[64,2048]{1,0:T(8,128)(2,1)} %bitcast.26), custom_call_target="tpu_custom_call" | custom-call | flops 11141120 | bytes 6684672 | tf_op jit(solution)/shard_map/mix/pallas_call | solution.py:272
  27.5 1.6 collective-permute-start.8
  29.1 1.8 collective-permute-start.9
  30.9 2.2 %collective-permute-start.10 = (bf16[1,1,5,32,512]{4,3,2,1,0:T(8,128)(2,1)S(1)}, bf16[1,1,5,32,512]{4,3,2,1,0:T(8,128)(2,1)S(1)}, u32[]{:S(2)}, u32[]{:S(2)}) collective-permute-start(bf16[1,1,5,32,512]{4,3,2,1,0:T(8,128)(2,1)S(1)} %get-tuple-element.140.refs_3_), channel_id=1, source_target_pairs={{0,24},{8,16},{16,8},{24,0},{1,25},{9,17},{17,9},{25,1},{2,26},{10... | collective-permute-start | bytes 491528 | tf_op jit(solution)/shard_map/ppermute | solution.py:25
  34.8 1.8 collective-permute-done.10.refs_7_
  37.3 2.1 %pack.4 = (bf16[1,2,5,32,512]{4,3,2,1,0:T(8,128)(2,1)S(1)}, bf16[2,1,5,32,512]{4,3,2,1,0:T(8,128)(2,1)S(1)}, bf16[1,2,5,32,512]{4,3,2,1,0:T(8,128)(2,1)S(1)}, bf16[2,1,5,32,512]{4,3,2,1,0:T(8,128)(2,1)S(1)}) custom-call(s32[4]{0:T(128)S(1)} %pad_add_fusion.place_ref, bf16[1,1,5,32,512]{4,3,2,1,0:T(8,128)(2,1)} %copy-done.29, ...), custom_call_target="tpu_custom_call" | custom-call | bytes 8388608 | tf_op jit(solution)/shard_map/pack/pallas_call | solution.py:171
  40.7 3.0 %collective-permute-start.13 = (bf16[1,2,5,32,512]{4,3,2,1,0:T(8,128)(2,1)S(1)}, bf16[1,2,5,32,512]{4,3,2,1,0:T(8,128)(2,1)S(1)}, u32[]{:S(2)}, u32[]{:S(2)}) collective-permute-start(bf16[1,2,5,32,512]{4,3,2,1,0:T(8,128)(2,1)S(1)} %get-tuple-element.90.refs_2_), channel_id=1, source_target_pairs={{0,24},{8,16},{16,8},{24,0},{1,25},{9,17},{17,9},{25,1},{2,26},{10... | collective-permute-start | bytes 983048 | tf_op jit(solution)/shard_map/ppermute | solution.py:25
  43.7 6.3 %mix.5 = (bf16[5,1088,2048]{2,1,0:T(8,128)(2,1)}, f32[1088,64]{1,0:T(8,128)S(1)}) custom-call(s32[4]{0:T(128)S(1)} %pad_add_fusion.place_ref, s32[2]{0:T(128)S(1)} %copy-done.19, bf16[1152,512]{1,0:T(8,128)(2,1)} %collective-permute-done.6.refs_0_, f32[5,2048]{1,0:T(8,128)} %refs_1_.9, bf16[64,2048]{1,0:T(8,128)(2,1)} %bitcast.27, ...), custom_call_target="tpu_custom_call", output_to_operand_aliasing={{0}: (6, {})} | custom-call | flops 11141120 | bytes 6684672 | tf_op jit(solution)/shard_map/mix/pallas_call | solution.py:272
  51.1 2.3 %pack.5 = (bf16[2,2,5,32,512]{4,3,2,1,0:T(8,128)(2,1)S(1)}, bf16[2,2,5,32,512]{4,3,2,1,0:T(8,128)(2,1)S(1)}, bf16[2,2,5,32,512]{4,3,2,1,0:T(8,128)(2,1)S(1)}, bf16[2,2,5,32,512]{4,3,2,1,0:T(8,128)(2,1)S(1)}) custom-call(s32[4]{0:T(128)S(1)} %pad_add_fusion.place_ref, bf16[1,2,5,32,512]{4,3,2,1,0:T(8,128)(2,1)} %copy-done.14, ...), custom_call_target="tpu_custom_call" | custom-call | bytes 8388608 | tf_op jit(solution)/shard_map/pack/pallas_call | solution.py:171
  56.0 5.3 %collective-permute-start.2 = (bf16[1152,512]{1,0:T(8,128)(2,1)S(1)}, bf16[1152,512]{1,0:T(8,128)(2,1)S(1)}, u32[]{:S(2)}, u32[]{:S(2)}) collective-permute-start(bf16[1152,512]{1,0:T(8,128)(2,1)S(1)} %collective-permute-done.1.refs_0_), channel_id=1, source_target_pairs={{0,32},{32,0},{64,96},{96,64},{1,33},{33,1},{65,97},{97,65},{2,34}... | collective-permute-start | bytes 3538952 | tf_op jit(solution)/shard_map/ppermute | solution.py:25
  61.4 6.3 %mix.6 = (bf16[5,1088,2048]{2,1,0:T(8,128)(2,1)}, f32[1088,64]{1,0:T(8,128)S(1)}) custom-call(s32[4]{0:T(128)S(1)} %pad_add_fusion.place_ref, s32[2]{0:T(128)S(1)} %copy-done.19, bf16[1152,512]{1,0:T(8,128)(2,1)} %copy-done.25, f32[5,2048]{1,0:T(8,128)} %refs_1_.9, bf16[64,2048]{1,0:T(8,128)(2,1)} %bitcast.28, ...), custom_call_target="tpu_custom_call", output_to_operand_aliasing={{0}: (6, {})} | custom-call | flops 11141120 | bytes 6684672 | tf_op jit(solution)/shard_map/mix/pallas_call | solution.py:272
  69.3 2.6 %pack.6 = (bf16[2,4,3,32,512]{4,3,2,1,0:T(8,128)(2,1)S(1)}, bf16[4,2,3,32,512]{4,3,2,1,0:T(8,128)(2,1)S(1)}, bf16[2,4,3,32,512]{4,3,2,1,0:T(8,128)(2,1)S(1)}, bf16[4,2,3,32,512]{4,3,2,1,0:T(8,128)(2,1)S(1)}) custom-call(s32[4]{0:T(128)S(1)} %pad_add_fusion.place_ref, bf16[2,2,5,32,512]{4,3,2,1,0:T(8,128)(2,1)} %copy-done.4, ...), custom_call_target="tpu_custom_call" | custom-call | bytes 8388608 | tf_op jit(solution)/shard_map/pack/pallas_call | solution.py:171
  71.9 2.3 %collective-permute-start.19 = (bf16[2,4,3,32,512]{4,3,2,1,0:T(8,128)(2,1)S(1)}, bf16[2,4,3,32,512]{4,3,2,1,0:T(8,128)(2,1)S(1)}, u32[]{:S(2)}, u32[]{:S(2)}) collective-permute-start(bf16[2,4,3,32,512]{4,3,2,1,0:T(8,128)(2,1)S(1)} %get-tuple-element.104.refs_0_), channel_id=1, source_target_pairs={{0,24},{8,16},{16,8},{24,0},{1,25},{9,17},{17,9},{25,1},{2,26},{10... | collective-permute-start | bytes 2359304 | tf_op jit(solution)/shard_map/ppermute | solution.py:25
  78.4 7.0 %mix.7 = (bf16[5,1088,2048]{2,1,0:T(8,128)(2,1)}, f32[1088,512]{1,0:T(8,128)S(1)}) custom-call(s32[4]{0:T(128)S(1)} %pad_add_fusion.place_ref, s32[2]{0:T(128)S(1)} %copy-done.19, bf16[1152,512]{1,0:T(8,128)(2,1)} %copy-done.26, f32[5,2048]{1,0:T(8,128)} %refs_1_.9, bf16[64,2048]{1,0:T(8,128)(2,1)} %bitcast.29, ...), custom_call_target="tpu_custom_call", output_to_operand_aliasing={{0}: (6, {})} | custom-call | flops 11141120 | bytes 6684672 | tf_op jit(solution)/shard_map/mix/pallas_call | solution.py:272
  85.4 2.3 %pack.7 = (bf16[2,4,2,32,512]{4,3,2,1,0:T(8,128)(2,1)S(1)}, bf16[4,2,2,32,512]{4,3,2,1,0:T(8,128)(2,1)S(1)}, bf16[2,4,2,32,512]{4,3,2,1,0:T(8,128)(2,1)S(1)}, bf16[4,2,2,32,512]{4,3,2,1,0:T(8,128)(2,1)S(1)}) custom-call(s32[4]{0:T(128)S(1)} %pad_add_fusion.place_ref, bf16[2,2,5,32,512]{4,3,2,1,0:T(8,128)(2,1)} %copy-done.4, ...), custom_call_target="tpu_custom_call" | custom-call | bytes 8388608 | tf_op jit(solution)/shard_map/pack/pallas_call | solution.py:171
  89.1 2.7 %collective-permute-done.22.refs_7_ = bf16[4,2,3,32,512]{4,3,2,1,0:T(8,128)(2,1)S(1)} collective-permute-done((bf16[4,2,3,32,512]{4,3,2,1,0:T(8,128)(2,1)S(1)}, bf16[4,2,3,32,512]{4,3,2,1,0:T(8,128)(2,1)S(1)}, u32[]{:S(2)}, u32[]{:S(2)}) %collective-permute-start.22) | collective-permute-done | bytes 786464 | tf_op jit(solution)/shard_map/ppermute | solution.py:25
  94.1 13.7 %project_rkv.1.refs_0_.refs_1_.refs_2_.refs_5_.refs_6_.refs_7_.refs_13_.refs_14_.refs_15_ = bf16[3,1088,512]{2,1,0:T(8,128)(2,1)} custom-call(s32[4]{0:T(128)S(1)} %pad_add_fusion.place_ref, bf16[5,1088,2048]{2,1,0:T(8,128)(2,1)} %get-tuple-element.86.x_ref, bf16[2,4,3,32,512]{4,3,2,1,0:T(8,128)(2,1)S(1)} %get-tuple-element.104.refs_0_, ...), custom_call_target="tpu_custom_call" | custom-call | flops 6845104128 | bytes 25165824 | tf_op jit(solution)/shard_map/project_rkv/pallas_call | solution.py:319
  107.9 5.9 %project_gate.1.refs_4_.refs_9_.refs_17_ = bf16[1088,512]{1,0:T(8,128)(2,1)S(1)} custom-call(s32[4]{0:T(128)S(1)} %pad_add_fusion.place_ref, bf16[5,1088,2048]{2,1,0:T(8,128)(2,1)} %get-tuple-element.86.x_ref, bf16[2,4,2,32,512]{4,3,2,1,0:T(8,128)(2,1)S(1)} %get-tuple-element.121.refs_0_.refs_4_.refs_8_, ...), custom_call_target="tpu_custom_call" | custom-call | flops 2281701376 | bytes 8388608 | tf_op jit(solution)/shard_map/project_gate/pallas_call | solution.py:353
  113.8 17.5 %wkv.3 = (bf16[544,512]{1,0:T(8,128)(2,1)}, f32[2,4,128,128]{3,2,1,0:T(8,128)S(1)}, f32[64,8,64,64]{3,2,1,0:T(8,128)}) custom-call(s32[2]{0:T(128)S(1)} %copy-done.20, s32[64]{0:T(128)S(1)} %compare_convert_fusion.keep_ref, bf16[456,128]{1,0:T(8,128)(2,1)S(1)} %copy-done.13, ...), custom_call_target="tpu_custom_call" | custom-call | flops 20480000000 | bytes 33554432 | tf_op jit(solution)/shard_map/wkv/pallas_call | solution.py:686
  131.4 6.0 %collective-permute-start.32 = (bf16[544,512]{1,0:T(8,128)(2,1)}, bf16[544,512]{1,0:T(8,128)(2,1)}, u32[]{:S(2)}, u32[]{:S(2)}) collective-permute-start(bf16[544,512]{1,0:T(8,128)(2,1)} %get-tuple-element.131.refs_0_), channel_id=1, source_target_pairs={{0,32},{32,0},{64,96},{96,64},{1,33},{33,1},{65,97},{97,65},{2,34}... | collective-permute-start | bytes 1671176 | tf_op jit(solution)/shard_map/ppermute | solution.py:25
  138.8 10.3 %wkv.4 = (bf16[272,512]{1,0:T(8,128)(2,1)S(1)}, f32[2,4,128,128]{3,2,1,0:T(8,128)S(1)}, f32[64,8,64,64]{3,2,1,0:T(8,128)}) custom-call(s32[2]{0:T(128)S(1)} %copy-done.20, s32[64]{0:T(128)S(1)} %compare_convert_fusion.keep_ref, bf16[456,128]{1,0:T(8,128)(2,1)S(1)} %copy-done.13, ...), custom_call_target="tpu_custom_call", output_to_operand_aliasing={{2}: (21, {})} | custom-call | flops 10240000000 | bytes 16777216 | tf_op jit(solution)/shard_map/wkv/pallas_call | solution.py:686
  150.7 2.7 %collective-permute-done.33.refs_2_ = bf16[544,512]{1,0:T(8,128)(2,1)} collective-permute-done((bf16[544,512]{1,0:T(8,128)(2,1)}, bf16[544,512]{1,0:T(8,128)(2,1)}, u32[]{:S(2)}, u32[]{:S(2)}) %collective-permute-start.33) | collective-permute-done | bytes 557088 | tf_op jit(solution)/shard_map/ppermute | solution.py:25
  154.6 11.5 %wkv.5 = (bf16[272,512]{1,0:T(8,128)(2,1)}, f32[2,4,128,128]{3,2,1,0:T(8,128)}, f32[64,8,64,64]{3,2,1,0:T(8,128)}, f32[2,8,64,64]{3,2,1,0:T(8,128)S(1)}) custom-call(s32[2]{0:T(128)S(1)} %copy-done.20, s32[64]{0:T(128)S(1)} %compare_convert_fusion.keep_ref, bf16[456,128]{1,0:T(8,128)(2,1)S(1)} %copy-done.13, ...), custom_call_target="tpu_custom_call", output_to_operand_aliasing={{2}: (21, {})} | custom-call | flops 10240000000 | bytes 16777216 | tf_op jit(solution)/shard_map/wkv/pallas_call | solution.py:686
  175.6 4.9 %project_result.2 = (bf16[2,512,512]{2,1,0:T(8,128)(2,1)}, bf16[64,512]{1,0:T(8,128)(2,1)}) custom-call(s32[4]{0:T(128)S(1)} %pad_add_fusion.place_ref, s32[2]{0:T(128)S(1)} %copy-done.20, s32[2]{0:T(128)S(1)} %broadcast_subtract_fusion.spot_ref, bf16[544,512]{1,0:T(8,128)(2,1)} %get-tuple-element.131.refs_0_, ...), custom_call_target="tpu_custom_call" | custom-call | flops 1073741824 | bytes 8388608 | tf_op jit(solution)/shard_map/project_result/pallas_call | solution.py:402
  180.8 1.7 slice_dynamic-update-slice_fusion.1
  182.5 1.7 slice_dynamic-update-slice_fusion
  184.2 5.4 %project_result.3 = (bf16[2,512,512]{2,1,0:T(8,128)(2,1)}, bf16[64,512]{1,0:T(8,128)(2,1)}) custom-call(s32[4]{0:T(128)S(1)} %pad_add_fusion.place_ref, s32[2]{0:T(128)S(1)} %copy-done.20, s32[2]{0:T(128)S(1)} %broadcast_subtract_fusion.spot_ref, bf16[272,512]{1,0:T(8,128)(2,1)S(1)} %get-tuple-element.127.refs_0_, ...), custom_call_target="tpu_custom_call", output_to_operand_aliasing={{0}: (19, {}), {1}: (20, {})} | custom-call | flops 1073741824 | bytes 8388608 | tf_op jit(solution)/shard_map/project_result/pallas_call | solution.py:402
  (155 shorter events, 34.2 us)
Async XLA Ops:
  5.6 20.4 %collective-permute-start.6 = (bf16[1152,512]{1,0:T(8,128)(2,1)S(1)}, bf16[1152,512]{1,0:T(8,128)(2,1)}, u32[]{:S(2)}, u32[]{:S(2)}) collective-permute-start(bf16[1152,512]{1,0:T(8,128)(2,1)S(1)} %get-tuple-element.74.refs_0_), channel_id=1, source_target_pairs={{0,32},{32,0},{64,96},{96,64},{1,33},{33,1},{65,97},{97,65},{2,34}... | collective-permute-start | bytes 3538952 | tf_op jit(solution)/shard_map/ppermute | solution.py:25
  7.1 5.7 %collective-permute-start = (bf16[5,16,512]{2,1,0:T(8,128)(2,1)S(1)}, bf16[5,16,512]{2,1,0:T(8,128)(2,1)S(1)}, u32[]{:S(2)}, u32[]{:S(2)}) collective-permute-start(bf16[5,16,512]{2,1,0:T(8,128)(2,1)S(1)} %get-tuple-element.73), channel_id=1, source_target_pairs={{0,96},{32,64},{64,32},{96,0},{1,97},{33,65},{65,33},{97,1},{2,98}... | collective-permute-start | bytes 245768 | tf_op jit(solution)/shard_map/ppermute | solution.py:25
  14.9 11.1 %collective-permute-start.5 = (bf16[4,5,16,512]{3,2,1,0:T(8,128)(2,1)S(1)}, bf16[4,5,16,512]{3,2,1,0:T(8,128)(2,1)S(1)}, u32[]{:S(2)}, u32[]{:S(2)}) collective-permute-start(bf16[4,5,16,512]{3,2,1,0:T(8,128)(2,1)S(1)} %pad_maximum_fusion), channel_id=1, source_target_pairs={{0,1},{1,0},{2,3},{3,2},{4,5},{5,4},{6,7},{7,6},{8,9},{9,8},{10,11... | collective-permute-start | bytes 983048 | tf_op jit(solution)/shard_map/ppermute | solution.py:25
  15.4 40.7 %collective-permute-start.1 = (bf16[1152,512]{1,0:T(8,128)(2,1)S(1)}, bf16[1152,512]{1,0:T(8,128)(2,1)S(1)}, u32[]{:S(2)}, u32[]{:S(2)}) collective-permute-start(bf16[1152,512]{1,0:T(8,128)(2,1)S(1)} %get-tuple-element.74.refs_0_), channel_id=1, source_target_pairs={{0,64},{32,96},{64,0},{96,32},{1,65},{33,97},{65,1},{97,33},{2,66}... | collective-permute-start | bytes 3538952 | tf_op jit(solution)/shard_map/ppermute | solution.py:25
  26.2 7.0 %collective-permute-start.7 = (bf16[1,1,5,32,512]{4,3,2,1,0:T(8,128)(2,1)S(1)}, bf16[1,1,5,32,512]{4,3,2,1,0:T(8,128)(2,1)S(1)}, u32[]{:S(2)}, u32[]{:S(2)}) collective-permute-start(bf16[1,1,5,32,512]{4,3,2,1,0:T(8,128)(2,1)S(1)} %get-tuple-element.141.refs_0_), channel_id=1, source_target_pairs={{0,2},{2,0},{4,6},{6,4},{1,3},{3,1},{5,7},{7,5},{8,10},{10,8},{12,... | collective-permute-start | bytes 491528 | tf_op jit(solution)/shard_map/ppermute | solution.py:25
  27.5 5.7 %collective-permute-start.8 = (bf16[1,1,5,32,512]{4,3,2,1,0:T(8,128)(2,1)S(1)}, bf16[1,1,5,32,512]{4,3,2,1,0:T(8,128)(2,1)S(1)}, u32[]{:S(2)}, u32[]{:S(2)}) collective-permute-start(bf16[1,1,5,32,512]{4,3,2,1,0:T(8,128)(2,1)S(1)} %get-tuple-element.142.refs_1_), channel_id=1, source_target_pairs={{0,8},{8,0},{16,24},{24,16},{1,9},{9,1},{17,25},{25,17},{2,10},{10... | collective-permute-start | bytes 491528 | tf_op jit(solution)/shard_map/ppermute | solution.py:25
  29.1 5.7 %collective-permute-start.9 = (bf16[1,1,5,32,512]{4,3,2,1,0:T(8,128)(2,1)S(1)}, bf16[1,1,5,32,512]{4,3,2,1,0:T(8,128)(2,1)S(1)}, u32[]{:S(2)}, u32[]{:S(2)}) collective-permute-start(bf16[1,1,5,32,512]{4,3,2,1,0:T(8,128)(2,1)S(1)} %get-tuple-element.143.refs_2_), channel_id=1, source_target_pairs={{0,6},{2,4},{4,2},{6,0},{1,7},{3,5},{5,3},{7,1},{8,14},{10,12},{12... | collective-permute-start | bytes 491528 | tf_op jit(solution)/shard_map/ppermute | solution.py:25
  39.4 10.6 %collective-permute-start.11 = (bf16[1,2,5,32,512]{4,3,2,1,0:T(8,128)(2,1)S(1)}, bf16[1,2,5,32,512]{4,3,2,1,0:T(8,128)(2,1)S(1)}, u32[]{:S(2)}, u32[]{:S(2)}) collective-permute-start(bf16[1,2,5,32,512]{4,3,2,1,0:T(8,128)(2,1)S(1)} %get-tuple-element.88.refs_0_), channel_id=1, source_target_pairs={{0,8},{8,0},{16,24},{24,16},{1,9},{9,1},{17,25},{25,17},{2,10},{10... | collective-permute-start | bytes 983048 | tf_op jit(solution)/shard_map/ppermute | solution.py:25
  39.8 10.3 %collective-permute-start.12 = (bf16[2,1,5,32,512]{4,3,2,1,0:T(8,128)(2,1)S(1)}, bf16[2,1,5,32,512]{4,3,2,1,0:T(8,128)(2,1)S(1)}, u32[]{:S(2)}, u32[]{:S(2)}) collective-permute-start(bf16[2,1,5,32,512]{4,3,2,1,0:T(8,128)(2,1)S(1)} %get-tuple-element.89.refs_1_), channel_id=1, source_target_pairs={{0,6},{2,4},{4,2},{6,0},{1,7},{3,5},{5,3},{7,1},{8,14},{10,12},{12... | collective-permute-start | bytes 983048 | tf_op jit(solution)/shard_map/ppermute | solution.py:25
  40.7 9.4 %collective-permute-start.13 = (bf16[1,2,5,32,512]{4,3,2,1,0:T(8,128)(2,1)S(1)}, bf16[1,2,5,32,512]{4,3,2,1,0:T(8,128)(2,1)S(1)}, u32[]{:S(2)}, u32[]{:S(2)}) collective-permute-start(bf16[1,2,5,32,512]{4,3,2,1,0:T(8,128)(2,1)S(1)} %get-tuple-element.90.refs_2_), channel_id=1, source_target_pairs={{0,24},{8,16},{16,8},{24,0},{1,25},{9,17},{17,9},{25,1},{2,26},{10... | collective-permute-start | bytes 983048 | tf_op jit(solution)/shard_map/ppermute | solution.py:25
  43.7 6.4 %collective-permute-start.14 = (bf16[2,1,5,32,512]{4,3,2,1,0:T(8,128)(2,1)S(1)}, bf16[2,1,5,32,512]{4,3,2,1,0:T(8,128)(2,1)S(1)}, u32[]{:S(2)}, u32[]{:S(2)}) collective-permute-start(bf16[2,1,5,32,512]{4,3,2,1,0:T(8,128)(2,1)S(1)} %get-tuple-element.91.refs_3_), channel_id=1, source_target_pairs={{0,2},{2,0},{4,6},{6,4},{1,3},{3,1},{5,7},{7,5},{8,10},{10,8},{12,... | collective-permute-start | bytes 983048 | tf_op jit(solution)/shard_map/ppermute | solution.py:25
  53.5 14.2 %collective-permute-start.15 = (bf16[2,2,5,32,512]{4,3,2,1,0:T(8,128)(2,1)S(1)}, bf16[2,2,5,32,512]{4,3,2,1,0:T(8,128)(2,1)S(1)}, u32[]{:S(2)}, u32[]{:S(2)}) collective-permute-start(bf16[2,2,5,32,512]{4,3,2,1,0:T(8,128)(2,1)S(1)} %get-tuple-element.96.refs_0_), channel_id=1, source_target_pairs={{0,6},{2,4},{4,2},{6,0},{1,7},{3,5},{5,3},{7,1},{8,14},{10,12},{12... | collective-permute-start | bytes 1966088 | tf_op jit(solution)/shard_map/ppermute | solution.py:25
  54.4 13.3 %collective-permute-start.16 = (bf16[2,2,5,32,512]{4,3,2,1,0:T(8,128)(2,1)S(1)}, bf16[2,2,5,32,512]{4,3,2,1,0:T(8,128)(2,1)S(1)}, u32[]{:S(2)}, u32[]{:S(2)}) collective-permute-start(bf16[2,2,5,32,512]{4,3,2,1,0:T(8,128)(2,1)S(1)} %get-tuple-element.97.refs_1_), channel_id=1, source_target_pairs={{0,24},{8,16},{16,8},{24,0},{1,25},{9,17},{17,9},{25,1},{2,26},{10... | collective-permute-start | bytes 1966088 | tf_op jit(solution)/shard_map/ppermute | solution.py:25
  55.3 12.4 %collective-permute-start.17 = (bf16[2,2,5,32,512]{4,3,2,1,0:T(8,128)(2,1)S(1)}, bf16[2,2,5,32,512]{4,3,2,1,0:T(8,128)(2,1)S(1)}, u32[]{:S(2)}, u32[]{:S(2)}) collective-permute-start(bf16[2,2,5,32,512]{4,3,2,1,0:T(8,128)(2,1)S(1)} %get-tuple-element.98.refs_2_), channel_id=1, source_target_pairs={{0,2},{2,0},{4,6},{6,4},{1,3},{3,1},{5,7},{7,5},{8,10},{10,8},{12,... | collective-permute-start | bytes 1966088 | tf_op jit(solution)/shard_map/ppermute | solution.py:25
  55.9 11.9 %collective-permute-start.18 = (bf16[2,2,5,32,512]{4,3,2,1,0:T(8,128)(2,1)S(1)}, bf16[2,2,5,32,512]{4,3,2,1,0:T(8,128)(2,1)S(1)}, u32[]{:S(2)}, u32[]{:S(2)}) collective-permute-start(bf16[2,2,5,32,512]{4,3,2,1,0:T(8,128)(2,1)S(1)} %get-tuple-element.99.refs_3_), channel_id=1, source_target_pairs={{0,8},{8,0},{16,24},{24,16},{1,9},{9,1},{17,25},{25,17},{2,10},{10... | collective-permute-start | bytes 1966088 | tf_op jit(solution)/shard_map/ppermute | solution.py:25
  56.0 21.4 %collective-permute-start.2 = (bf16[1152,512]{1,0:T(8,128)(2,1)S(1)}, bf16[1152,512]{1,0:T(8,128)(2,1)S(1)}, u32[]{:S(2)}, u32[]{:S(2)}) collective-permute-start(bf16[1152,512]{1,0:T(8,128)(2,1)S(1)} %collective-permute-done.1.refs_0_), channel_id=1, source_target_pairs={{0,32},{32,0},{64,96},{96,64},{1,33},{33,1},{65,97},{97,65},{2,34}... | collective-permute-start | bytes 3538952 | tf_op jit(solution)/shard_map/ppermute | solution.py:25
  71.9 15.8 %collective-permute-start.19 = (bf16[2,4,3,32,512]{4,3,2,1,0:T(8,128)(2,1)S(1)}, bf16[2,4,3,32,512]{4,3,2,1,0:T(8,128)(2,1)S(1)}, u32[]{:S(2)}, u32[]{:S(2)}) collective-permute-start(bf16[2,4,3,32,512]{4,3,2,1,0:T(8,128)(2,1)S(1)} %get-tuple-element.104.refs_0_), channel_id=1, source_target_pairs={{0,24},{8,16},{16,8},{24,0},{1,25},{9,17},{17,9},{25,1},{2,26},{10... | collective-permute-start | bytes 2359304 | tf_op jit(solution)/shard_map/ppermute | solution.py:25
  74.2 14.3 %collective-permute-start.20 = (bf16[4,2,3,32,512]{4,3,2,1,0:T(8,128)(2,1)S(1)}, bf16[4,2,3,32,512]{4,3,2,1,0:T(8,128)(2,1)S(1)}, u32[]{:S(2)}, u32[]{:S(2)}) collective-permute-start(bf16[4,2,3,32,512]{4,3,2,1,0:T(8,128)(2,1)S(1)} %get-tuple-element.105.refs_1_), channel_id=1, source_target_pairs={{0,2},{2,0},{4,6},{6,4},{1,3},{3,1},{5,7},{7,5},{8,10},{10,8},{12,... | collective-permute-start | bytes 2359304 | tf_op jit(solution)/shard_map/ppermute | solution.py:25
  74.9 14.1 %collective-permute-start.21 = (bf16[2,4,3,32,512]{4,3,2,1,0:T(8,128)(2,1)S(1)}, bf16[2,4,3,32,512]{4,3,2,1,0:T(8,128)(2,1)S(1)}, u32[]{:S(2)}, u32[]{:S(2)}) collective-permute-start(bf16[2,4,3,32,512]{4,3,2,1,0:T(8,128)(2,1)S(1)} %get-tuple-element.106.refs_2_), channel_id=1, source_target_pairs={{0,8},{8,0},{16,24},{24,16},{1,9},{9,1},{17,25},{25,17},{2,10},{10... | collective-permute-start | bytes 2359304 | tf_op jit(solution)/shard_map/ppermute | solution.py:25
  75.7 16.1 %collective-permute-start.22 = (bf16[4,2,3,32,512]{4,3,2,1,0:T(8,128)(2,1)S(1)}, bf16[4,2,3,32,512]{4,3,2,1,0:T(8,128)(2,1)S(1)}, u32[]{:S(2)}, u32[]{:S(2)}) collective-permute-start(bf16[4,2,3,32,512]{4,3,2,1,0:T(8,128)(2,1)S(1)} %get-tuple-element.107.refs_3_), channel_id=1, source_target_pairs={{0,6},{2,4},{4,2},{6,0},{1,7},{3,5},{5,3},{7,1},{8,14},{10,12},{12... | collective-permute-start | bytes 2359304 | tf_op jit(solution)/shard_map/ppermute | solution.py:25
  91.8 16.1 %collective-permute-start.23 = (bf16[2,4,2,32,512]{4,3,2,1,0:T(8,128)(2,1)S(1)}, bf16[2,4,2,32,512]{4,3,2,1,0:T(8,128)(2,1)S(1)}, u32[]{:S(2)}, u32[]{:S(2)}) collective-permute-start(bf16[2,4,2,32,512]{4,3,2,1,0:T(8,128)(2,1)S(1)} %get-tuple-element.121.refs_0_.refs_4_.refs_8_), channel_id=1, source_target_pairs={{0,24},{8,16},{16,8},{24,0},{1,25},{9,17},{17,9},{25,1},{2,26},{10... | collective-permute-start | bytes 1572872 | tf_op jit(solution)/shard_map/ppermute | solution.py:25
  92.8 15.0 %collective-permute-start.24 = (bf16[4,2,2,32,512]{4,3,2,1,0:T(8,128)(2,1)S(1)}, bf16[4,2,2,32,512]{4,3,2,1,0:T(8,128)(2,1)S(1)}, u32[]{:S(2)}, u32[]{:S(2)}) collective-permute-start(bf16[4,2,2,32,512]{4,3,2,1,0:T(8,128)(2,1)S(1)} %get-tuple-element.122.refs_1_.refs_5_.refs_9_), channel_id=1, source_target_pairs={{0,2},{2,0},{4,6},{6,4},{1,3},{3,1},{5,7},{7,5},{8,10},{10,8},{12,... | collective-permute-start | bytes 1572872 | tf_op jit(solution)/shard_map/ppermute | solution.py:25
  92.8 15.0 %collective-permute-start.25 = (bf16[2,4,2,32,512]{4,3,2,1,0:T(8,128)(2,1)S(1)}, bf16[2,4,2,32,512]{4,3,2,1,0:T(8,128)(2,1)S(1)}, u32[]{:S(2)}, u32[]{:S(2)}) collective-permute-start(bf16[2,4,2,32,512]{4,3,2,1,0:T(8,128)(2,1)S(1)} %get-tuple-element.123.refs_2_.refs_6_.refs_10_), channel_id=1, source_target_pairs={{0,8},{8,0},{16,24},{24,16},{1,9},{9,1},{17,25},{25,17},{2,10},{10... | collective-permute-start | bytes 1572872 | tf_op jit(solution)/shard_map/ppermute | solution.py:25
  92.8 15.1 %collective-permute-start.26 = (bf16[4,2,2,32,512]{4,3,2,1,0:T(8,128)(2,1)S(1)}, bf16[4,2,2,32,512]{4,3,2,1,0:T(8,128)(2,1)S(1)}, u32[]{:S(2)}, u32[]{:S(2)}) collective-permute-start(bf16[4,2,2,32,512]{4,3,2,1,0:T(8,128)(2,1)S(1)} %get-tuple-element.124.refs_3_.refs_7_.refs_11_), channel_id=1, source_target_pairs={{0,6},{2,4},{4,2},{6,0},{1,7},{3,5},{5,3},{7,1},{8,14},{10,12},{12... | collective-permute-start | bytes 1572872 | tf_op jit(solution)/shard_map/ppermute | solution.py:25
  131.4 41.8 %collective-permute-start.32 = (bf16[544,512]{1,0:T(8,128)(2,1)}, bf16[544,512]{1,0:T(8,128)(2,1)}, u32[]{:S(2)}, u32[]{:S(2)}) collective-permute-start(bf16[544,512]{1,0:T(8,128)(2,1)} %get-tuple-element.131.refs_0_), channel_id=1, source_target_pairs={{0,32},{32,0},{64,96},{96,64},{1,33},{33,1},{65,97},{97,65},{2,34}... | collective-permute-start | bytes 1671176 | tf_op jit(solution)/shard_map/ppermute | solution.py:25
  137.4 16.0 %collective-permute-start.33 = (bf16[544,512]{1,0:T(8,128)(2,1)}, bf16[544,512]{1,0:T(8,128)(2,1)}, u32[]{:S(2)}, u32[]{:S(2)}) collective-permute-start(bf16[544,512]{1,0:T(8,128)(2,1)} %get-tuple-element.131.refs_0_), channel_id=1, source_target_pairs={{0,64},{32,96},{64,0},{96,32},{1,65},{33,97},{65,1},{97,33},{2,66}... | collective-permute-start | bytes 1671176 | tf_op jit(solution)/shard_map/ppermute | solution.py:25
  149.1 23.8 %collective-permute-start.28 = (bf16[272,512]{1,0:T(8,128)(2,1)S(1)}, bf16[272,512]{1,0:T(8,128)(2,1)}, u32[]{:S(2)}, u32[]{:S(2)}) collective-permute-start(bf16[272,512]{1,0:T(8,128)(2,1)S(1)} %get-tuple-element.127.refs_0_), channel_id=1, source_target_pairs={{0,64},{32,96},{64,0},{96,32},{1,65},{33,97},{65,1},{97,33},{2,66}... | collective-permute-start | bytes 835592 | tf_op jit(solution)/shard_map/ppermute | solution.py:25
  153.4 20.1 %collective-permute-start.34 = (bf16[544,512]{1,0:T(8,128)(2,1)}, bf16[544,512]{1,0:T(8,128)(2,1)}, u32[]{:S(2)}, u32[]{:S(2)}) collective-permute-start(bf16[544,512]{1,0:T(8,128)(2,1)} %collective-permute-done.33.refs_2_), channel_id=1, source_target_pairs={{0,32},{32,0},{64,96},{96,64},{1,33},{33,1},{65,97},{97,65},{2,34}... | collective-permute-start | bytes 1671176 | tf_op jit(solution)/shard_map/ppermute | solution.py:25
  166.8 13.7 %collective-permute-start.31 = (bf16[272,512]{1,0:T(8,128)(2,1)}, bf16[272,512]{1,0:T(8,128)(2,1)}, u32[]{:S(2)}, u32[]{:S(2)}) collective-permute-start(bf16[272,512]{1,0:T(8,128)(2,1)} %get-tuple-element.130.refs_4_), channel_id=1, source_target_pairs={{0,64},{32,96},{64,0},{96,32},{1,65},{33,97},{65,1},{97,33},{2,66}... | collective-permute-start | bytes 835592 | tf_op jit(solution)/shard_map/ppermute | solution.py:25
  172.6 11.6 %collective-permute-start.27 = (bf16[272,512]{1,0:T(8,128)(2,1)S(1)}, bf16[272,512]{1,0:T(8,128)(2,1)S(1)}, u32[]{:S(2)}, u32[]{:S(2)}) collective-permute-start(bf16[272,512]{1,0:T(8,128)(2,1)S(1)} %get-tuple-element.127.refs_0_), channel_id=1, source_target_pairs={{0,32},{32,0},{64,96},{96,64},{1,33},{33,1},{65,97},{97,65},{2,34}... | collective-permute-start | bytes 835592 | tf_op jit(solution)/shard_map/ppermute | solution.py:25
  172.9 11.2 %collective-permute-start.30 = (bf16[272,512]{1,0:T(8,128)(2,1)}, bf16[272,512]{1,0:T(8,128)(2,1)S(1)}, u32[]{:S(2)}, u32[]{:S(2)}) collective-permute-start(bf16[272,512]{1,0:T(8,128)(2,1)} %get-tuple-element.130.refs_4_), channel_id=1, source_target_pairs={{0,32},{32,0},{64,96},{96,64},{1,33},{33,1},{65,97},{97,65},{2,34}... | collective-permute-start | bytes 835592 | tf_op jit(solution)/shard_map/ppermute | solution.py:25
  173.2 11.0 %collective-permute-start.29 = (bf16[272,512]{1,0:T(8,128)(2,1)}, bf16[272,512]{1,0:T(8,128)(2,1)S(1)}, u32[]{:S(2)}, u32[]{:S(2)}) collective-permute-start(bf16[272,512]{1,0:T(8,128)(2,1)} %collective-permute-done.28.refs_2_), channel_id=1, source_target_pairs={{0,32},{32,0},{64,96},{96,64},{1,33},{33,1},{65,97},{97,65},{2,34}... | collective-permute-start | bytes 835592 | tf_op jit(solution)/shard_map/ppermute | solution.py:25
  (47 other events, 361.6 us)

commit v3 on v2

--- a/solution.py
+++ b/solution.py
@@ -48,6 +48,14 @@
     return pltpu.CompilerParams(
         dimension_semantics=("arbitrary",) * axes, vmem_limit_bytes=48 << 20
     )
+
+
+def kept_of(fresh_ref, n):
+    return jnp.where(fresh_ref[n] == 1, 0.0, 1.0)
+
+
+def slot_of(place_ref, spot_ref, p):
+    return spot_ref[p] - (place_ref[1] * 8 + place_ref[2] * 2 + place_ref[3]) * 64
 
 
 def split_kernel(place_ref, keep_ref, count_ref, spot_ref, *refs):
@@ -66,7 +74,7 @@
     row = lax.broadcasted_iota(jnp.int32, (slots, 512), 0)
     keep = jnp.zeros((slots, 512), F32)
     for n in range(slots):
-        keep = jnp.where(row == n, keep_ref[n].astype(F32), keep)
+        keep = jnp.where(row == n, kept_of(keep_ref, n), keep)
     for m in range(5):
         copies[m].wait()
     for d in range(4):
@@ -85,7 +93,7 @@
         base = pl.multiple_of((at >> 4) << 4, 16)
         near = own_ref[pl.ds(base, 16)].astype(F32)
         last = jnp.sum(jnp.where(few == (at & 15), near, 0.0), axis=0, keepdims=True)
-        shift = jnp.where(row == spot_ref[p], last, shift)
+        shift = jnp.where(row == slot_of(place_ref, spot_ref, p), last, shift)
     shift_ref[...] = shift.astype(BF)
 
 
@@ -181,7 +189,7 @@
         compiler_params=params(1),
         cost_estimate=cost(0, 8 << 20),
         name="pack",
-    )(place, *in_hbm(*owns, *recvs))
+    )(place, *(in_hbm(*owns, *recvs) if n == 2 else (*owns, *recvs)))
 
 
 def swap_all(owns, n):
@@ -253,7 +261,7 @@
 def mix(place, counts, hidden, d, mu, narrow, low, held, widen, speed, slots, length):
     rows = hidden.shape[0] - slots
     once = lambda i, s, c: (0, 0)
-    args = in_hbm(hidden, mu, narrow)
+    args = [hidden] + in_hbm(mu, narrow)
     specs = [
         pl.BlockSpec(hidden.shape, once),
         pl.BlockSpec((5, 512), lambda i, s, c: (0, s[0] ^ d)),
@@ -261,7 +269,7 @@
     ]
     alias = {}
     if d > 0:
-        args += in_hbm(low, held)
+        args += [low, held]
         specs += [pl.BlockSpec(low.shape, once), ANY]
         alias = {6: 0}
     wide = 64
@@ -387,7 +395,9 @@
         start += span
         more = total.shape[0] - 2 * span
         which = lax.broadcasted_iota(jnp.int32, (more, 512), 0) + (slot0 + slot)
-        taken = jnp.logical_or(which == spot_ref[0], which == spot_ref[1])
+        taken = jnp.logical_or(
+            which == slot_of(place_ref, spot_ref, 0), which == slot_of(place_ref, spot_ref, 1)
+        )
         own = jnp.where(taken, 0.0, total[2 * span :])
         slot_ref[slot : slot + more] = own.astype(slot_ref.dtype)
         slot += more
@@ -421,7 +431,7 @@
         compiler_params=params(1),
         cost_estimate=cost(4 * span * 2048 * 512, 8 << 20),
         name="project_result",
-    )(place, counts, spots, *xs, *pieces, *(earlier if chained else []))
+    )(place, counts, spots, *xs, *in_hbm(*pieces), *(earlier if chained else []))
 
 
 SLOT_BLOCK = 8
@@ -466,7 +476,7 @@
         slot = first + s
         hit = row == jnp.where(low, slot, slot + 64)
         pick = jnp.where(hit, 1.0, 0.0).astype(BF)
-        kept = jnp.where(hit, keep_ref[slot].astype(F32), 0.0).astype(BF)
+        kept = jnp.where(hit, kept_of(keep_ref, slot), 0.0).astype(BF)
         r_b = jnp.dot(rt_ref[...].reshape(256, 128), kept, preferred_element_type=F32)
         k_b = jnp.dot(kt_ref[...].reshape(256, 128), pick, preferred_element_type=F32)
         d_b = jnp.dot(
@@ -498,6 +508,37 @@
         normed = center * lax.rsqrt(spread + NORM_EPS) * scale[:, cols] + offset[:, cols]
         out.append((normed * g_ref[here, cols].astype(F32)).astype(BF))
     return jnp.concatenate(out, axis=1)
+
+
+def place_kernel(place_ref, spot_ref, final_ref, _, state_ref, sem):
+    copies = [
+        pltpu.make_async_copy(
+            final_ref.at[p], state_ref.at[slot_of(place_ref, spot_ref, p)], sem.at[p]
+        )
+        for p in range(2)
+    ]
+    for copy in copies:
+        copy.start()
+    for copy in copies:
+        copy.wait()
+
+
+def place_states(place, spots, final, states):
+    return pl.pallas_call(
+        place_kernel,
+        out_shape=jax.ShapeDtypeStruct(states.shape, F32),
+        grid_spec=pltpu.PrefetchScalarGridSpec(
+            num_scalar_prefetch=2,
+            grid=(1,),
+            in_specs=[pl.BlockSpec(final.shape, lambda i, *s: (0, 0, 0, 0)), ANY],
+            out_specs=ANY,
+            scratch_shapes=[pltpu.SemaphoreType.DMA((2,))],
+        ),
+        input_output_aliases={3: 0},
+        compiler_params=params(1),
+        cost_estimate=cost(0, 2 << 20),
+        name="place_states",
+    )(place, spots, final, states)
 
 
 def span_tables():
@@ -736,19 +777,17 @@
 ):
     h = lax.axis_index("yh") * 2 + lax.axis_index("core")
     z, x, yl = lax.axis_index("z"), lax.axis_index("x"), lax.axis_index("yl")
-    req = z * 8 + x * 2 + yl
     place = jnp.stack([h, z, x, yl]).astype(jnp.int32)
     prompts, length, width = request_hidden_entries.shape
     slots, groups, breadth = place_memory_matrix.shape[:3]
     tokens = prompts * length
     rows = tokens + slots
-    keep = place_newness_marks != 1
     counts = request_valid_count
 
-    spots = request_destination_place - req * slots
+    spots = request_destination_place
     parts, own, new_shift = split(
         place,
-        keep.astype(jnp.int32),
+        place_newness_marks,
         counts,
         spots,
         [
@@ -815,11 +854,10 @@
     sent = []
     t0 = 0
     new_state = None
-    kept = keep.astype(jnp.int32)
     for t1 in (256, 384, 512):
         out = wkv(
             counts,
-            kept,
+            place_newness_marks,
             rkv,
             log_decay,
             gate,
@@ -846,8 +884,7 @@
         place, counts, spots, sent[1] + sent[2], late, (128, 128), 256, result, length, slots
     )
     final_state = out[3]
-    for n in range(prompts):
-        new_state = lax.dynamic_update_slice(new_state, final_state[n : n + 1], (spots[n], 0, 0, 0))
+    new_state = place_states(place, spots, final_state, new_state)
     return (prompt_hidden, decode_hidden, new_state, new_shift)
 
 

time: 190 us -> 180 us (0.947)
  local copies, waits for them, and re-layouts: 13.2 us -> 4.98 us
  waiting for transfers between devices: 14.3 us -> 18.9 us
  between operations: 5.33 us -> 1.33 us
  Pallas kernels: 107 us -> 104 us
    ppermute x36, waiting for transfers between devices: 14.3 us -> 18.9 us  [swap(): return lax.ppermute(a, names, [(i, i ^ bits) for i in range(sizes[axes])])]
    unnamed x86 -> x66, local copies, waits for them, and re-layouts: 9.18 us -> 4.86 us
    dynamic_update_slice x2 -> x0, local copies, waits for them, and re-layouts: 3.34 us -> none  [on_device(): lax.dynamic_update_slice(new_state, final_state[n:n + 1], (spots[n], 0, 0...]
    pallas_call x4, Pallas kernels: 25.8 us -> 23.6 us  [mix(): pl.pallas_call(functools.partial(mix_kernel, d=d, length=length), out_sha...]
  transfers between devices with their start and end apart: 36 -> 36, of which waited for: 8 -> 10; matrix products, arithmetic and copies ran while one was open for 2% -> 1% of each run, Pallas kernels for 40% -> 41%
where the time goes in v3:
time: 180 us
  Pallas kernels  104 us (58%)
  starting transfers between devices  48.9 us (27%)
  waiting for transfers between devices  18.9 us (10%)
  local copies, waits for them, and re-layouts  4.98 us (3%)
  other arithmetic  2.14 us (1%)
    ppermute x36, starting transfers between devices, swap(): return lax.ppermute(a, names, [(i, i ^ bits) for i in range(sizes[axes])])  48.9 us
    pallas_call x3, Pallas kernels, wkv(): pl.pallas_call(functools.partial(wkv_kernel, t0=t0, span=span, slot0=c0 *...  39.1 us
    pallas_call x4, Pallas kernels, mix(): pl.pallas_call(functools.partial(mix_kernel, d=d, length=length), out_sha...  23.6 us
    ppermute x36, waiting for transfers between devices, swap(): return lax.ppermute(a, names, [(i, i ^ bits) for i in range(sizes[axes])])  18.9 us
    pallas_call x1, Pallas kernels, project_rkv(): pl.pallas_call(rkv_kernel, out_shape=jax.ShapeDtypeStruct((3, rows, 512),...  13.7 us
    pallas_call x4, Pallas kernels, pack(): pl.pallas_call(functools.partial(pack_kernel, n=n, lot=lot), out_shape=sh...  8.62 us
    pallas_call x2, Pallas kernels, project_result(): pl.pallas_call(functools.partial(result_kernel, spans=spans, t0=t0, slot0...  8.55 us
    pallas_call x1, Pallas kernels, project_gate(): pl.pallas_call(gate_kernel, out_shape=jax.ShapeDtypeStruct((rows, 512), B...  5.97 us
  transfers between devices with their start and end apart: 36, of which 10 were waited for; matrix products, arithmetic and copies ran while one was open for 1% of the time, Pallas kernels for 41%

profile of v3, /device:TPU:1, one launch (start us, length us, event | category | flops | bytes accessed | tf_op | source)
XLA Modules:
  0.0 179.9 jit_solution(383606069159704470)
XLA Ops:
  2.7 2.9 %split.1 = (bf16[5,16,512]{2,1,0:T(8,128)(2,1)S(1)}, bf16[5,16,512]{2,1,0:T(8,128)(2,1)S(1)}, bf16[5,16,512]{2,1,0:T(8,128)(2,1)S(1)}, bf16[5,16,512]{2,1,0:T(8,...) custom-call(s32[4]{0:T(128)S(1)} %pad_add_fusion.place_ref, s32[64]{0:T(128)S(1)} %copy-done.20, ...), custom_call_target="tpu_custom_call" | custom-call | tf_op jit(solution)/shard_map/split/pallas_call | solution.py:105
  7.1 3.0 %collective-permute-start = (bf16[5,16,512]{2,1,0:T(8,128)(2,1)S(1)}, bf16[5,16,512]{2,1,0:T(8,128)(2,1)S(1)}, u32[]{:S(2)}, u32[]{:S(2)}) collective-permute-start(bf16[5,16,512]{2,1,0:T(8,128)(2,1)S(1)} %get-tuple-element.73), channel_id=1, source_target_pairs={{0,96},{32,64},{64,32},{96,0},{1,97},{33,65},{65,33},{97,1},{2,98}... | collective-permute-start | bytes 245768 | tf_op jit(solution)/shard_map/ppermute | solution.py:25
  10.7 2.0 %collective-permute-done = bf16[5,16,512]{2,1,0:T(8,128)(2,1)S(1)} collective-permute-done((bf16[5,16,512]{2,1,0:T(8,128)(2,1)S(1)}, bf16[5,16,512]{2,1,0:T(8,128)(2,1)S(1)}, u32[]{:S(2)}, u32[]{:S(2)}) %collective-permute-start) | collective-permute-done | bytes 81952 | tf_op jit(solution)/shard_map/ppermute | solution.py:25
  12.8 2.1 %collective-permute-done.4 = bf16[5,16,512]{2,1,0:T(8,128)(2,1)S(1)} collective-permute-done((bf16[5,16,512]{2,1,0:T(8,128)(2,1)S(1)}, bf16[5,16,512]{2,1,0:T(8,128)(2,1)S(1)}, u32[]{:S(2)}, u32[]{:S(2)}) %collective-permute-start.4) | collective-permute-done | bytes 81952 | tf_op jit(solution)/shard_map/ppermute | solution.py:25
  16.0 3.0 %collective-permute-start.1 = (bf16[1152,512]{1,0:T(8,128)(2,1)S(1)}, bf16[1152,512]{1,0:T(8,128)(2,1)S(1)}, u32[]{:S(2)}, u32[]{:S(2)}) collective-permute-start(bf16[1152,512]{1,0:T(8,128)(2,1)S(1)} %get-tuple-element.74.refs_0_), channel_id=1, source_target_pairs={{0,64},{32,96},{64,0},{96,32},{1,65},{33,97},{65,1},{97,33},{2,66}... | collective-permute-start | bytes 3538952 | tf_op jit(solution)/shard_map/ppermute | solution.py:25
  19.7 5.7 %mix.4 = (bf16[5,1088,2048]{2,1,0:T(8,128)(2,1)}, f32[1088,64]{1,0:T(8,128)S(1)}) custom-call(s32[4]{0:T(128)S(1)} %pad_add_fusion.place_ref, s32[2]{0:T(128)S(1)} %copy-done.15, bf16[1152,512]{1,0:T(8,128)(2,1)S(1)} %get-tuple-element.74.refs_0_, f32[5,2048]{1,0:T(8,128)} %refs_1_.9, bf16[64,2048]{1,0:T(8,128)(2,1)} %bitcast.24), custom_call_target="tpu_custom_call" | custom-call | flops 11141120 | bytes 6684672 | tf_op jit(solution)/shard_map/mix/pallas_call | solution.py:280
  29.6 1.8 %collective-permute-start.9 = (bf16[1,1,5,32,512]{4,3,2,1,0:T(8,128)(2,1)S(1)}, bf16[1,1,5,32,512]{4,3,2,1,0:T(8,128)(2,1)S(1)}, u32[]{:S(2)}, u32[]{:S(2)}) collective-permute-start(bf16[1,1,5,32,512]{4,3,2,1,0:T(8,128)(2,1)S(1)} %get-tuple-element.143.refs_2_), channel_id=1, source_target_pairs={{0,6},{2,4},{4,2},{6,0},{1,7},{3,5},{5,3},{7,1},{8,14},{10,12},{12... | collective-permute-start | bytes 491528 | tf_op jit(solution)/shard_map/ppermute | solution.py:25
  31.5 2.2 %collective-permute-start.10 = (bf16[1,1,5,32,512]{4,3,2,1,0:T(8,128)(2,1)S(1)}, bf16[1,1,5,32,512]{4,3,2,1,0:T(8,128)(2,1)S(1)}, u32[]{:S(2)}, u32[]{:S(2)}) collective-permute-start(bf16[1,1,5,32,512]{4,3,2,1,0:T(8,128)(2,1)S(1)} %get-tuple-element.140.refs_3_), channel_id=1, source_target_pairs={{0,24},{8,16},{16,8},{24,0},{1,25},{9,17},{17,9},{25,1},{2,26},{10... | collective-permute-start | bytes 491528 | tf_op jit(solution)/shard_map/ppermute | solution.py:25
  35.3 1.8 %collective-permute-done.10.refs_7_ = bf16[1,1,5,32,512]{4,3,2,1,0:T(8,128)(2,1)S(1)} collective-permute-done((bf16[1,1,5,32,512]{4,3,2,1,0:T(8,128)(2,1)S(1)}, bf16[1,1,5,32,512]{4,3,2,1,0:T(8,128)(2,1)S(1)}, u32[]{:S(2)}, u32[]{:S(2)}) %collective-permute-start.10) | collective-permute-done | bytes 163872 | tf_op jit(solution)/shard_map/ppermute | solution.py:25
  37.1 2.4 %pack.4 = (bf16[1,2,5,32,512]{4,3,2,1,0:T(8,128)(2,1)S(1)}, bf16[2,1,5,32,512]{4,3,2,1,0:T(8,128)(2,1)S(1)}, bf16[1,2,5,32,512]{4,3,2,1,0:T(8,128)(2,1)S(1)}, bf16[2,1,5,32,512]{4,3,2,1,0:T(8,128)(2,1)S(1)}) custom-call(s32[4]{0:T(128)S(1)} %pad_add_fusion.place_ref, bf16[1,1,5,32,512]{4,3,2,1,0:T(8,128)(2,1)S(1)} %get-tuple-element.141.refs_0_, ...), custom_call_target="tpu_custom_call" | custom-call | bytes 8388608 | tf_op jit(solution)/shard_map/pack/pallas_call | solution.py:179
  40.8 2.4 %collective-permute-start.13 = (bf16[1,2,5,32,512]{4,3,2,1,0:T(8,128)(2,1)S(1)}, bf16[1,2,5,32,512]{4,3,2,1,0:T(8,128)(2,1)S(1)}, u32[]{:S(2)}, u32[]{:S(2)}) collective-permute-start(bf16[1,2,5,32,512]{4,3,2,1,0:T(8,128)(2,1)S(1)} %get-tuple-element.90.refs_2_), channel_id=1, source_target_pairs={{0,24},{8,16},{16,8},{24,0},{1,25},{9,17},{17,9},{25,1},{2,26},{10... | collective-permute-start | bytes 983048 | tf_op jit(solution)/shard_map/ppermute | solution.py:25
  43.8 5.7 %mix.5 = (bf16[5,1088,2048]{2,1,0:T(8,128)(2,1)}, f32[1088,64]{1,0:T(8,128)S(1)}) custom-call(s32[4]{0:T(128)S(1)} %pad_add_fusion.place_ref, s32[2]{0:T(128)S(1)} %copy-done.16, bf16[1152,512]{1,0:T(8,128)(2,1)S(1)} %collective-permute-done.6.refs_0_, f32[5,2048]{1,0:T(8,128)} %refs_1_.9, ...), custom_call_target="tpu_custom_call", output_to_operand_aliasing={{0}: (6, {})} | custom-call | flops 11141120 | bytes 6684672 | tf_op jit(solution)/shard_map/mix/pallas_call | solution.py:280
  54.2 6.5 %collective-permute-start.2 = (bf16[1152,512]{1,0:T(8,128)(2,1)S(1)}, bf16[1152,512]{1,0:T(8,128)(2,1)S(1)}, u32[]{:S(2)}, u32[]{:S(2)}) collective-permute-start(bf16[1152,512]{1,0:T(8,128)(2,1)S(1)} %collective-permute-done.1.refs_0_), channel_id=1, source_target_pairs={{0,32},{32,0},{64,96},{96,64},{1,33},{33,1},{65,97},{97,65},{2,34}... | collective-permute-start | bytes 3538952 | tf_op jit(solution)/shard_map/ppermute | solution.py:25
  60.6 5.7 %mix.6 = (bf16[5,1088,2048]{2,1,0:T(8,128)(2,1)}, f32[1088,64]{1,0:T(8,128)S(1)}) custom-call(s32[4]{0:T(128)S(1)} %pad_add_fusion.place_ref, s32[2]{0:T(128)S(1)} %copy-done.16, bf16[1152,512]{1,0:T(8,128)(2,1)S(1)} %collective-permute-done.1.refs_0_, f32[5,2048]{1,0:T(8,128)} %refs_1_.9, ...), custom_call_target="tpu_custom_call", output_to_operand_aliasing={{0}: (6, {})} | custom-call | flops 11141120 | bytes 6684672 | tf_op jit(solution)/shard_map/mix/pallas_call | solution.py:280
  67.9 2.6 %pack.6 = (bf16[2,4,3,32,512]{4,3,2,1,0:T(8,128)(2,1)S(1)}, bf16[4,2,3,32,512]{4,3,2,1,0:T(8,128)(2,1)S(1)}, bf16[2,4,3,32,512]{4,3,2,1,0:T(8,128)(2,1)S(1)}, bf16[4,2,3,32,512]{4,3,2,1,0:T(8,128)(2,1)S(1)}) custom-call(s32[4]{0:T(128)S(1)} %pad_add_fusion.place_ref, bf16[2,2,5,32,512]{4,3,2,1,0:T(8,128)(2,1)} %copy-done.8, ...), custom_call_target="tpu_custom_call" | custom-call | bytes 8388608 | tf_op jit(solution)/shard_map/pack/pallas_call | solution.py:179
  70.5 2.3 %collective-permute-start.19 = (bf16[2,4,3,32,512]{4,3,2,1,0:T(8,128)(2,1)S(1)}, bf16[2,4,3,32,512]{4,3,2,1,0:T(8,128)(2,1)S(1)}, u32[]{:S(2)}, u32[]{:S(2)}) collective-permute-start(bf16[2,4,3,32,512]{4,3,2,1,0:T(8,128)(2,1)S(1)} %get-tuple-element.104.refs_0_), channel_id=1, source_target_pairs={{0,24},{8,16},{16,8},{24,0},{1,25},{9,17},{17,9},{25,1},{2,26},{10... | collective-permute-start | bytes 2359304 | tf_op jit(solution)/shard_map/ppermute | solution.py:25
  75.6 6.4 %mix.7 = (bf16[5,1088,2048]{2,1,0:T(8,128)(2,1)}, f32[1088,512]{1,0:T(8,128)S(1)}) custom-call(s32[4]{0:T(128)S(1)} %pad_add_fusion.place_ref, s32[2]{0:T(128)S(1)} %copy-done.17, bf16[1152,512]{1,0:T(8,128)(2,1)S(1)} %collective-permute-done.2.refs_0_, f32[5,2048]{1,0:T(8,128)} %refs_1_.9, ...), custom_call_target="tpu_custom_call", output_to_operand_aliasing={{0}: (6, {})} | custom-call | flops 11141120 | bytes 6684672 | tf_op jit(solution)/shard_map/mix/pallas_call | solution.py:280
  82.1 2.3 %pack.7 = (bf16[2,4,2,32,512]{4,3,2,1,0:T(8,128)(2,1)S(1)}, bf16[4,2,2,32,512]{4,3,2,1,0:T(8,128)(2,1)S(1)}, bf16[2,4,2,32,512]{4,3,2,1,0:T(8,128)(2,1)S(1)}, bf16[4,2,2,32,512]{4,3,2,1,0:T(8,128)(2,1)S(1)}) custom-call(s32[4]{0:T(128)S(1)} %pad_add_fusion.place_ref, bf16[2,2,5,32,512]{4,3,2,1,0:T(8,128)(2,1)} %copy-done.8, ...), custom_call_target="tpu_custom_call" | custom-call | bytes 8388608 | tf_op jit(solution)/shard_map/pack/pallas_call | solution.py:179
  84.4 2.1 %collective-permute-done.19.refs_4_ = bf16[2,4,3,32,512]{4,3,2,1,0:T(8,128)(2,1)S(1)} collective-permute-done((bf16[2,4,3,32,512]{4,3,2,1,0:T(8,128)(2,1)S(1)}, bf16[2,4,3,32,512]{4,3,2,1,0:T(8,128)(2,1)S(1)}, u32[]{:S(2)}, u32[]{:S(2)}) %collective-permute-start.19) | collective-permute-done | bytes 786464 | tf_op jit(solution)/shard_map/ppermute | solution.py:25
  88.9 2.3 %collective-permute-done.22.refs_7_ = bf16[4,2,3,32,512]{4,3,2,1,0:T(8,128)(2,1)S(1)} collective-permute-done((bf16[4,2,3,32,512]{4,3,2,1,0:T(8,128)(2,1)S(1)}, bf16[4,2,3,32,512]{4,3,2,1,0:T(8,128)(2,1)S(1)}, u32[]{:S(2)}, u32[]{:S(2)}) %collective-permute-start.22) | collective-permute-done | bytes 786464 | tf_op jit(solution)/shard_map/ppermute | solution.py:25
  92.8 13.7 %project_rkv.1.refs_0_.refs_1_.refs_2_.refs_5_.refs_6_.refs_7_.refs_13_.refs_14_.refs_15_ = bf16[3,1088,512]{2,1,0:T(8,128)(2,1)} custom-call(s32[4]{0:T(128)S(1)} %pad_add_fusion.place_ref, bf16[5,1088,2048]{2,1,0:T(8,128)(2,1)} %get-tuple-element.86.x_ref, bf16[2,4,3,32,512]{4,3,2,1,0:T(8,128)(2,1)S(1)} %get-tuple-element.104.refs_0_, ...), custom_call_target="tpu_custom_call" | custom-call | flops 6845104128 | bytes 25165824 | tf_op jit(solution)/shard_map/project_rkv/pallas_call | solution.py:327
  106.6 6.0 %project_gate.1.refs_4_.refs_9_.refs_17_ = bf16[1088,512]{1,0:T(8,128)(2,1)S(1)} custom-call(s32[4]{0:T(128)S(1)} %pad_add_fusion.place_ref, bf16[5,1088,2048]{2,1,0:T(8,128)(2,1)} %get-tuple-element.86.x_ref, bf16[2,4,2,32,512]{4,3,2,1,0:T(8,128)(2,1)S(1)} %get-tuple-element.121.refs_0_.refs_4_.refs_8_, ...), custom_call_target="tpu_custom_call" | custom-call | flops 2281701376 | bytes 8388608 | tf_op jit(solution)/shard_map/project_gate/pallas_call | solution.py:361
  112.7 17.4 %wkv.3 = (bf16[544,512]{1,0:T(8,128)(2,1)S(1)}, f32[2,4,128,128]{3,2,1,0:T(8,128)S(1)}, f32[64,8,64,64]{3,2,1,0:T(8,128)}) custom-call(s32[2]{0:T(128)S(1)} %copy-done.17, s32[64]{0:T(128)S(1)} %copy-done.21, bf16[456,128]{1,0:T(8,128)(2,1)S(1)} %copy-done.12, ...), custom_call_target="tpu_custom_call" | custom-call | flops 20480000000 | bytes 33554432 | tf_op jit(solution)/shard_map/wkv/pallas_call | solution.py:727
  130.1 5.4 %collective-permute-start.32 = (bf16[544,512]{1,0:T(8,128)(2,1)S(1)}, bf16[544,512]{1,0:T(8,128)(2,1)S(1)}, u32[]{:S(2)}, u32[]{:S(2)}) collective-permute-start(bf16[544,512]{1,0:T(8,128)(2,1)S(1)} %get-tuple-element.131.refs_0_), channel_id=1, source_target_pairs={{0,32},{32,0},{64,96},{96,64},{1,33},{33,1},{65,97},{97,65},{2,34}... | collective-permute-start | bytes 1671176 | tf_op jit(solution)/shard_map/ppermute | solution.py:25
  135.5 2.1 %collective-permute-start.33 = (bf16[544,512]{1,0:T(8,128)(2,1)S(1)}, bf16[544,512]{1,0:T(8,128)(2,1)S(1)}, u32[]{:S(2)}, u32[]{:S(2)}) collective-permute-start(bf16[544,512]{1,0:T(8,128)(2,1)S(1)} %get-tuple-element.131.refs_0_), channel_id=1, source_target_pairs={{0,64},{32,96},{64,0},{96,32},{1,65},{33,97},{65,1},{97,33},{2,66}... | collective-permute-start | bytes 1671176 | tf_op jit(solution)/shard_map/ppermute | solution.py:25
  137.7 10.3 %wkv.4 = (bf16[272,512]{1,0:T(8,128)(2,1)S(1)}, f32[2,4,128,128]{3,2,1,0:T(8,128)S(1)}, f32[64,8,64,64]{3,2,1,0:T(8,128)}) custom-call(s32[2]{0:T(128)S(1)} %copy-done.17, s32[64]{0:T(128)S(1)} %copy-done.21, bf16[456,128]{1,0:T(8,128)(2,1)S(1)} %copy-done.12, ...), custom_call_target="tpu_custom_call", output_to_operand_aliasing={{2}: (21, {})} | custom-call | flops 10240000000 | bytes 16777216 | tf_op jit(solution)/shard_map/wkv/pallas_call | solution.py:727
  148.9 2.4 %collective-permute-done.33.refs_2_ = bf16[544,512]{1,0:T(8,128)(2,1)S(1)} collective-permute-done((bf16[544,512]{1,0:T(8,128)(2,1)S(1)}, bf16[544,512]{1,0:T(8,128)(2,1)S(1)}, u32[]{:S(2)}, u32[]{:S(2)}) %collective-permute-start.33) | collective-permute-done | bytes 557088 | tf_op jit(solution)/shard_map/ppermute | solution.py:25
  152.1 11.4 %wkv.5 = (bf16[272,512]{1,0:T(8,128)(2,1)S(1)}, f32[2,4,128,128]{3,2,1,0:T(8,128)}, f32[64,8,64,64]{3,2,1,0:T(8,128)}, f32[2,8,64,64]{3,2,1,0:T(8,128)S(1)}) custom-call(s32[2]{0:T(128)S(1)} %copy-done.17, s32[64]{0:T(128)S(1)} %copy-done.21, bf16[456,128]{1,0:T(8,128)(2,1)S(1)} %copy-done.12, ...), custom_call_target="tpu_custom_call", output_to_operand_aliasing={{2}: (21, {})} | custom-call | flops 10240000000 | bytes 16777216 | tf_op jit(solution)/shard_map/wkv/pallas_call | solution.py:727
  163.5 2.6 %collective-permute-start.31 = (bf16[272,512]{1,0:T(8,128)(2,1)S(1)}, bf16[272,512]{1,0:T(8,128)(2,1)S(1)}, u32[]{:S(2)}, u32[]{:S(2)}) collective-permute-start(bf16[272,512]{1,0:T(8,128)(2,1)S(1)} %get-tuple-element.130.refs_4_), channel_id=1, source_target_pairs={{0,64},{32,96},{64,0},{96,32},{1,65},{33,97},{65,1},{97,33},{2,66}... | collective-permute-start | bytes 835592 | tf_op jit(solution)/shard_map/ppermute | solution.py:25
  166.9 4.3 %project_result.2 = (bf16[2,512,512]{2,1,0:T(8,128)(2,1)}, bf16[64,512]{1,0:T(8,128)(2,1)}) custom-call(s32[4]{0:T(128)S(1)} %pad_add_fusion.place_ref, s32[2]{0:T(128)S(1)} %copy-done.17, s32[2]{0:T(128)S(1)} %copy-done.19, bf16[544,512]{1,0:T(8,128)(2,1)S(1)} %get-tuple-element.131.refs_0_, bf16[544,512]{1,0:T(8,128)(2,1)S(1)} %collective-permute-done.32.refs_1_, ...), custom_call_target="tpu_custom_call" | custom-call | flops 1073741824 | bytes 8388608 | tf_op jit(solution)/shard_map/project_result/pallas_call | solution.py:412
  171.2 2.1 %collective-permute-done.31.refs_6_ = bf16[272,512]{1,0:T(8,128)(2,1)S(1)} collective-permute-done((bf16[272,512]{1,0:T(8,128)(2,1)S(1)}, bf16[272,512]{1,0:T(8,128)(2,1)S(1)}, u32[]{:S(2)}, u32[]{:S(2)}) %collective-permute-start.31) | collective-permute-done | bytes 278560 | tf_op jit(solution)/shard_map/ppermute | solution.py:25
  175.5 4.3 %project_result.3 = (bf16[2,512,512]{2,1,0:T(8,128)(2,1)}, bf16[64,512]{1,0:T(8,128)(2,1)}) custom-call(s32[4]{0:T(128)S(1)} %pad_add_fusion.place_ref, s32[2]{0:T(128)S(1)} %copy-done.17, s32[2]{0:T(128)S(1)} %copy-done.19, bf16[272,512]{1,0:T(8,128)(2,1)S(1)} %get-tuple-element.127.refs_0_, ...), custom_call_target="tpu_custom_call", output_to_operand_aliasing={{0}: (19, {}), {1}: (20, {})} | custom-call | flops 1073741824 | bytes 8388608 | tf_op jit(solution)/shard_map/project_result/pallas_call | solution.py:412
  (131 shorter events, 31.4 us)
Async XLA Ops:
  5.6 19.9 %collective-permute-start.6 = (bf16[1152,512]{1,0:T(8,128)(2,1)S(1)}, bf16[1152,512]{1,0:T(8,128)(2,1)S(1)}, u32[]{:S(2)}, u32[]{:S(2)}) collective-permute-start(bf16[1152,512]{1,0:T(8,128)(2,1)S(1)} %get-tuple-element.74.refs_0_), channel_id=1, source_target_pairs={{0,32},{32,0},{64,96},{96,64},{1,33},{33,1},{65,97},{97,65},{2,34}... | collective-permute-start | bytes 3538952 | tf_op jit(solution)/shard_map/ppermute | solution.py:25
  7.1 5.7 %collective-permute-start = (bf16[5,16,512]{2,1,0:T(8,128)(2,1)S(1)}, bf16[5,16,512]{2,1,0:T(8,128)(2,1)S(1)}, u32[]{:S(2)}, u32[]{:S(2)}) collective-permute-start(bf16[5,16,512]{2,1,0:T(8,128)(2,1)S(1)} %get-tuple-element.73), channel_id=1, source_target_pairs={{0,96},{32,64},{64,32},{96,0},{1,97},{33,65},{65,33},{97,1},{2,98}... | collective-permute-start | bytes 245768 | tf_op jit(solution)/shard_map/ppermute | solution.py:25
  15.6 9.9 %collective-permute-start.5 = (bf16[4,5,16,512]{3,2,1,0:T(8,128)(2,1)}, bf16[4,5,16,512]{3,2,1,0:T(8,128)(2,1)}, u32[]{:S(2)}, u32[]{:S(2)}) collective-permute-start(bf16[4,5,16,512]{3,2,1,0:T(8,128)(2,1)} %pad_maximum_fusion), channel_id=1, source_target_pairs={{0,1},{1,0},{2,3},{3,2},{4,5},{5,4},{6,7},{7,6},{8,9},{9,8},{10,11... | collective-permute-start | bytes 983048 | tf_op jit(solution)/shard_map/ppermute | solution.py:25
  16.0 38.1 %collective-permute-start.1 = (bf16[1152,512]{1,0:T(8,128)(2,1)S(1)}, bf16[1152,512]{1,0:T(8,128)(2,1)S(1)}, u32[]{:S(2)}, u32[]{:S(2)}) collective-permute-start(bf16[1152,512]{1,0:T(8,128)(2,1)S(1)} %get-tuple-element.74.refs_0_), channel_id=1, source_target_pairs={{0,64},{32,96},{64,0},{96,32},{1,65},{33,97},{65,1},{97,33},{2,66}... | collective-permute-start | bytes 3538952 | tf_op jit(solution)/shard_map/ppermute | solution.py:25
  26.7 7.0 %collective-permute-start.7 = (bf16[1,1,5,32,512]{4,3,2,1,0:T(8,128)(2,1)S(1)}, bf16[1,1,5,32,512]{4,3,2,1,0:T(8,128)(2,1)S(1)}, u32[]{:S(2)}, u32[]{:S(2)}) collective-permute-start(bf16[1,1,5,32,512]{4,3,2,1,0:T(8,128)(2,1)S(1)} %get-tuple-element.141.refs_0_), channel_id=1, source_target_pairs={{0,2},{2,0},{4,6},{6,4},{1,3},{3,1},{5,7},{7,5},{8,10},{10,8},{12,... | collective-permute-start | bytes 491528 | tf_op jit(solution)/shard_map/ppermute | solution.py:25
  28.0 5.7 %collective-permute-start.8 = (bf16[1,1,5,32,512]{4,3,2,1,0:T(8,128)(2,1)S(1)}, bf16[1,1,5,32,512]{4,3,2,1,0:T(8,128)(2,1)S(1)}, u32[]{:S(2)}, u32[]{:S(2)}) collective-permute-start(bf16[1,1,5,32,512]{4,3,2,1,0:T(8,128)(2,1)S(1)} %get-tuple-element.142.refs_1_), channel_id=1, source_target_pairs={{0,8},{8,0},{16,24},{24,16},{1,9},{9,1},{17,25},{25,17},{2,10},{10... | collective-permute-start | bytes 491528 | tf_op jit(solution)/shard_map/ppermute | solution.py:25
  31.5 5.7 %collective-permute-start.10 = (bf16[1,1,5,32,512]{4,3,2,1,0:T(8,128)(2,1)S(1)}, bf16[1,1,5,32,512]{4,3,2,1,0:T(8,128)(2,1)S(1)}, u32[]{:S(2)}, u32[]{:S(2)}) collective-permute-start(bf16[1,1,5,32,512]{4,3,2,1,0:T(8,128)(2,1)S(1)} %get-tuple-element.140.refs_3_), channel_id=1, source_target_pairs={{0,24},{8,16},{16,8},{24,0},{1,25},{9,17},{17,9},{25,1},{2,26},{10... | collective-permute-start | bytes 491528 | tf_op jit(solution)/shard_map/ppermute | solution.py:25
  39.5 10.1 %collective-permute-start.11 = (bf16[1,2,5,32,512]{4,3,2,1,0:T(8,128)(2,1)S(1)}, bf16[1,2,5,32,512]{4,3,2,1,0:T(8,128)(2,1)S(1)}, u32[]{:S(2)}, u32[]{:S(2)}) collective-permute-start(bf16[1,2,5,32,512]{4,3,2,1,0:T(8,128)(2,1)S(1)} %get-tuple-element.88.refs_0_), channel_id=1, source_target_pairs={{0,8},{8,0},{16,24},{24,16},{1,9},{9,1},{17,25},{25,17},{2,10},{10... | collective-permute-start | bytes 983048 | tf_op jit(solution)/shard_map/ppermute | solution.py:25
  39.9 9.7 %collective-permute-start.12 = (bf16[2,1,5,32,512]{4,3,2,1,0:T(8,128)(2,1)S(1)}, bf16[2,1,5,32,512]{4,3,2,1,0:T(8,128)(2,1)S(1)}, u32[]{:S(2)}, u32[]{:S(2)}) collective-permute-start(bf16[2,1,5,32,512]{4,3,2,1,0:T(8,128)(2,1)S(1)} %get-tuple-element.89.refs_1_), channel_id=1, source_target_pairs={{0,6},{2,4},{4,2},{6,0},{1,7},{3,5},{5,3},{7,1},{8,14},{10,12},{12... | collective-permute-start | bytes 983048 | tf_op jit(solution)/shard_map/ppermute | solution.py:25
  40.8 8.8 %collective-permute-start.13 = (bf16[1,2,5,32,512]{4,3,2,1,0:T(8,128)(2,1)S(1)}, bf16[1,2,5,32,512]{4,3,2,1,0:T(8,128)(2,1)S(1)}, u32[]{:S(2)}, u32[]{:S(2)}) collective-permute-start(bf16[1,2,5,32,512]{4,3,2,1,0:T(8,128)(2,1)S(1)} %get-tuple-element.90.refs_2_), channel_id=1, source_target_pairs={{0,24},{8,16},{16,8},{24,0},{1,25},{9,17},{17,9},{25,1},{2,26},{10... | collective-permute-start | bytes 983048 | tf_op jit(solution)/shard_map/ppermute | solution.py:25
  43.2 6.4 %collective-permute-start.14 = (bf16[2,1,5,32,512]{4,3,2,1,0:T(8,128)(2,1)S(1)}, bf16[2,1,5,32,512]{4,3,2,1,0:T(8,128)(2,1)S(1)}, u32[]{:S(2)}, u32[]{:S(2)}) collective-permute-start(bf16[2,1,5,32,512]{4,3,2,1,0:T(8,128)(2,1)S(1)} %get-tuple-element.91.refs_3_), channel_id=1, source_target_pairs={{0,2},{2,0},{4,6},{6,4},{1,3},{3,1},{5,7},{7,5},{8,10},{10,8},{12,... | collective-permute-start | bytes 983048 | tf_op jit(solution)/shard_map/ppermute | solution.py:25
  51.0 15.3 %collective-permute-start.15 = (bf16[2,2,5,32,512]{4,3,2,1,0:T(8,128)(2,1)S(1)}, bf16[2,2,5,32,512]{4,3,2,1,0:T(8,128)(2,1)S(1)}, u32[]{:S(2)}, u32[]{:S(2)}) collective-permute-start(bf16[2,2,5,32,512]{4,3,2,1,0:T(8,128)(2,1)S(1)} %get-tuple-element.96.refs_0_), channel_id=1, source_target_pairs={{0,6},{2,4},{4,2},{6,0},{1,7},{3,5},{5,3},{7,1},{8,14},{10,12},{12... | collective-permute-start | bytes 1966088 | tf_op jit(solution)/shard_map/ppermute | solution.py:25
  52.6 13.8 %collective-permute-start.16 = (bf16[2,2,5,32,512]{4,3,2,1,0:T(8,128)(2,1)S(1)}, bf16[2,2,5,32,512]{4,3,2,1,0:T(8,128)(2,1)S(1)}, u32[]{:S(2)}, u32[]{:S(2)}) collective-permute-start(bf16[2,2,5,32,512]{4,3,2,1,0:T(8,128)(2,1)S(1)} %get-tuple-element.97.refs_1_), channel_id=1, source_target_pairs={{0,24},{8,16},{16,8},{24,0},{1,25},{9,17},{17,9},{25,1},{2,26},{10... | collective-permute-start | bytes 1966088 | tf_op jit(solution)/shard_map/ppermute | solution.py:25
  53.6 12.8 %collective-permute-start.17 = (bf16[2,2,5,32,512]{4,3,2,1,0:T(8,128)(2,1)S(1)}, bf16[2,2,5,32,512]{4,3,2,1,0:T(8,128)(2,1)S(1)}, u32[]{:S(2)}, u32[]{:S(2)}) collective-permute-start(bf16[2,2,5,32,512]{4,3,2,1,0:T(8,128)(2,1)S(1)} %get-tuple-element.98.refs_2_), channel_id=1, source_target_pairs={{0,2},{2,0},{4,6},{6,4},{1,3},{3,1},{5,7},{7,5},{8,10},{10,8},{12,... | collective-permute-start | bytes 1966088 | tf_op jit(solution)/shard_map/ppermute | solution.py:25
  54.0 12.3 %collective-permute-start.18 = (bf16[2,2,5,32,512]{4,3,2,1,0:T(8,128)(2,1)S(1)}, bf16[2,2,5,32,512]{4,3,2,1,0:T(8,128)(2,1)S(1)}, u32[]{:S(2)}, u32[]{:S(2)}) collective-permute-start(bf16[2,2,5,32,512]{4,3,2,1,0:T(8,128)(2,1)S(1)} %get-tuple-element.99.refs_3_), channel_id=1, source_target_pairs={{0,8},{8,0},{16,24},{24,16},{1,9},{9,1},{17,25},{25,17},{2,10},{10... | collective-permute-start | bytes 1966088 | tf_op jit(solution)/shard_map/ppermute | solution.py:25
  54.2 21.5 %collective-permute-start.2 = (bf16[1152,512]{1,0:T(8,128)(2,1)S(1)}, bf16[1152,512]{1,0:T(8,128)(2,1)S(1)}, u32[]{:S(2)}, u32[]{:S(2)}) collective-permute-start(bf16[1152,512]{1,0:T(8,128)(2,1)S(1)} %collective-permute-done.1.refs_0_), channel_id=1, source_target_pairs={{0,32},{32,0},{64,96},{96,64},{1,33},{33,1},{65,97},{97,65},{2,34}... | collective-permute-start | bytes 3538952 | tf_op jit(solution)/shard_map/ppermute | solution.py:25
  70.5 16.0 %collective-permute-start.19 = (bf16[2,4,3,32,512]{4,3,2,1,0:T(8,128)(2,1)S(1)}, bf16[2,4,3,32,512]{4,3,2,1,0:T(8,128)(2,1)S(1)}, u32[]{:S(2)}, u32[]{:S(2)}) collective-permute-start(bf16[2,4,3,32,512]{4,3,2,1,0:T(8,128)(2,1)S(1)} %get-tuple-element.104.refs_0_), channel_id=1, source_target_pairs={{0,24},{8,16},{16,8},{24,0},{1,25},{9,17},{17,9},{25,1},{2,26},{10... | collective-permute-start | bytes 2359304 | tf_op jit(solution)/shard_map/ppermute | solution.py:25
  72.8 14.8 %collective-permute-start.20 = (bf16[4,2,3,32,512]{4,3,2,1,0:T(8,128)(2,1)S(1)}, bf16[4,2,3,32,512]{4,3,2,1,0:T(8,128)(2,1)S(1)}, u32[]{:S(2)}, u32[]{:S(2)}) collective-permute-start(bf16[4,2,3,32,512]{4,3,2,1,0:T(8,128)(2,1)S(1)} %get-tuple-element.105.refs_1_), channel_id=1, source_target_pairs={{0,2},{2,0},{4,6},{6,4},{1,3},{3,1},{5,7},{7,5},{8,10},{10,8},{12,... | collective-permute-start | bytes 2359304 | tf_op jit(solution)/shard_map/ppermute | solution.py:25
  74.0 14.9 %collective-permute-start.21 = (bf16[2,4,3,32,512]{4,3,2,1,0:T(8,128)(2,1)S(1)}, bf16[2,4,3,32,512]{4,3,2,1,0:T(8,128)(2,1)S(1)}, u32[]{:S(2)}, u32[]{:S(2)}) collective-permute-start(bf16[2,4,3,32,512]{4,3,2,1,0:T(8,128)(2,1)S(1)} %get-tuple-element.106.refs_2_), channel_id=1, source_target_pairs={{0,8},{8,0},{16,24},{24,16},{1,9},{9,1},{17,25},{25,17},{2,10},{10... | collective-permute-start | bytes 2359304 | tf_op jit(solution)/shard_map/ppermute | solution.py:25
  74.5 16.7 %collective-permute-start.22 = (bf16[4,2,3,32,512]{4,3,2,1,0:T(8,128)(2,1)S(1)}, bf16[4,2,3,32,512]{4,3,2,1,0:T(8,128)(2,1)S(1)}, u32[]{:S(2)}, u32[]{:S(2)}) collective-permute-start(bf16[4,2,3,32,512]{4,3,2,1,0:T(8,128)(2,1)S(1)} %get-tuple-element.107.refs_3_), channel_id=1, source_target_pairs={{0,6},{2,4},{4,2},{6,0},{1,7},{3,5},{5,3},{7,1},{8,14},{10,12},{12... | collective-permute-start | bytes 2359304 | tf_op jit(solution)/shard_map/ppermute | solution.py:25
  91.2 15.4 %collective-permute-start.23 = (bf16[2,4,2,32,512]{4,3,2,1,0:T(8,128)(2,1)S(1)}, bf16[2,4,2,32,512]{4,3,2,1,0:T(8,128)(2,1)S(1)}, u32[]{:S(2)}, u32[]{:S(2)}) collective-permute-start(bf16[2,4,2,32,512]{4,3,2,1,0:T(8,128)(2,1)S(1)} %get-tuple-element.121.refs_0_.refs_4_.refs_8_), channel_id=1, source_target_pairs={{0,24},{8,16},{16,8},{24,0},{1,25},{9,17},{17,9},{25,1},{2,26},{10... | collective-permute-start | bytes 1572872 | tf_op jit(solution)/shard_map/ppermute | solution.py:25
  92.1 14.4 %collective-permute-start.24 = (bf16[4,2,2,32,512]{4,3,2,1,0:T(8,128)(2,1)S(1)}, bf16[4,2,2,32,512]{4,3,2,1,0:T(8,128)(2,1)S(1)}, u32[]{:S(2)}, u32[]{:S(2)}) collective-permute-start(bf16[4,2,2,32,512]{4,3,2,1,0:T(8,128)(2,1)S(1)} %get-tuple-element.122.refs_1_.refs_5_.refs_9_), channel_id=1, source_target_pairs={{0,2},{2,0},{4,6},{6,4},{1,3},{3,1},{5,7},{7,5},{8,10},{10,8},{12,... | collective-permute-start | bytes 1572872 | tf_op jit(solution)/shard_map/ppermute | solution.py:25
  92.1 14.5 %collective-permute-start.25 = (bf16[2,4,2,32,512]{4,3,2,1,0:T(8,128)(2,1)S(1)}, bf16[2,4,2,32,512]{4,3,2,1,0:T(8,128)(2,1)S(1)}, u32[]{:S(2)}, u32[]{:S(2)}) collective-permute-start(bf16[2,4,2,32,512]{4,3,2,1,0:T(8,128)(2,1)S(1)} %get-tuple-element.123.refs_2_.refs_6_.refs_10_), channel_id=1, source_target_pairs={{0,8},{8,0},{16,24},{24,16},{1,9},{9,1},{17,25},{25,17},{2,10},{10... | collective-permute-start | bytes 1572872 | tf_op jit(solution)/shard_map/ppermute | solution.py:25
  92.1 14.5 %collective-permute-start.26 = (bf16[4,2,2,32,512]{4,3,2,1,0:T(8,128)(2,1)S(1)}, bf16[4,2,2,32,512]{4,3,2,1,0:T(8,128)(2,1)S(1)}, u32[]{:S(2)}, u32[]{:S(2)}) collective-permute-start(bf16[4,2,2,32,512]{4,3,2,1,0:T(8,128)(2,1)S(1)} %get-tuple-element.124.refs_3_.refs_7_.refs_11_), channel_id=1, source_target_pairs={{0,6},{2,4},{4,2},{6,0},{1,7},{3,5},{5,3},{7,1},{8,14},{10,12},{12... | collective-permute-start | bytes 1572872 | tf_op jit(solution)/shard_map/ppermute | solution.py:25
  130.1 36.5 %collective-permute-start.32 = (bf16[544,512]{1,0:T(8,128)(2,1)S(1)}, bf16[544,512]{1,0:T(8,128)(2,1)S(1)}, u32[]{:S(2)}, u32[]{:S(2)}) collective-permute-start(bf16[544,512]{1,0:T(8,128)(2,1)S(1)} %get-tuple-element.131.refs_0_), channel_id=1, source_target_pairs={{0,32},{32,0},{64,96},{96,64},{1,33},{33,1},{65,97},{97,65},{2,34}... | collective-permute-start | bytes 1671176 | tf_op jit(solution)/shard_map/ppermute | solution.py:25
  135.5 15.7 %collective-permute-start.33 = (bf16[544,512]{1,0:T(8,128)(2,1)S(1)}, bf16[544,512]{1,0:T(8,128)(2,1)S(1)}, u32[]{:S(2)}, u32[]{:S(2)}) collective-permute-start(bf16[544,512]{1,0:T(8,128)(2,1)S(1)} %get-tuple-element.131.refs_0_), channel_id=1, source_target_pairs={{0,64},{32,96},{64,0},{96,32},{1,65},{33,97},{65,1},{97,33},{2,66}... | collective-permute-start | bytes 1671176 | tf_op jit(solution)/shard_map/ppermute | solution.py:25
  148.0 18.4 %collective-permute-start.28 = (bf16[272,512]{1,0:T(8,128)(2,1)S(1)}, bf16[272,512]{1,0:T(8,128)(2,1)S(1)}, u32[]{:S(2)}, u32[]{:S(2)}) collective-permute-start(bf16[272,512]{1,0:T(8,128)(2,1)S(1)} %get-tuple-element.127.refs_0_), channel_id=1, source_target_pairs={{0,64},{32,96},{64,0},{96,32},{1,65},{33,97},{65,1},{97,33},{2,66}... | collective-permute-start | bytes 835592 | tf_op jit(solution)/shard_map/ppermute | solution.py:25
  151.2 15.6 %collective-permute-start.34 = (bf16[544,512]{1,0:T(8,128)(2,1)S(1)}, bf16[544,512]{1,0:T(8,128)(2,1)S(1)}, u32[]{:S(2)}, u32[]{:S(2)}) collective-permute-start(bf16[544,512]{1,0:T(8,128)(2,1)S(1)} %collective-permute-done.33.refs_2_), channel_id=1, source_target_pairs={{0,32},{32,0},{64,96},{96,64},{1,33},{33,1},{65,97},{97,65},{2,34}... | collective-permute-start | bytes 1671176 | tf_op jit(solution)/shard_map/ppermute | solution.py:25
  163.5 9.8 %collective-permute-start.31 = (bf16[272,512]{1,0:T(8,128)(2,1)S(1)}, bf16[272,512]{1,0:T(8,128)(2,1)S(1)}, u32[]{:S(2)}, u32[]{:S(2)}) collective-permute-start(bf16[272,512]{1,0:T(8,128)(2,1)S(1)} %get-tuple-element.130.refs_4_), channel_id=1, source_target_pairs={{0,64},{32,96},{64,0},{96,32},{1,65},{33,97},{65,1},{97,33},{2,66}... | collective-permute-start | bytes 835592 | tf_op jit(solution)/shard_map/ppermute | solution.py:25
  166.1 9.4 %collective-permute-start.27 = (bf16[272,512]{1,0:T(8,128)(2,1)S(1)}, bf16[272,512]{1,0:T(8,128)(2,1)S(1)}, u32[]{:S(2)}, u32[]{:S(2)}) collective-permute-start(bf16[272,512]{1,0:T(8,128)(2,1)S(1)} %get-tuple-element.127.refs_0_), channel_id=1, source_target_pairs={{0,32},{32,0},{64,96},{96,64},{1,33},{33,1},{65,97},{97,65},{2,34}... | collective-permute-start | bytes 835592 | tf_op jit(solution)/shard_map/ppermute | solution.py:25
  166.4 9.1 %collective-permute-start.30 = (bf16[272,512]{1,0:T(8,128)(2,1)S(1)}, bf16[272,512]{1,0:T(8,128)(2,1)S(1)}, u32[]{:S(2)}, u32[]{:S(2)}) collective-permute-start(bf16[272,512]{1,0:T(8,128)(2,1)S(1)} %get-tuple-element.130.refs_4_), channel_id=1, source_target_pairs={{0,32},{32,0},{64,96},{96,64},{1,33},{33,1},{65,97},{97,65},{2,34}... | collective-permute-start | bytes 835592 | tf_op jit(solution)/shard_map/ppermute | solution.py:25
  166.6 8.9 %collective-permute-start.29 = (bf16[272,512]{1,0:T(8,128)(2,1)S(1)}, bf16[272,512]{1,0:T(8,128)(2,1)S(1)}, u32[]{:S(2)}, u32[]{:S(2)}) collective-permute-start(bf16[272,512]{1,0:T(8,128)(2,1)S(1)} %collective-permute-done.28.refs_2_), channel_id=1, source_target_pairs={{0,32},{32,0},{64,96},{96,64},{1,33},{33,1},{65,97},{97,65},{2,34}... | collective-permute-start | bytes 835592 | tf_op jit(solution)/shard_map/ppermute | solution.py:25
  (37 other events, 442.7 us)

commit v4 on v3

--- a/solution.py
+++ b/solution.py
@@ -782,12 +782,13 @@
     slots, groups, breadth = place_memory_matrix.shape[:3]
     tokens = prompts * length
     rows = tokens + slots
-    counts = request_valid_count
-
-    spots = request_destination_place
+    counts, spots, marks = in_hbm(
+        request_valid_count, request_destination_place, place_newness_marks
+    )
+
     parts, own, new_shift = split(
         place,
-        place_newness_marks,
+        marks,
         counts,
         spots,
         [
@@ -854,10 +855,10 @@
     sent = []
     t0 = 0
     new_state = None
-    for t1 in (256, 384, 512):
+    for t1 in (256, 448, 512):
         out = wkv(
             counts,
-            place_newness_marks,
+            marks,
             rkv,
             log_decay,
             gate,
@@ -881,7 +882,7 @@
         sent.append([normed, n_side, n_far, n_far_side])
         t0 = t1
     prompt_hidden, decode_hidden = project_result(
-        place, counts, spots, sent[1] + sent[2], late, (128, 128), 256, result, length, slots
+        place, counts, spots, sent[1] + sent[2], late, (192, 64), 256, result, length, slots
     )
     final_state = out[3]
     new_state = place_states(place, spots, final_state, new_state)

time: 180 us -> 181 us (level)
  starting transfers between devices: 48.9 us -> 54.4 us
  local copies, waits for them, and re-layouts: 4.98 us -> 1.67 us
  waiting for transfers between devices: 18.9 us -> 16.9 us
    ppermute x36, starting transfers between devices: 48.9 us -> 54.4 us  [swap(): return lax.ppermute(a, names, [(i, i ^ bits) for i in range(sizes[axes])])]
    unnamed x66 -> x50, local copies, waits for them, and re-layouts: 4.86 us -> 1.56 us
    ppermute x36, waiting for transfers between devices: 18.9 us -> 16.9 us  [swap(): return lax.ppermute(a, names, [(i, i ^ bits) for i in range(sizes[axes])])]
  transfers between devices with their start and end apart: 36 -> 36, of which waited for: 10 -> 11; matrix products, arithmetic and copies ran while one was open for 1% -> 1% of each run, Pallas kernels for 41% -> 40%
where the time goes in v4:
time: 181 us; the launch traced here: 180 us
  Pallas kernels  104 us (57%)
  starting transfers between devices  54.4 us (30%)
  waiting for transfers between devices  16.9 us (9%)
  other arithmetic  2.14 us (1%)
    ppermute x36, starting transfers between devices, swap(): return lax.ppermute(a, names, [(i, i ^ bits) for i in range(sizes[axes])])  54.4 us
    pallas_call x3, Pallas kernels, wkv(): pl.pallas_call(functools.partial(wkv_kernel, t0=t0, span=span, slot0=c0 *...  38.1 us
    pallas_call x4, Pallas kernels, mix(): pl.pallas_call(functools.partial(mix_kernel, d=d, length=length), out_sha...  24.1 us
    ppermute x36, waiting for transfers between devices, swap(): return lax.ppermute(a, names, [(i, i ^ bits) for i in range(sizes[axes])])  16.9 us
    pallas_call x1, Pallas kernels, project_rkv(): pl.pallas_call(rkv_kernel, out_shape=jax.ShapeDtypeStruct((3, rows, 512),...  13.7 us
    pallas_call x2, Pallas kernels, project_result(): pl.pallas_call(functools.partial(result_kernel, spans=spans, t0=t0, slot0...  8.85 us
    pallas_call x4, Pallas kernels, pack(): pl.pallas_call(functools.partial(pack_kernel, n=n, lot=lot), out_shape=sh...  8.62 us
    pallas_call x1, Pallas kernels, project_gate(): pl.pallas_call(gate_kernel, out_shape=jax.ShapeDtypeStruct((rows, 512), B...  5.97 us
  transfers between devices with their start and end apart: 36, of which 11 were waited for; matrix products, arithmetic and copies ran while one was open for 1% of the time, Pallas kernels for 40%

profile of v4, /device:TPU:1, one launch (start us, length us, event | category | flops | bytes accessed | tf_op | source)
XLA Modules:
  0.0 180.3 jit_solution(5819992969431257109)
XLA Ops:
  0.7 3.0 %split.1 = (bf16[5,16,512]{2,1,0:T(8,128)(2,1)S(1)}, bf16[5,16,512]{2,1,0:T(8,128)(2,1)S(1)}, bf16[5,16,512]{2,1,0:T(8,128)(2,1)S(1)}, bf16[5,16,512]{2,1,0:T(8,...) custom-call(s32[4]{0:T(128)S(1)} %pad_add_fusion.place_ref, s32[64]{0:T(128)} %keep_ref.7, ...), custom_call_target="tpu_custom_call" | custom-call | tf_op jit(solution)/shard_map/split/pallas_call | solution.py:105
  5.2 3.0 %collective-permute-start = (bf16[5,16,512]{2,1,0:T(8,128)(2,1)S(1)}, bf16[5,16,512]{2,1,0:T(8,128)(2,1)S(1)}, u32[]{:S(2)}, u32[]{:S(2)}) collective-permute-start(bf16[5,16,512]{2,1,0:T(8,128)(2,1)S(1)} %get-tuple-element.73), channel_id=1, source_target_pairs={{0,96},{32,64},{64,32},{96,0},{1,97},{33,65},{65,33},{97,1},{2,98}... | collective-permute-start | bytes 245768 | tf_op jit(solution)/shard_map/ppermute | solution.py:25
  8.9 2.0 %collective-permute-done = bf16[5,16,512]{2,1,0:T(8,128)(2,1)S(1)} collective-permute-done((bf16[5,16,512]{2,1,0:T(8,128)(2,1)S(1)}, bf16[5,16,512]{2,1,0:T(8,128)(2,1)S(1)}, u32[]{:S(2)}, u32[]{:S(2)}) %collective-permute-start) | collective-permute-done | bytes 81952 | tf_op jit(solution)/shard_map/ppermute | solution.py:25
  10.9 2.1 %collective-permute-done.4 = bf16[5,16,512]{2,1,0:T(8,128)(2,1)S(1)} collective-permute-done((bf16[5,16,512]{2,1,0:T(8,128)(2,1)S(1)}, bf16[5,16,512]{2,1,0:T(8,128)(2,1)S(1)}, u32[]{:S(2)}, u32[]{:S(2)}) %collective-permute-start.4) | collective-permute-done | bytes 81952 | tf_op jit(solution)/shard_map/ppermute | solution.py:25
  14.2 3.0 %collective-permute-start.1 = (bf16[1152,512]{1,0:T(8,128)(2,1)S(1)}, bf16[1152,512]{1,0:T(8,128)(2,1)S(1)}, u32[]{:S(2)}, u32[]{:S(2)}) collective-permute-start(bf16[1152,512]{1,0:T(8,128)(2,1)S(1)} %get-tuple-element.74.refs_0_), channel_id=1, source_target_pairs={{0,64},{32,96},{64,0},{96,32},{1,65},{33,97},{65,1},{97,33},{2,66}... | collective-permute-start | bytes 3538952 | tf_op jit(solution)/shard_map/ppermute | solution.py:25
  17.2 5.9 %mix.4 = (bf16[5,1088,2048]{2,1,0:T(8,128)(2,1)}, f32[1088,64]{1,0:T(8,128)S(1)}) custom-call(s32[4]{0:T(128)S(1)} %pad_add_fusion.place_ref, s32[2]{0:T(128)} %count_ref.19, bf16[1152,512]{1,0:T(8,128)(2,1)S(1)} %get-tuple-element.74.refs_0_, f32[5,2048]{1,0:T(8,128)} %refs_1_.9, bf16[64,2048]{1,0:T(8,128)(2,1)} %bitcast.24), custom_call_target="tpu_custom_call" | custom-call | flops 11141120 | bytes 6684672 | tf_op jit(solution)/shard_map/mix/pallas_call | solution.py:280
  25.7 1.6 collective-permute-start.8
  27.3 1.8 %collective-permute-start.9 = (bf16[1,1,5,32,512]{4,3,2,1,0:T(8,128)(2,1)S(1)}, bf16[1,1,5,32,512]{4,3,2,1,0:T(8,128)(2,1)S(1)}, u32[]{:S(2)}, u32[]{:S(2)}) collective-permute-start(bf16[1,1,5,32,512]{4,3,2,1,0:T(8,128)(2,1)S(1)} %get-tuple-element.143.refs_2_), channel_id=1, source_target_pairs={{0,6},{2,4},{4,2},{6,0},{1,7},{3,5},{5,3},{7,1},{8,14},{10,12},{12... | collective-permute-start | bytes 491528 | tf_op jit(solution)/shard_map/ppermute | solution.py:25
  29.1 2.2 %collective-permute-start.10 = (bf16[1,1,5,32,512]{4,3,2,1,0:T(8,128)(2,1)S(1)}, bf16[1,1,5,32,512]{4,3,2,1,0:T(8,128)(2,1)S(1)}, u32[]{:S(2)}, u32[]{:S(2)}) collective-permute-start(bf16[1,1,5,32,512]{4,3,2,1,0:T(8,128)(2,1)S(1)} %get-tuple-element.140.refs_3_), channel_id=1, source_target_pairs={{0,24},{8,16},{16,8},{24,0},{1,25},{9,17},{17,9},{25,1},{2,26},{10... | collective-permute-start | bytes 491528 | tf_op jit(solution)/shard_map/ppermute | solution.py:25
  33.0 1.8 %collective-permute-done.10.refs_7_ = bf16[1,1,5,32,512]{4,3,2,1,0:T(8,128)(2,1)S(1)} collective-permute-done((bf16[1,1,5,32,512]{4,3,2,1,0:T(8,128)(2,1)S(1)}, bf16[1,1,5,32,512]{4,3,2,1,0:T(8,128)(2,1)S(1)}, u32[]{:S(2)}, u32[]{:S(2)}) %collective-permute-start.10) | collective-permute-done | bytes 163872 | tf_op jit(solution)/shard_map/ppermute | solution.py:25
  34.8 2.4 %pack.4 = (bf16[1,2,5,32,512]{4,3,2,1,0:T(8,128)(2,1)S(1)}, bf16[2,1,5,32,512]{4,3,2,1,0:T(8,128)(2,1)S(1)}, bf16[1,2,5,32,512]{4,3,2,1,0:T(8,128)(2,1)S(1)}, bf16[2,1,5,32,512]{4,3,2,1,0:T(8,128)(2,1)S(1)}) custom-call(s32[4]{0:T(128)S(1)} %pad_add_fusion.place_ref, bf16[1,1,5,32,512]{4,3,2,1,0:T(8,128)(2,1)S(1)} %get-tuple-element.141.refs_0_, ...), custom_call_target="tpu_custom_call" | custom-call | bytes 8388608 | tf_op jit(solution)/shard_map/pack/pallas_call | solution.py:179
  38.4 2.4 %collective-permute-start.13 = (bf16[1,2,5,32,512]{4,3,2,1,0:T(8,128)(2,1)S(1)}, bf16[1,2,5,32,512]{4,3,2,1,0:T(8,128)(2,1)S(1)}, u32[]{:S(2)}, u32[]{:S(2)}) collective-permute-start(bf16[1,2,5,32,512]{4,3,2,1,0:T(8,128)(2,1)S(1)} %get-tuple-element.90.refs_2_), channel_id=1, source_target_pairs={{0,24},{8,16},{16,8},{24,0},{1,25},{9,17},{17,9},{25,1},{2,26},{10... | collective-permute-start | bytes 983048 | tf_op jit(solution)/shard_map/ppermute | solution.py:25
  40.8 5.8 %mix.5 = (bf16[5,1088,2048]{2,1,0:T(8,128)(2,1)}, f32[1088,64]{1,0:T(8,128)S(1)}) custom-call(s32[4]{0:T(128)S(1)} %pad_add_fusion.place_ref, s32[2]{0:T(128)} %count_ref.19, bf16[1152,512]{1,0:T(8,128)(2,1)S(1)} %collective-permute-done.6.refs_0_, f32[5,2048]{1,0:T(8,128)} %refs_1_.9, bf16[64,2048]{1,0:T(8,128)(2,1)} %bitcast.25, ...), custom_call_target="tpu_custom_call", output_to_operand_aliasing={{0}: (6, {})} | custom-call | flops 11141120 | bytes 6684672 | tf_op jit(solution)/shard_map/mix/pallas_call | solution.py:280
  51.3 7.4 %collective-permute-start.2 = (bf16[1152,512]{1,0:T(8,128)(2,1)S(1)}, bf16[1152,512]{1,0:T(8,128)(2,1)S(1)}, u32[]{:S(2)}, u32[]{:S(2)}) collective-permute-start(bf16[1152,512]{1,0:T(8,128)(2,1)S(1)} %collective-permute-done.1.refs_0_), channel_id=1, source_target_pairs={{0,32},{32,0},{64,96},{96,64},{1,33},{33,1},{65,97},{97,65},{2,34}... | collective-permute-start | bytes 3538952 | tf_op jit(solution)/shard_map/ppermute | solution.py:25
  58.6 5.8 %mix.6 = (bf16[5,1088,2048]{2,1,0:T(8,128)(2,1)}, f32[1088,64]{1,0:T(8,128)S(1)}) custom-call(s32[4]{0:T(128)S(1)} %pad_add_fusion.place_ref, s32[2]{0:T(128)} %count_ref.19, bf16[1152,512]{1,0:T(8,128)(2,1)S(1)} %collective-permute-done.1.refs_0_, f32[5,2048]{1,0:T(8,128)} %refs_1_.9, bf16[64,2048]{1,0:T(8,128)(2,1)} %bitcast.26, ...), custom_call_target="tpu_custom_call", output_to_operand_aliasing={{0}: (6, {})} | custom-call | flops 11141120 | bytes 6684672 | tf_op jit(solution)/shard_map/mix/pallas_call | solution.py:280
  66.0 2.6 %pack.6 = (bf16[2,4,3,32,512]{4,3,2,1,0:T(8,128)(2,1)S(1)}, bf16[4,2,3,32,512]{4,3,2,1,0:T(8,128)(2,1)S(1)}, bf16[2,4,3,32,512]{4,3,2,1,0:T(8,128)(2,1)S(1)}, bf16[4,2,3,32,512]{4,3,2,1,0:T(8,128)(2,1)S(1)}) custom-call(s32[4]{0:T(128)S(1)} %pad_add_fusion.place_ref, bf16[2,2,5,32,512]{4,3,2,1,0:T(8,128)(2,1)} %copy-done.8, ...), custom_call_target="tpu_custom_call" | custom-call | bytes 8388608 | tf_op jit(solution)/shard_map/pack/pallas_call | solution.py:179
  68.6 2.4 %collective-permute-start.19 = (bf16[2,4,3,32,512]{4,3,2,1,0:T(8,128)(2,1)S(1)}, bf16[2,4,3,32,512]{4,3,2,1,0:T(8,128)(2,1)S(1)}, u32[]{:S(2)}, u32[]{:S(2)}) collective-permute-start(bf16[2,4,3,32,512]{4,3,2,1,0:T(8,128)(2,1)S(1)} %get-tuple-element.104.refs_0_), channel_id=1, source_target_pairs={{0,24},{8,16},{16,8},{24,0},{1,25},{9,17},{17,9},{25,1},{2,26},{10... | collective-permute-start | bytes 2359304 | tf_op jit(solution)/shard_map/ppermute | solution.py:25
  71.1 1.7 collective-permute-start.20
  73.9 6.6 %mix.7 = (bf16[5,1088,2048]{2,1,0:T(8,128)(2,1)}, f32[1088,512]{1,0:T(8,128)S(1)}) custom-call(s32[4]{0:T(128)S(1)} %pad_add_fusion.place_ref, s32[2]{0:T(128)} %count_ref.19, bf16[1152,512]{1,0:T(8,128)(2,1)S(1)} %collective-permute-done.2.refs_0_, f32[5,2048]{1,0:T(8,128)} %refs_1_.9, bf16[64,2048]{1,0:T(8,128)(2,1)} %bitcast.27, ...), custom_call_target="tpu_custom_call", output_to_operand_aliasing={{0}: (6, {})} | custom-call | flops 11141120 | bytes 6684672 | tf_op jit(solution)/shard_map/mix/pallas_call | solution.py:280
  80.5 2.3 %pack.7 = (bf16[2,4,2,32,512]{4,3,2,1,0:T(8,128)(2,1)S(1)}, bf16[4,2,2,32,512]{4,3,2,1,0:T(8,128)(2,1)S(1)}, bf16[2,4,2,32,512]{4,3,2,1,0:T(8,128)(2,1)S(1)}, bf16[4,2,2,32,512]{4,3,2,1,0:T(8,128)(2,1)S(1)}) custom-call(s32[4]{0:T(128)S(1)} %pad_add_fusion.place_ref, bf16[2,2,5,32,512]{4,3,2,1,0:T(8,128)(2,1)} %copy-done.8, ...), custom_call_target="tpu_custom_call" | custom-call | bytes 8388608 | tf_op jit(solution)/shard_map/pack/pallas_call | solution.py:179
  82.8 2.2 %collective-permute-done.19.refs_4_ = bf16[2,4,3,32,512]{4,3,2,1,0:T(8,128)(2,1)S(1)} collective-permute-done((bf16[2,4,3,32,512]{4,3,2,1,0:T(8,128)(2,1)S(1)}, bf16[2,4,3,32,512]{4,3,2,1,0:T(8,128)(2,1)S(1)}, u32[]{:S(2)}, u32[]{:S(2)}) %collective-permute-start.19) | collective-permute-done | bytes 786464 | tf_op jit(solution)/shard_map/ppermute | solution.py:25
  85.0 2.3 %collective-permute-done.20.refs_5_ = bf16[4,2,3,32,512]{4,3,2,1,0:T(8,128)(2,1)S(1)} collective-permute-done((bf16[4,2,3,32,512]{4,3,2,1,0:T(8,128)(2,1)S(1)}, bf16[4,2,3,32,512]{4,3,2,1,0:T(8,128)(2,1)S(1)}, u32[]{:S(2)}, u32[]{:S(2)}) %collective-permute-start.20) | collective-permute-done | bytes 786464 | tf_op jit(solution)/shard_map/ppermute | solution.py:25
  91.5 13.7 %project_rkv.1.refs_0_.refs_1_.refs_2_.refs_5_.refs_6_.refs_7_.refs_13_.refs_14_.refs_15_ = bf16[3,1088,512]{2,1,0:T(8,128)(2,1)} custom-call(s32[4]{0:T(128)S(1)} %pad_add_fusion.place_ref, bf16[5,1088,2048]{2,1,0:T(8,128)(2,1)} %get-tuple-element.86.x_ref, bf16[2,4,3,32,512]{4,3,2,1,0:T(8,128)(2,1)S(1)} %get-tuple-element.104.refs_0_, ...), custom_call_target="tpu_custom_call" | custom-call | flops 6845104128 | bytes 25165824 | tf_op jit(solution)/shard_map/project_rkv/pallas_call | solution.py:327
  105.3 6.0 %project_gate.1.refs_4_.refs_9_.refs_17_ = bf16[1088,512]{1,0:T(8,128)(2,1)S(1)} custom-call(s32[4]{0:T(128)S(1)} %pad_add_fusion.place_ref, bf16[5,1088,2048]{2,1,0:T(8,128)(2,1)} %get-tuple-element.86.x_ref, bf16[2,4,2,32,512]{4,3,2,1,0:T(8,128)(2,1)S(1)} %get-tuple-element.121.refs_0_.refs_4_.refs_8_, ...), custom_call_target="tpu_custom_call" | custom-call | flops 2281701376 | bytes 8388608 | tf_op jit(solution)/shard_map/project_gate/pallas_call | solution.py:361
  111.4 17.5 %wkv.3 = (bf16[544,512]{1,0:T(8,128)(2,1)S(1)}, f32[2,4,128,128]{3,2,1,0:T(8,128)S(1)}, f32[64,8,64,64]{3,2,1,0:T(8,128)}) custom-call(s32[2]{0:T(128)} %count_ref.19, s32[64]{0:T(128)} %keep_ref.7, bf16[456,128]{1,0:T(8,128)(2,1)S(1)} %copy-done.12, ...), custom_call_target="tpu_custom_call" | custom-call | flops 20480000000 | bytes 33554432 | tf_op jit(solution)/shard_map/wkv/pallas_call | solution.py:727
  129.0 2.1 %collective-permute-start.33 = (bf16[544,512]{1,0:T(8,128)(2,1)S(1)}, bf16[544,512]{1,0:T(8,128)(2,1)S(1)}, u32[]{:S(2)}, u32[]{:S(2)}) collective-permute-start(bf16[544,512]{1,0:T(8,128)(2,1)S(1)} %get-tuple-element.131.refs_0_), channel_id=1, source_target_pairs={{0,64},{32,96},{64,0},{96,32},{1,65},{33,97},{65,1},{97,33},{2,66}... | collective-permute-start | bytes 1671176 | tf_op jit(solution)/shard_map/ppermute | solution.py:25
  131.0 13.9 %wkv.4 = (bf16[408,512]{1,0:T(8,128)(2,1)S(1)}, f32[2,4,128,128]{3,2,1,0:T(8,128)S(1)}, f32[64,8,64,64]{3,2,1,0:T(8,128)}) custom-call(s32[2]{0:T(128)} %count_ref.19, s32[64]{0:T(128)} %keep_ref.7, bf16[456,128]{1,0:T(8,128)(2,1)S(1)} %copy-done.12, ...), custom_call_target="tpu_custom_call", output_to_operand_aliasing={{2}: (21, {})} | custom-call | flops 15360000000 | bytes 25165824 | tf_op jit(solution)/shard_map/wkv/pallas_call | solution.py:727
  145.9 5.5 %collective-permute-start.32 = (bf16[544,512]{1,0:T(8,128)(2,1)S(1)}, bf16[544,512]{1,0:T(8,128)(2,1)S(1)}, u32[]{:S(2)}, u32[]{:S(2)}) collective-permute-start(bf16[544,512]{1,0:T(8,128)(2,1)S(1)} %get-tuple-element.131.refs_0_), channel_id=1, source_target_pairs={{0,32},{32,0},{64,96},{96,64},{1,33},{33,1},{65,97},{97,65},{2,34}... | collective-permute-start | bytes 1671176 | tf_op jit(solution)/shard_map/ppermute | solution.py:25
  153.3 6.5 %collective-permute-start.29 = (bf16[408,512]{1,0:T(8,128)(2,1)S(1)}, bf16[408,512]{1,0:T(8,128)(2,1)S(1)}, u32[]{:S(2)}, u32[]{:S(2)}) collective-permute-start(bf16[408,512]{1,0:T(8,128)(2,1)S(1)} %collective-permute-done.28.refs_2_), channel_id=1, source_target_pairs={{0,32},{32,0},{64,96},{96,64},{1,33},{33,1},{65,97},{97,65},{2,34}... | collective-permute-start | bytes 1253384 | tf_op jit(solution)/shard_map/ppermute | solution.py:25
  159.8 6.7 %wkv.5 = (bf16[136,512]{1,0:T(8,128)(2,1)S(1)}, f32[2,4,128,128]{3,2,1,0:T(8,128)}, f32[64,8,64,64]{3,2,1,0:T(8,128)}, f32[2,8,64,64]{3,2,1,0:T(8,128)S(1)}) custom-call(s32[2]{0:T(128)} %count_ref.19, s32[64]{0:T(128)} %keep_ref.7, bf16[456,128]{1,0:T(8,128)(2,1)S(1)} %copy-done.12, ...), custom_call_target="tpu_custom_call", output_to_operand_aliasing={{2}: (21, {})} | custom-call | flops 5120000000 | bytes 8388608 | tf_op jit(solution)/shard_map/wkv/pallas_call | solution.py:727
  167.6 4.4 %project_result.2 = (bf16[2,512,512]{2,1,0:T(8,128)(2,1)}, bf16[64,512]{1,0:T(8,128)(2,1)}) custom-call(s32[4]{0:T(128)S(1)} %pad_add_fusion.place_ref, s32[2]{0:T(128)} %count_ref.19, s32[2]{0:T(128)} %spot_ref.7, bf16[544,512]{1,0:T(8,128)(2,1)S(1)} %get-tuple-element.131.refs_0_, bf16[544,512]{1,0:T(8,128)(2,1)S(1)} %collective-permute-done.32.refs_1_, ...), custom_call_target="tpu_custom_call" | custom-call | flops 1073741824 | bytes 8388608 | tf_op jit(solution)/shard_map/project_result/pallas_call | solution.py:412
  175.6 4.4 %project_result.3 = (bf16[2,512,512]{2,1,0:T(8,128)(2,1)}, bf16[64,512]{1,0:T(8,128)(2,1)}) custom-call(s32[4]{0:T(128)S(1)} %pad_add_fusion.place_ref, s32[2]{0:T(128)} %count_ref.19, s32[2]{0:T(128)} %spot_ref.7, bf16[408,512]{1,0:T(8,128)(2,1)S(1)} %get-tuple-element.127.refs_0_, ...), custom_call_target="tpu_custom_call", output_to_operand_aliasing={{0}: (19, {}), {1}: (20, {})} | custom-call | flops 1073741824 | bytes 8388608 | tf_op jit(solution)/shard_map/project_result/pallas_call | solution.py:412
  (115 shorter events, 27.8 us)
Async XLA Ops:
  3.7 19.4 %collective-permute-start.6 = (bf16[1152,512]{1,0:T(8,128)(2,1)S(1)}, bf16[1152,512]{1,0:T(8,128)(2,1)S(1)}, u32[]{:S(2)}, u32[]{:S(2)}) collective-permute-start(bf16[1152,512]{1,0:T(8,128)(2,1)S(1)} %get-tuple-element.74.refs_0_), channel_id=1, source_target_pairs={{0,32},{32,0},{64,96},{96,64},{1,33},{33,1},{65,97},{97,65},{2,34}... | collective-permute-start | bytes 3538952 | tf_op jit(solution)/shard_map/ppermute | solution.py:25
  5.2 5.7 %collective-permute-start = (bf16[5,16,512]{2,1,0:T(8,128)(2,1)S(1)}, bf16[5,16,512]{2,1,0:T(8,128)(2,1)S(1)}, u32[]{:S(2)}, u32[]{:S(2)}) collective-permute-start(bf16[5,16,512]{2,1,0:T(8,128)(2,1)S(1)} %get-tuple-element.73), channel_id=1, source_target_pairs={{0,96},{32,64},{64,32},{96,0},{1,97},{33,65},{65,33},{97,1},{2,98}... | collective-permute-start | bytes 245768 | tf_op jit(solution)/shard_map/ppermute | solution.py:25
  13.8 9.3 %collective-permute-start.5 = (bf16[4,5,16,512]{3,2,1,0:T(8,128)(2,1)}, bf16[4,5,16,512]{3,2,1,0:T(8,128)(2,1)}, u32[]{:S(2)}, u32[]{:S(2)}) collective-permute-start(bf16[4,5,16,512]{3,2,1,0:T(8,128)(2,1)} %pad_maximum_fusion), channel_id=1, source_target_pairs={{0,1},{1,0},{2,3},{3,2},{4,5},{5,4},{6,7},{7,6},{8,9},{9,8},{10,11... | collective-permute-start | bytes 983048 | tf_op jit(solution)/shard_map/ppermute | solution.py:25
  14.2 37.1 %collective-permute-start.1 = (bf16[1152,512]{1,0:T(8,128)(2,1)S(1)}, bf16[1152,512]{1,0:T(8,128)(2,1)S(1)}, u32[]{:S(2)}, u32[]{:S(2)}) collective-permute-start(bf16[1152,512]{1,0:T(8,128)(2,1)S(1)} %get-tuple-element.74.refs_0_), channel_id=1, source_target_pairs={{0,64},{32,96},{64,0},{96,32},{1,65},{33,97},{65,1},{97,33},{2,66}... | collective-permute-start | bytes 3538952 | tf_op jit(solution)/shard_map/ppermute | solution.py:25
  24.4 7.0 %collective-permute-start.7 = (bf16[1,1,5,32,512]{4,3,2,1,0:T(8,128)(2,1)S(1)}, bf16[1,1,5,32,512]{4,3,2,1,0:T(8,128)(2,1)S(1)}, u32[]{:S(2)}, u32[]{:S(2)}) collective-permute-start(bf16[1,1,5,32,512]{4,3,2,1,0:T(8,128)(2,1)S(1)} %get-tuple-element.141.refs_0_), channel_id=1, source_target_pairs={{0,2},{2,0},{4,6},{6,4},{1,3},{3,1},{5,7},{7,5},{8,10},{10,8},{12,... | collective-permute-start | bytes 491528 | tf_op jit(solution)/shard_map/ppermute | solution.py:25
  25.7 5.7 %collective-permute-start.8 = (bf16[1,1,5,32,512]{4,3,2,1,0:T(8,128)(2,1)S(1)}, bf16[1,1,5,32,512]{4,3,2,1,0:T(8,128)(2,1)S(1)}, u32[]{:S(2)}, u32[]{:S(2)}) collective-permute-start(bf16[1,1,5,32,512]{4,3,2,1,0:T(8,128)(2,1)S(1)} %get-tuple-element.142.refs_1_), channel_id=1, source_target_pairs={{0,8},{8,0},{16,24},{24,16},{1,9},{9,1},{17,25},{25,17},{2,10},{10... | collective-permute-start | bytes 491528 | tf_op jit(solution)/shard_map/ppermute | solution.py:25
  27.3 5.7 %collective-permute-start.9 = (bf16[1,1,5,32,512]{4,3,2,1,0:T(8,128)(2,1)S(1)}, bf16[1,1,5,32,512]{4,3,2,1,0:T(8,128)(2,1)S(1)}, u32[]{:S(2)}, u32[]{:S(2)}) collective-permute-start(bf16[1,1,5,32,512]{4,3,2,1,0:T(8,128)(2,1)S(1)} %get-tuple-element.143.refs_2_), channel_id=1, source_target_pairs={{0,6},{2,4},{4,2},{6,0},{1,7},{3,5},{5,3},{7,1},{8,14},{10,12},{12... | collective-permute-start | bytes 491528 | tf_op jit(solution)/shard_map/ppermute | solution.py:25
  37.2 9.5 %collective-permute-start.11 = (bf16[1,2,5,32,512]{4,3,2,1,0:T(8,128)(2,1)S(1)}, bf16[1,2,5,32,512]{4,3,2,1,0:T(8,128)(2,1)S(1)}, u32[]{:S(2)}, u32[]{:S(2)}) collective-permute-start(bf16[1,2,5,32,512]{4,3,2,1,0:T(8,128)(2,1)S(1)} %get-tuple-element.88.refs_0_), channel_id=1, source_target_pairs={{0,8},{8,0},{16,24},{24,16},{1,9},{9,1},{17,25},{25,17},{2,10},{10... | collective-permute-start | bytes 983048 | tf_op jit(solution)/shard_map/ppermute | solution.py:25
  37.6 9.1 %collective-permute-start.12 = (bf16[2,1,5,32,512]{4,3,2,1,0:T(8,128)(2,1)S(1)}, bf16[2,1,5,32,512]{4,3,2,1,0:T(8,128)(2,1)S(1)}, u32[]{:S(2)}, u32[]{:S(2)}) collective-permute-start(bf16[2,1,5,32,512]{4,3,2,1,0:T(8,128)(2,1)S(1)} %get-tuple-element.89.refs_1_), channel_id=1, source_target_pairs={{0,6},{2,4},{4,2},{6,0},{1,7},{3,5},{5,3},{7,1},{8,14},{10,12},{12... | collective-permute-start | bytes 983048 | tf_op jit(solution)/shard_map/ppermute | solution.py:25
  38.4 8.3 %collective-permute-start.13 = (bf16[1,2,5,32,512]{4,3,2,1,0:T(8,128)(2,1)S(1)}, bf16[1,2,5,32,512]{4,3,2,1,0:T(8,128)(2,1)S(1)}, u32[]{:S(2)}, u32[]{:S(2)}) collective-permute-start(bf16[1,2,5,32,512]{4,3,2,1,0:T(8,128)(2,1)S(1)} %get-tuple-element.90.refs_2_), channel_id=1, source_target_pairs={{0,24},{8,16},{16,8},{24,0},{1,25},{9,17},{17,9},{25,1},{2,26},{10... | collective-permute-start | bytes 983048 | tf_op jit(solution)/shard_map/ppermute | solution.py:25
  40.8 6.2 %collective-permute-start.14 = (bf16[2,1,5,32,512]{4,3,2,1,0:T(8,128)(2,1)S(1)}, bf16[2,1,5,32,512]{4,3,2,1,0:T(8,128)(2,1)S(1)}, u32[]{:S(2)}, u32[]{:S(2)}) collective-permute-start(bf16[2,1,5,32,512]{4,3,2,1,0:T(8,128)(2,1)S(1)} %get-tuple-element.91.refs_3_), channel_id=1, source_target_pairs={{0,2},{2,0},{4,6},{6,4},{1,3},{3,1},{5,7},{7,5},{8,10},{10,8},{12,... | collective-permute-start | bytes 983048 | tf_op jit(solution)/shard_map/ppermute | solution.py:25
  48.5 16.0 %collective-permute-start.15 = (bf16[2,2,5,32,512]{4,3,2,1,0:T(8,128)(2,1)S(1)}, bf16[2,2,5,32,512]{4,3,2,1,0:T(8,128)(2,1)S(1)}, u32[]{:S(2)}, u32[]{:S(2)}) collective-permute-start(bf16[2,2,5,32,512]{4,3,2,1,0:T(8,128)(2,1)S(1)} %get-tuple-element.96.refs_0_), channel_id=1, source_target_pairs={{0,6},{2,4},{4,2},{6,0},{1,7},{3,5},{5,3},{7,1},{8,14},{10,12},{12... | collective-permute-start | bytes 1966088 | tf_op jit(solution)/shard_map/ppermute | solution.py:25
  50.0 14.5 %collective-permute-start.16 = (bf16[2,2,5,32,512]{4,3,2,1,0:T(8,128)(2,1)S(1)}, bf16[2,2,5,32,512]{4,3,2,1,0:T(8,128)(2,1)S(1)}, u32[]{:S(2)}, u32[]{:S(2)}) collective-permute-start(bf16[2,2,5,32,512]{4,3,2,1,0:T(8,128)(2,1)S(1)} %get-tuple-element.97.refs_1_), channel_id=1, source_target_pairs={{0,24},{8,16},{16,8},{24,0},{1,25},{9,17},{17,9},{25,1},{2,26},{10... | collective-permute-start | bytes 1966088 | tf_op jit(solution)/shard_map/ppermute | solution.py:25
  51.2 13.3 %collective-permute-start.17 = (bf16[2,2,5,32,512]{4,3,2,1,0:T(8,128)(2,1)S(1)}, bf16[2,2,5,32,512]{4,3,2,1,0:T(8,128)(2,1)S(1)}, u32[]{:S(2)}, u32[]{:S(2)}) collective-permute-start(bf16[2,2,5,32,512]{4,3,2,1,0:T(8,128)(2,1)S(1)} %get-tuple-element.98.refs_2_), channel_id=1, source_target_pairs={{0,2},{2,0},{4,6},{6,4},{1,3},{3,1},{5,7},{7,5},{8,10},{10,8},{12,... | collective-permute-start | bytes 1966088 | tf_op jit(solution)/shard_map/ppermute | solution.py:25
  51.2 13.3 %collective-permute-start.18 = (bf16[2,2,5,32,512]{4,3,2,1,0:T(8,128)(2,1)S(1)}, bf16[2,2,5,32,512]{4,3,2,1,0:T(8,128)(2,1)S(1)}, u32[]{:S(2)}, u32[]{:S(2)}) collective-permute-start(bf16[2,2,5,32,512]{4,3,2,1,0:T(8,128)(2,1)S(1)} %get-tuple-element.99.refs_3_), channel_id=1, source_target_pairs={{0,8},{8,0},{16,24},{24,16},{1,9},{9,1},{17,25},{25,17},{2,10},{10... | collective-permute-start | bytes 1966088 | tf_op jit(solution)/shard_map/ppermute | solution.py:25
  51.3 22.7 %collective-permute-start.2 = (bf16[1152,512]{1,0:T(8,128)(2,1)S(1)}, bf16[1152,512]{1,0:T(8,128)(2,1)S(1)}, u32[]{:S(2)}, u32[]{:S(2)}) collective-permute-start(bf16[1152,512]{1,0:T(8,128)(2,1)S(1)} %collective-permute-done.1.refs_0_), channel_id=1, source_target_pairs={{0,32},{32,0},{64,96},{96,64},{1,33},{33,1},{65,97},{97,65},{2,34}... | collective-permute-start | bytes 3538952 | tf_op jit(solution)/shard_map/ppermute | solution.py:25
  68.6 16.3 %collective-permute-start.19 = (bf16[2,4,3,32,512]{4,3,2,1,0:T(8,128)(2,1)S(1)}, bf16[2,4,3,32,512]{4,3,2,1,0:T(8,128)(2,1)S(1)}, u32[]{:S(2)}, u32[]{:S(2)}) collective-permute-start(bf16[2,4,3,32,512]{4,3,2,1,0:T(8,128)(2,1)S(1)} %get-tuple-element.104.refs_0_), channel_id=1, source_target_pairs={{0,24},{8,16},{16,8},{24,0},{1,25},{9,17},{17,9},{25,1},{2,26},{10... | collective-permute-start | bytes 2359304 | tf_op jit(solution)/shard_map/ppermute | solution.py:25
  71.1 16.2 %collective-permute-start.20 = (bf16[4,2,3,32,512]{4,3,2,1,0:T(8,128)(2,1)S(1)}, bf16[4,2,3,32,512]{4,3,2,1,0:T(8,128)(2,1)S(1)}, u32[]{:S(2)}, u32[]{:S(2)}) collective-permute-start(bf16[4,2,3,32,512]{4,3,2,1,0:T(8,128)(2,1)S(1)} %get-tuple-element.105.refs_1_), channel_id=1, source_target_pairs={{0,2},{2,0},{4,6},{6,4},{1,3},{3,1},{5,7},{7,5},{8,10},{10,8},{12,... | collective-permute-start | bytes 2359304 | tf_op jit(solution)/shard_map/ppermute | solution.py:25
  72.8 15.6 %collective-permute-start.21 = (bf16[2,4,3,32,512]{4,3,2,1,0:T(8,128)(2,1)S(1)}, bf16[2,4,3,32,512]{4,3,2,1,0:T(8,128)(2,1)S(1)}, u32[]{:S(2)}, u32[]{:S(2)}) collective-permute-start(bf16[2,4,3,32,512]{4,3,2,1,0:T(8,128)(2,1)S(1)} %get-tuple-element.106.refs_2_), channel_id=1, source_target_pairs={{0,8},{8,0},{16,24},{24,16},{1,9},{9,1},{17,25},{25,17},{2,10},{10... | collective-permute-start | bytes 2359304 | tf_op jit(solution)/shard_map/ppermute | solution.py:25
  72.8 16.3 %collective-permute-start.22 = (bf16[4,2,3,32,512]{4,3,2,1,0:T(8,128)(2,1)S(1)}, bf16[4,2,3,32,512]{4,3,2,1,0:T(8,128)(2,1)S(1)}, u32[]{:S(2)}, u32[]{:S(2)}) collective-permute-start(bf16[4,2,3,32,512]{4,3,2,1,0:T(8,128)(2,1)S(1)} %get-tuple-element.107.refs_3_), channel_id=1, source_target_pairs={{0,6},{2,4},{4,2},{6,0},{1,7},{3,5},{5,3},{7,1},{8,14},{10,12},{12... | collective-permute-start | bytes 2359304 | tf_op jit(solution)/shard_map/ppermute | solution.py:25
  89.1 16.2 %collective-permute-start.23 = (bf16[2,4,2,32,512]{4,3,2,1,0:T(8,128)(2,1)S(1)}, bf16[2,4,2,32,512]{4,3,2,1,0:T(8,128)(2,1)S(1)}, u32[]{:S(2)}, u32[]{:S(2)}) collective-permute-start(bf16[2,4,2,32,512]{4,3,2,1,0:T(8,128)(2,1)S(1)} %get-tuple-element.121.refs_0_.refs_4_.refs_8_), channel_id=1, source_target_pairs={{0,24},{8,16},{16,8},{24,0},{1,25},{9,17},{17,9},{25,1},{2,26},{10... | collective-permute-start | bytes 1572872 | tf_op jit(solution)/shard_map/ppermute | solution.py:25
  90.6 14.7 %collective-permute-start.24 = (bf16[4,2,2,32,512]{4,3,2,1,0:T(8,128)(2,1)S(1)}, bf16[4,2,2,32,512]{4,3,2,1,0:T(8,128)(2,1)S(1)}, u32[]{:S(2)}, u32[]{:S(2)}) collective-permute-start(bf16[4,2,2,32,512]{4,3,2,1,0:T(8,128)(2,1)S(1)} %get-tuple-element.122.refs_1_.refs_5_.refs_9_), channel_id=1, source_target_pairs={{0,2},{2,0},{4,6},{6,4},{1,3},{3,1},{5,7},{7,5},{8,10},{10,8},{12,... | collective-permute-start | bytes 1572872 | tf_op jit(solution)/shard_map/ppermute | solution.py:25
  90.6 14.7 %collective-permute-start.25 = (bf16[2,4,2,32,512]{4,3,2,1,0:T(8,128)(2,1)S(1)}, bf16[2,4,2,32,512]{4,3,2,1,0:T(8,128)(2,1)S(1)}, u32[]{:S(2)}, u32[]{:S(2)}) collective-permute-start(bf16[2,4,2,32,512]{4,3,2,1,0:T(8,128)(2,1)S(1)} %get-tuple-element.123.refs_2_.refs_6_.refs_10_), channel_id=1, source_target_pairs={{0,8},{8,0},{16,24},{24,16},{1,9},{9,1},{17,25},{25,17},{2,10},{10... | collective-permute-start | bytes 1572872 | tf_op jit(solution)/shard_map/ppermute | solution.py:25
  90.9 14.4 %collective-permute-start.26 = (bf16[4,2,2,32,512]{4,3,2,1,0:T(8,128)(2,1)S(1)}, bf16[4,2,2,32,512]{4,3,2,1,0:T(8,128)(2,1)S(1)}, u32[]{:S(2)}, u32[]{:S(2)}) collective-permute-start(bf16[4,2,2,32,512]{4,3,2,1,0:T(8,128)(2,1)S(1)} %get-tuple-element.124.refs_3_.refs_7_.refs_11_), channel_id=1, source_target_pairs={{0,6},{2,4},{4,2},{6,0},{1,7},{3,5},{5,3},{7,1},{8,14},{10,12},{12... | collective-permute-start | bytes 1572872 | tf_op jit(solution)/shard_map/ppermute | solution.py:25
  129.0 22.5 %collective-permute-start.33 = (bf16[544,512]{1,0:T(8,128)(2,1)S(1)}, bf16[544,512]{1,0:T(8,128)(2,1)S(1)}, u32[]{:S(2)}, u32[]{:S(2)}) collective-permute-start(bf16[544,512]{1,0:T(8,128)(2,1)S(1)} %get-tuple-element.131.refs_0_), channel_id=1, source_target_pairs={{0,64},{32,96},{64,0},{96,32},{1,65},{33,97},{65,1},{97,33},{2,66}... | collective-permute-start | bytes 1671176 | tf_op jit(solution)/shard_map/ppermute | solution.py:25
  144.9 8.4 %collective-permute-start.28 = (bf16[408,512]{1,0:T(8,128)(2,1)S(1)}, bf16[408,512]{1,0:T(8,128)(2,1)S(1)}, u32[]{:S(2)}, u32[]{:S(2)}) collective-permute-start(bf16[408,512]{1,0:T(8,128)(2,1)S(1)} %get-tuple-element.127.refs_0_), channel_id=1, source_target_pairs={{0,64},{32,96},{64,0},{96,32},{1,65},{33,97},{65,1},{97,33},{2,66}... | collective-permute-start | bytes 1253384 | tf_op jit(solution)/shard_map/ppermute | solution.py:25
  145.9 21.4 %collective-permute-start.32 = (bf16[544,512]{1,0:T(8,128)(2,1)S(1)}, bf16[544,512]{1,0:T(8,128)(2,1)S(1)}, u32[]{:S(2)}, u32[]{:S(2)}) collective-permute-start(bf16[544,512]{1,0:T(8,128)(2,1)S(1)} %get-tuple-element.131.refs_0_), channel_id=1, source_target_pairs={{0,32},{32,0},{64,96},{96,64},{1,33},{33,1},{65,97},{97,65},{2,34}... | collective-permute-start | bytes 1671176 | tf_op jit(solution)/shard_map/ppermute | solution.py:25
  151.4 16.2 %collective-permute-start.34 = (bf16[544,512]{1,0:T(8,128)(2,1)S(1)}, bf16[544,512]{1,0:T(8,128)(2,1)S(1)}, u32[]{:S(2)}, u32[]{:S(2)}) collective-permute-start(bf16[544,512]{1,0:T(8,128)(2,1)S(1)} %collective-permute-done.33.refs_2_), channel_id=1, source_target_pairs={{0,32},{32,0},{64,96},{96,64},{1,33},{33,1},{65,97},{97,65},{2,34}... | collective-permute-start | bytes 1671176 | tf_op jit(solution)/shard_map/ppermute | solution.py:25
  151.4 24.2 %collective-permute-start.27 = (bf16[408,512]{1,0:T(8,128)(2,1)S(1)}, bf16[408,512]{1,0:T(8,128)(2,1)S(1)}, u32[]{:S(2)}, u32[]{:S(2)}) collective-permute-start(bf16[408,512]{1,0:T(8,128)(2,1)S(1)} %get-tuple-element.127.refs_0_), channel_id=1, source_target_pairs={{0,32},{32,0},{64,96},{96,64},{1,33},{33,1},{65,97},{97,65},{2,34}... | collective-permute-start | bytes 1253384 | tf_op jit(solution)/shard_map/ppermute | solution.py:25
  153.3 22.3 %collective-permute-start.29 = (bf16[408,512]{1,0:T(8,128)(2,1)S(1)}, bf16[408,512]{1,0:T(8,128)(2,1)S(1)}, u32[]{:S(2)}, u32[]{:S(2)}) collective-permute-start(bf16[408,512]{1,0:T(8,128)(2,1)S(1)} %collective-permute-done.28.refs_2_), channel_id=1, source_target_pairs={{0,32},{32,0},{64,96},{96,64},{1,33},{33,1},{65,97},{97,65},{2,34}... | collective-permute-start | bytes 1253384 | tf_op jit(solution)/shard_map/ppermute | solution.py:25
  166.5 6.8 %collective-permute-start.31 = (bf16[136,512]{1,0:T(8,128)(2,1)S(1)}, bf16[136,512]{1,0:T(8,128)(2,1)S(1)}, u32[]{:S(2)}, u32[]{:S(2)}) collective-permute-start(bf16[136,512]{1,0:T(8,128)(2,1)S(1)} %get-tuple-element.130.refs_4_), channel_id=1, source_target_pairs={{0,64},{32,96},{64,0},{96,32},{1,65},{33,97},{65,1},{97,33},{2,66}... | collective-permute-start | bytes 417800 | tf_op jit(solution)/shard_map/ppermute | solution.py:25
  167.3 8.2 %collective-permute-start.30 = (bf16[136,512]{1,0:T(8,128)(2,1)S(1)}, bf16[136,512]{1,0:T(8,128)(2,1)S(1)}, u32[]{:S(2)}, u32[]{:S(2)}) collective-permute-start(bf16[136,512]{1,0:T(8,128)(2,1)S(1)} %get-tuple-element.130.refs_4_), channel_id=1, source_target_pairs={{0,32},{32,0},{64,96},{96,64},{1,33},{33,1},{65,97},{97,65},{2,34}... | collective-permute-start | bytes 417800 | tf_op jit(solution)/shard_map/ppermute | solution.py:25
  (29 other events, 401.2 us)

commit v5 on v4

--- a/solution.py
+++ b/solution.py
@@ -874,12 +874,15 @@
         n_side = swap(normed, "head", 1)
         n_far = swap(normed, "head", 2)
         if t1 == length:
+            sent[1][2] = after(sent[1][2], normed)
+            sent[1].append(swap(sent[1][2], "head", 1))
             result = project_result(
                 place, counts, spots, sent[0], late, (256,), 0, None, length, slots
             )
             n_far = after(n_far, result[1])
-        n_far_side = swap(n_far, "head", 1)
-        sent.append([normed, n_side, n_far, n_far_side])
+        sent.append([normed, n_side, n_far])
+        if t0 == 0 or t1 == length:
+            sent[-1].append(swap(n_far, "head", 1))
         t0 = t1
     prompt_hidden, decode_hidden = project_result(
         place, counts, spots, sent[1] + sent[2], late, (192, 64), 256, result, length, slots

time: 181 us -> 178 us (0.983)
  starting transfers between devices: 54.4 us -> 48.5 us
  waiting for transfers between devices: 16.9 us -> 20.2 us
    ppermute x36, starting transfers between devices: 54.4 us -> 48.5 us  [swap(): return lax.ppermute(a, names, [(i, i ^ bits) for i in range(sizes[axes])])]
    ppermute x36, waiting for transfers between devices: 16.9 us -> 20.2 us  [swap(): return lax.ppermute(a, names, [(i, i ^ bits) for i in range(sizes[axes])])]
  transfers between devices with their start and end apart: 36 -> 36, of which waited for: 11 -> 11; matrix products, arithmetic and copies ran while one was open for 1% -> 1% of each run, Pallas kernels for 40% -> 41%
where the time goes in v5:
time: 178 us
  Pallas kernels  104 us (58%)
  starting transfers between devices  48.5 us (27%)
  waiting for transfers between devices  20.2 us (11%)
  other arithmetic  2.14 us (1%)
    ppermute x36, starting transfers between devices, swap(): return lax.ppermute(a, names, [(i, i ^ bits) for i in range(sizes[axes])])  48.5 us
    pallas_call x3, Pallas kernels, wkv(): pl.pallas_call(functools.partial(wkv_kernel, t0=t0, span=span, slot0=c0 *...  38.2 us
    pallas_call x4, Pallas kernels, mix(): pl.pallas_call(functools.partial(mix_kernel, d=d, length=length), out_sha...  24.1 us
    ppermute x36, waiting for transfers between devices, swap(): return lax.ppermute(a, names, [(i, i ^ bits) for i in range(sizes[axes])])  20.2 us
    pallas_call x1, Pallas kernels, project_rkv(): pl.pallas_call(rkv_kernel, out_shape=jax.ShapeDtypeStruct((3, rows, 512),...  13.7 us
    pallas_call x2, Pallas kernels, project_result(): pl.pallas_call(functools.partial(result_kernel, spans=spans, t0=t0, slot0...  8.86 us
    pallas_call x4, Pallas kernels, pack(): pl.pallas_call(functools.partial(pack_kernel, n=n, lot=lot), out_shape=sh...  8.62 us
    pallas_call x1, Pallas kernels, project_gate(): pl.pallas_call(gate_kernel, out_shape=jax.ShapeDtypeStruct((rows, 512), B...  5.97 us
  transfers between devices with their start and end apart: 36, of which 11 were waited for; matrix products, arithmetic and copies ran while one was open for 1% of the time, Pallas kernels for 41%

profile of v5, /device:TPU:1, one launch (start us, length us, event | category | flops | bytes accessed | tf_op | source)
XLA Modules:
  0.0 177.7 jit_solution(17501028504318639343)
XLA Ops:
  0.7 3.0 %split.1 = (bf16[5,16,512]{2,1,0:T(8,128)(2,1)S(1)}, bf16[5,16,512]{2,1,0:T(8,128)(2,1)S(1)}, bf16[5,16,512]{2,1,0:T(8,128)(2,1)S(1)}, bf16[5,16,512]{2,1,0:T(8,...) custom-call(s32[4]{0:T(128)S(1)} %pad_add_fusion.place_ref, s32[64]{0:T(128)} %keep_ref.7, ...), custom_call_target="tpu_custom_call" | custom-call | tf_op jit(solution)/shard_map/split/pallas_call | solution.py:105
  5.2 3.0 %collective-permute-start = (bf16[5,16,512]{2,1,0:T(8,128)(2,1)S(1)}, bf16[5,16,512]{2,1,0:T(8,128)(2,1)S(1)}, u32[]{:S(2)}, u32[]{:S(2)}) collective-permute-start(bf16[5,16,512]{2,1,0:T(8,128)(2,1)S(1)} %get-tuple-element.74), channel_id=1, source_target_pairs={{0,96},{32,64},{64,32},{96,0},{1,97},{33,65},{65,33},{97,1},{2,98}... | collective-permute-start | bytes 245768 | tf_op jit(solution)/shard_map/ppermute | solution.py:25
  8.9 2.0 %collective-permute-done = bf16[5,16,512]{2,1,0:T(8,128)(2,1)S(1)} collective-permute-done((bf16[5,16,512]{2,1,0:T(8,128)(2,1)S(1)}, bf16[5,16,512]{2,1,0:T(8,128)(2,1)S(1)}, u32[]{:S(2)}, u32[]{:S(2)}) %collective-permute-start) | collective-permute-done | bytes 81952 | tf_op jit(solution)/shard_map/ppermute | solution.py:25
  10.9 2.1 %collective-permute-done.4 = bf16[5,16,512]{2,1,0:T(8,128)(2,1)S(1)} collective-permute-done((bf16[5,16,512]{2,1,0:T(8,128)(2,1)S(1)}, bf16[5,16,512]{2,1,0:T(8,128)(2,1)S(1)}, u32[]{:S(2)}, u32[]{:S(2)}) %collective-permute-start.4) | collective-permute-done | bytes 81952 | tf_op jit(solution)/shard_map/ppermute | solution.py:25
  14.2 3.0 %collective-permute-start.1 = (bf16[1152,512]{1,0:T(8,128)(2,1)S(1)}, bf16[1152,512]{1,0:T(8,128)(2,1)S(1)}, u32[]{:S(2)}, u32[]{:S(2)}) collective-permute-start(bf16[1152,512]{1,0:T(8,128)(2,1)S(1)} %get-tuple-element.75.refs_0_), channel_id=1, source_target_pairs={{0,64},{32,96},{64,0},{96,32},{1,65},{33,97},{65,1},{97,33},{2,66}... | collective-permute-start | bytes 3538952 | tf_op jit(solution)/shard_map/ppermute | solution.py:25
  17.2 5.9 %mix.4 = (bf16[5,1088,2048]{2,1,0:T(8,128)(2,1)}, f32[1088,64]{1,0:T(8,128)S(1)}) custom-call(s32[4]{0:T(128)S(1)} %pad_add_fusion.place_ref, s32[2]{0:T(128)} %count_ref.19, bf16[1152,512]{1,0:T(8,128)(2,1)S(1)} %get-tuple-element.75.refs_0_, f32[5,2048]{1,0:T(8,128)} %refs_1_.9, bf16[64,2048]{1,0:T(8,128)(2,1)} %bitcast.24), custom_call_target="tpu_custom_call" | custom-call | flops 11141120 | bytes 6684672 | tf_op jit(solution)/shard_map/mix/pallas_call | solution.py:280
  25.7 1.6 collective-permute-start.8
  27.3 1.8 %collective-permute-start.9 = (bf16[1,1,5,32,512]{4,3,2,1,0:T(8,128)(2,1)S(1)}, bf16[1,1,5,32,512]{4,3,2,1,0:T(8,128)(2,1)S(1)}, u32[]{:S(2)}, u32[]{:S(2)}) collective-permute-start(bf16[1,1,5,32,512]{4,3,2,1,0:T(8,128)(2,1)S(1)} %get-tuple-element.145.refs_2_), channel_id=1, source_target_pairs={{0,6},{2,4},{4,2},{6,0},{1,7},{3,5},{5,3},{7,1},{8,14},{10,12},{12... | collective-permute-start | bytes 491528 | tf_op jit(solution)/shard_map/ppermute | solution.py:25
  29.1 2.2 %collective-permute-start.10 = (bf16[1,1,5,32,512]{4,3,2,1,0:T(8,128)(2,1)S(1)}, bf16[1,1,5,32,512]{4,3,2,1,0:T(8,128)(2,1)S(1)}, u32[]{:S(2)}, u32[]{:S(2)}) collective-permute-start(bf16[1,1,5,32,512]{4,3,2,1,0:T(8,128)(2,1)S(1)} %get-tuple-element.142.refs_3_), channel_id=1, source_target_pairs={{0,24},{8,16},{16,8},{24,0},{1,25},{9,17},{17,9},{25,1},{2,26},{10... | collective-permute-start | bytes 491528 | tf_op jit(solution)/shard_map/ppermute | solution.py:25
  33.0 1.8 %collective-permute-done.10.refs_7_ = bf16[1,1,5,32,512]{4,3,2,1,0:T(8,128)(2,1)S(1)} collective-permute-done((bf16[1,1,5,32,512]{4,3,2,1,0:T(8,128)(2,1)S(1)}, bf16[1,1,5,32,512]{4,3,2,1,0:T(8,128)(2,1)S(1)}, u32[]{:S(2)}, u32[]{:S(2)}) %collective-permute-start.10) | collective-permute-done | bytes 163872 | tf_op jit(solution)/shard_map/ppermute | solution.py:25
  34.8 2.4 %pack.4 = (bf16[1,2,5,32,512]{4,3,2,1,0:T(8,128)(2,1)S(1)}, bf16[2,1,5,32,512]{4,3,2,1,0:T(8,128)(2,1)S(1)}, bf16[1,2,5,32,512]{4,3,2,1,0:T(8,128)(2,1)S(1)}, bf16[2,1,5,32,512]{4,3,2,1,0:T(8,128)(2,1)S(1)}) custom-call(s32[4]{0:T(128)S(1)} %pad_add_fusion.place_ref, bf16[1,1,5,32,512]{4,3,2,1,0:T(8,128)(2,1)S(1)} %get-tuple-element.143.refs_0_, ...), custom_call_target="tpu_custom_call" | custom-call | bytes 8388608 | tf_op jit(solution)/shard_map/pack/pallas_call | solution.py:179
  38.4 2.4 %collective-permute-start.13 = (bf16[1,2,5,32,512]{4,3,2,1,0:T(8,128)(2,1)S(1)}, bf16[1,2,5,32,512]{4,3,2,1,0:T(8,128)(2,1)S(1)}, u32[]{:S(2)}, u32[]{:S(2)}) collective-permute-start(bf16[1,2,5,32,512]{4,3,2,1,0:T(8,128)(2,1)S(1)} %get-tuple-element.91.refs_2_), channel_id=1, source_target_pairs={{0,24},{8,16},{16,8},{24,0},{1,25},{9,17},{17,9},{25,1},{2,26},{10... | collective-permute-start | bytes 983048 | tf_op jit(solution)/shard_map/ppermute | solution.py:25
  40.8 5.8 %mix.5 = (bf16[5,1088,2048]{2,1,0:T(8,128)(2,1)}, f32[1088,64]{1,0:T(8,128)S(1)}) custom-call(s32[4]{0:T(128)S(1)} %pad_add_fusion.place_ref, s32[2]{0:T(128)} %count_ref.19, bf16[1152,512]{1,0:T(8,128)(2,1)S(1)} %collective-permute-done.6.refs_0_, f32[5,2048]{1,0:T(8,128)} %refs_1_.9, bf16[64,2048]{1,0:T(8,128)(2,1)} %bitcast.25, ...), custom_call_target="tpu_custom_call", output_to_operand_aliasing={{0}: (6, {})} | custom-call | flops 11141120 | bytes 6684672 | tf_op jit(solution)/shard_map/mix/pallas_call | solution.py:280
  51.3 7.4 %collective-permute-start.2 = (bf16[1152,512]{1,0:T(8,128)(2,1)S(1)}, bf16[1152,512]{1,0:T(8,128)(2,1)S(1)}, u32[]{:S(2)}, u32[]{:S(2)}) collective-permute-start(bf16[1152,512]{1,0:T(8,128)(2,1)S(1)} %collective-permute-done.1.refs_0_), channel_id=1, source_target_pairs={{0,32},{32,0},{64,96},{96,64},{1,33},{33,1},{65,97},{97,65},{2,34}... | collective-permute-start | bytes 3538952 | tf_op jit(solution)/shard_map/ppermute | solution.py:25
  58.6 5.8 %mix.6 = (bf16[5,1088,2048]{2,1,0:T(8,128)(2,1)}, f32[1088,64]{1,0:T(8,128)S(1)}) custom-call(s32[4]{0:T(128)S(1)} %pad_add_fusion.place_ref, s32[2]{0:T(128)} %count_ref.19, bf16[1152,512]{1,0:T(8,128)(2,1)S(1)} %collective-permute-done.1.refs_0_, f32[5,2048]{1,0:T(8,128)} %refs_1_.9, bf16[64,2048]{1,0:T(8,128)(2,1)} %bitcast.26, ...), custom_call_target="tpu_custom_call", output_to_operand_aliasing={{0}: (6, {})} | custom-call | flops 11141120 | bytes 6684672 | tf_op jit(solution)/shard_map/mix/pallas_call | solution.py:280
  66.0 2.6 %pack.6 = (bf16[2,4,3,32,512]{4,3,2,1,0:T(8,128)(2,1)S(1)}, bf16[4,2,3,32,512]{4,3,2,1,0:T(8,128)(2,1)S(1)}, bf16[2,4,3,32,512]{4,3,2,1,0:T(8,128)(2,1)S(1)}, bf16[4,2,3,32,512]{4,3,2,1,0:T(8,128)(2,1)S(1)}) custom-call(s32[4]{0:T(128)S(1)} %pad_add_fusion.place_ref, bf16[2,2,5,32,512]{4,3,2,1,0:T(8,128)(2,1)} %copy-done.8, ...), custom_call_target="tpu_custom_call" | custom-call | bytes 8388608 | tf_op jit(solution)/shard_map/pack/pallas_call | solution.py:179
  68.6 2.4 %collective-permute-start.19 = (bf16[2,4,3,32,512]{4,3,2,1,0:T(8,128)(2,1)S(1)}, bf16[2,4,3,32,512]{4,3,2,1,0:T(8,128)(2,1)S(1)}, u32[]{:S(2)}, u32[]{:S(2)}) collective-permute-start(bf16[2,4,3,32,512]{4,3,2,1,0:T(8,128)(2,1)S(1)} %get-tuple-element.105.refs_0_), channel_id=1, source_target_pairs={{0,24},{8,16},{16,8},{24,0},{1,25},{9,17},{17,9},{25,1},{2,26},{10... | collective-permute-start | bytes 2359304 | tf_op jit(solution)/shard_map/ppermute | solution.py:25
  71.1 1.7 collective-permute-start.20
  73.9 6.6 %mix.7 = (bf16[5,1088,2048]{2,1,0:T(8,128)(2,1)}, f32[1088,512]{1,0:T(8,128)S(1)}) custom-call(s32[4]{0:T(128)S(1)} %pad_add_fusion.place_ref, s32[2]{0:T(128)} %count_ref.19, bf16[1152,512]{1,0:T(8,128)(2,1)S(1)} %collective-permute-done.2.refs_0_, f32[5,2048]{1,0:T(8,128)} %refs_1_.9, bf16[64,2048]{1,0:T(8,128)(2,1)} %bitcast.27, ...), custom_call_target="tpu_custom_call", output_to_operand_aliasing={{0}: (6, {})} | custom-call | flops 11141120 | bytes 6684672 | tf_op jit(solution)/shard_map/mix/pallas_call | solution.py:280
  80.5 2.3 %pack.7 = (bf16[2,4,2,32,512]{4,3,2,1,0:T(8,128)(2,1)S(1)}, bf16[4,2,2,32,512]{4,3,2,1,0:T(8,128)(2,1)S(1)}, bf16[2,4,2,32,512]{4,3,2,1,0:T(8,128)(2,1)S(1)}, bf16[4,2,2,32,512]{4,3,2,1,0:T(8,128)(2,1)S(1)}) custom-call(s32[4]{0:T(128)S(1)} %pad_add_fusion.place_ref, bf16[2,2,5,32,512]{4,3,2,1,0:T(8,128)(2,1)} %copy-done.8, ...), custom_call_target="tpu_custom_call" | custom-call | bytes 8388608 | tf_op jit(solution)/shard_map/pack/pallas_call | solution.py:179
  82.8 2.2 %collective-permute-done.19.refs_4_ = bf16[2,4,3,32,512]{4,3,2,1,0:T(8,128)(2,1)S(1)} collective-permute-done((bf16[2,4,3,32,512]{4,3,2,1,0:T(8,128)(2,1)S(1)}, bf16[2,4,3,32,512]{4,3,2,1,0:T(8,128)(2,1)S(1)}, u32[]{:S(2)}, u32[]{:S(2)}) %collective-permute-start.19) | collective-permute-done | bytes 786464 | tf_op jit(solution)/shard_map/ppermute | solution.py:25
  85.0 2.3 %collective-permute-done.20.refs_5_ = bf16[4,2,3,32,512]{4,3,2,1,0:T(8,128)(2,1)S(1)} collective-permute-done((bf16[4,2,3,32,512]{4,3,2,1,0:T(8,128)(2,1)S(1)}, bf16[4,2,3,32,512]{4,3,2,1,0:T(8,128)(2,1)S(1)}, u32[]{:S(2)}, u32[]{:S(2)}) %collective-permute-start.20) | collective-permute-done | bytes 786464 | tf_op jit(solution)/shard_map/ppermute | solution.py:25
  91.5 13.7 %project_rkv.1.refs_0_.refs_1_.refs_2_.refs_5_.refs_6_.refs_7_.refs_13_.refs_14_.refs_15_ = bf16[3,1088,512]{2,1,0:T(8,128)(2,1)} custom-call(s32[4]{0:T(128)S(1)} %pad_add_fusion.place_ref, bf16[5,1088,2048]{2,1,0:T(8,128)(2,1)} %get-tuple-element.87.x_ref, bf16[2,4,3,32,512]{4,3,2,1,0:T(8,128)(2,1)S(1)} %get-tuple-element.105.refs_0_, ...), custom_call_target="tpu_custom_call" | custom-call | flops 6845104128 | bytes 25165824 | tf_op jit(solution)/shard_map/project_rkv/pallas_call | solution.py:327
  105.3 6.0 %project_gate.1.refs_4_.refs_9_.refs_17_ = bf16[1088,512]{1,0:T(8,128)(2,1)S(1)} custom-call(s32[4]{0:T(128)S(1)} %pad_add_fusion.place_ref, bf16[5,1088,2048]{2,1,0:T(8,128)(2,1)} %get-tuple-element.87.x_ref, bf16[2,4,2,32,512]{4,3,2,1,0:T(8,128)(2,1)S(1)} %get-tuple-element.122.refs_0_.refs_4_.refs_8_, ...), custom_call_target="tpu_custom_call" | custom-call | flops 2281701376 | bytes 8388608 | tf_op jit(solution)/shard_map/project_gate/pallas_call | solution.py:361
  111.4 17.5 %wkv.3 = (bf16[544,512]{1,0:T(8,128)(2,1)S(1)}, f32[2,4,128,128]{3,2,1,0:T(8,128)S(1)}, f32[64,8,64,64]{3,2,1,0:T(8,128)}) custom-call(s32[2]{0:T(128)} %count_ref.19, s32[64]{0:T(128)} %keep_ref.7, bf16[456,128]{1,0:T(8,128)(2,1)S(1)} %copy-done.12, ...), custom_call_target="tpu_custom_call" | custom-call | flops 20480000000 | bytes 33554432 | tf_op jit(solution)/shard_map/wkv/pallas_call | solution.py:727
  129.0 2.1 %collective-permute-start.33 = (bf16[544,512]{1,0:T(8,128)(2,1)S(1)}, bf16[544,512]{1,0:T(8,128)(2,1)S(1)}, u32[]{:S(2)}, u32[]{:S(2)}) collective-permute-start(bf16[544,512]{1,0:T(8,128)(2,1)S(1)} %get-tuple-element.133.refs_0_), channel_id=1, source_target_pairs={{0,64},{32,96},{64,0},{96,32},{1,65},{33,97},{65,1},{97,33},{2,66}... | collective-permute-start | bytes 1671176 | tf_op jit(solution)/shard_map/ppermute | solution.py:25
  131.0 14.0 %wkv.4 = (bf16[408,512]{1,0:T(8,128)(2,1)S(1)}, f32[2,4,128,128]{3,2,1,0:T(8,128)S(1)}, f32[64,8,64,64]{3,2,1,0:T(8,128)}) custom-call(s32[2]{0:T(128)} %count_ref.19, s32[64]{0:T(128)} %keep_ref.7, bf16[456,128]{1,0:T(8,128)(2,1)S(1)} %copy-done.12, ...), custom_call_target="tpu_custom_call", output_to_operand_aliasing={{2}: (21, {})} | custom-call | flops 15360000000 | bytes 25165824 | tf_op jit(solution)/shard_map/wkv/pallas_call | solution.py:727
  145.0 5.4 %collective-permute-start.27 = (bf16[408,512]{1,0:T(8,128)(2,1)S(1)}, bf16[408,512]{1,0:T(8,128)(2,1)S(1)}, u32[]{:S(2)}, u32[]{:S(2)}) collective-permute-start(bf16[408,512]{1,0:T(8,128)(2,1)S(1)} %get-tuple-element.128.refs_0_), channel_id=1, source_target_pairs={{0,32},{32,0},{64,96},{96,64},{1,33},{33,1},{65,97},{97,65},{2,34}... | collective-permute-start | bytes 1253384 | tf_op jit(solution)/shard_map/ppermute | solution.py:25
  151.7 6.7 %wkv.5 = (bf16[136,512]{1,0:T(8,128)(2,1)S(1)}, f32[2,4,128,128]{3,2,1,0:T(8,128)}, f32[64,8,64,64]{3,2,1,0:T(8,128)}, f32[2,8,64,64]{3,2,1,0:T(8,128)S(1)}) custom-call(s32[2]{0:T(128)} %count_ref.19, s32[64]{0:T(128)} %keep_ref.7, bf16[456,128]{1,0:T(8,128)(2,1)S(1)} %copy-done.12, ...), custom_call_target="tpu_custom_call", output_to_operand_aliasing={{2}: (21, {})} | custom-call | flops 5120000000 | bytes 8388608 | tf_op jit(solution)/shard_map/wkv/pallas_call | solution.py:727
  158.4 4.7 %collective-permute-done.28.refs_2_ = bf16[408,512]{1,0:T(8,128)(2,1)S(1)} collective-permute-done((bf16[408,512]{1,0:T(8,128)(2,1)S(1)}, bf16[408,512]{1,0:T(8,128)(2,1)S(1)}, u32[]{:S(2)}, u32[]{:S(2)}) %collective-permute-start.28) | collective-permute-done | bytes 417824 | tf_op jit(solution)/shard_map/ppermute | solution.py:25
  165.1 4.4 %project_result.2 = (bf16[2,512,512]{2,1,0:T(8,128)(2,1)}, bf16[64,512]{1,0:T(8,128)(2,1)}) custom-call(s32[4]{0:T(128)S(1)} %pad_add_fusion.place_ref, s32[2]{0:T(128)} %count_ref.19, s32[2]{0:T(128)} %spot_ref.7, bf16[544,512]{1,0:T(8,128)(2,1)S(1)} %get-tuple-element.133.refs_0_, bf16[544,512]{1,0:T(8,128)(2,1)S(1)} %collective-permute-done.32.refs_1_, ...), custom_call_target="tpu_custom_call" | custom-call | flops 1073741824 | bytes 8388608 | tf_op jit(solution)/shard_map/project_result/pallas_call | solution.py:412
  173.1 4.5 %project_result.3 = (bf16[2,512,512]{2,1,0:T(8,128)(2,1)}, bf16[64,512]{1,0:T(8,128)(2,1)}) custom-call(s32[4]{0:T(128)S(1)} %pad_add_fusion.place_ref, s32[2]{0:T(128)} %count_ref.19, s32[2]{0:T(128)} %spot_ref.7, bf16[408,512]{1,0:T(8,128)(2,1)S(1)} %get-tuple-element.128.refs_0_, ...), custom_call_target="tpu_custom_call", output_to_operand_aliasing={{0}: (19, {}), {1}: (20, {})} | custom-call | flops 1073741824 | bytes 8388608 | tf_op jit(solution)/shard_map/project_result/pallas_call | solution.py:412
  (115 shorter events, 27.2 us)
Async XLA Ops:
  3.7 19.4 %collective-permute-start.6 = (bf16[1152,512]{1,0:T(8,128)(2,1)S(1)}, bf16[1152,512]{1,0:T(8,128)(2,1)S(1)}, u32[]{:S(2)}, u32[]{:S(2)}) collective-permute-start(bf16[1152,512]{1,0:T(8,128)(2,1)S(1)} %get-tuple-element.75.refs_0_), channel_id=1, source_target_pairs={{0,32},{32,0},{64,96},{96,64},{1,33},{33,1},{65,97},{97,65},{2,34}... | collective-permute-start | bytes 3538952 | tf_op jit(solution)/shard_map/ppermute | solution.py:25
  5.2 5.7 %collective-permute-start = (bf16[5,16,512]{2,1,0:T(8,128)(2,1)S(1)}, bf16[5,16,512]{2,1,0:T(8,128)(2,1)S(1)}, u32[]{:S(2)}, u32[]{:S(2)}) collective-permute-start(bf16[5,16,512]{2,1,0:T(8,128)(2,1)S(1)} %get-tuple-element.74), channel_id=1, source_target_pairs={{0,96},{32,64},{64,32},{96,0},{1,97},{33,65},{65,33},{97,1},{2,98}... | collective-permute-start | bytes 245768 | tf_op jit(solution)/shard_map/ppermute | solution.py:25
  13.8 9.3 %collective-permute-start.5 = (bf16[4,5,16,512]{3,2,1,0:T(8,128)(2,1)}, bf16[4,5,16,512]{3,2,1,0:T(8,128)(2,1)}, u32[]{:S(2)}, u32[]{:S(2)}) collective-permute-start(bf16[4,5,16,512]{3,2,1,0:T(8,128)(2,1)} %pad_maximum_fusion), channel_id=1, source_target_pairs={{0,1},{1,0},{2,3},{3,2},{4,5},{5,4},{6,7},{7,6},{8,9},{9,8},{10,11... | collective-permute-start | bytes 983048 | tf_op jit(solution)/shard_map/ppermute | solution.py:25
  14.2 37.1 %collective-permute-start.1 = (bf16[1152,512]{1,0:T(8,128)(2,1)S(1)}, bf16[1152,512]{1,0:T(8,128)(2,1)S(1)}, u32[]{:S(2)}, u32[]{:S(2)}) collective-permute-start(bf16[1152,512]{1,0:T(8,128)(2,1)S(1)} %get-tuple-element.75.refs_0_), channel_id=1, source_target_pairs={{0,64},{32,96},{64,0},{96,32},{1,65},{33,97},{65,1},{97,33},{2,66}... | collective-permute-start | bytes 3538952 | tf_op jit(solution)/shard_map/ppermute | solution.py:25
  24.4 7.0 %collective-permute-start.7 = (bf16[1,1,5,32,512]{4,3,2,1,0:T(8,128)(2,1)S(1)}, bf16[1,1,5,32,512]{4,3,2,1,0:T(8,128)(2,1)S(1)}, u32[]{:S(2)}, u32[]{:S(2)}) collective-permute-start(bf16[1,1,5,32,512]{4,3,2,1,0:T(8,128)(2,1)S(1)} %get-tuple-element.143.refs_0_), channel_id=1, source_target_pairs={{0,2},{2,0},{4,6},{6,4},{1,3},{3,1},{5,7},{7,5},{8,10},{10,8},{12,... | collective-permute-start | bytes 491528 | tf_op jit(solution)/shard_map/ppermute | solution.py:25
  25.7 5.7 %collective-permute-start.8 = (bf16[1,1,5,32,512]{4,3,2,1,0:T(8,128)(2,1)S(1)}, bf16[1,1,5,32,512]{4,3,2,1,0:T(8,128)(2,1)S(1)}, u32[]{:S(2)}, u32[]{:S(2)}) collective-permute-start(bf16[1,1,5,32,512]{4,3,2,1,0:T(8,128)(2,1)S(1)} %get-tuple-element.144.refs_1_), channel_id=1, source_target_pairs={{0,8},{8,0},{16,24},{24,16},{1,9},{9,1},{17,25},{25,17},{2,10},{10... | collective-permute-start | bytes 491528 | tf_op jit(solution)/shard_map/ppermute | solution.py:25
  27.3 5.7 %collective-permute-start.9 = (bf16[1,1,5,32,512]{4,3,2,1,0:T(8,128)(2,1)S(1)}, bf16[1,1,5,32,512]{4,3,2,1,0:T(8,128)(2,1)S(1)}, u32[]{:S(2)}, u32[]{:S(2)}) collective-permute-start(bf16[1,1,5,32,512]{4,3,2,1,0:T(8,128)(2,1)S(1)} %get-tuple-element.145.refs_2_), channel_id=1, source_target_pairs={{0,6},{2,4},{4,2},{6,0},{1,7},{3,5},{5,3},{7,1},{8,14},{10,12},{12... | collective-permute-start | bytes 491528 | tf_op jit(solution)/shard_map/ppermute | solution.py:25
  37.2 9.5 %collective-permute-start.11 = (bf16[1,2,5,32,512]{4,3,2,1,0:T(8,128)(2,1)S(1)}, bf16[1,2,5,32,512]{4,3,2,1,0:T(8,128)(2,1)S(1)}, u32[]{:S(2)}, u32[]{:S(2)}) collective-permute-start(bf16[1,2,5,32,512]{4,3,2,1,0:T(8,128)(2,1)S(1)} %get-tuple-element.89.refs_0_), channel_id=1, source_target_pairs={{0,8},{8,0},{16,24},{24,16},{1,9},{9,1},{17,25},{25,17},{2,10},{10... | collective-permute-start | bytes 983048 | tf_op jit(solution)/shard_map/ppermute | solution.py:25
  37.6 9.1 %collective-permute-start.12 = (bf16[2,1,5,32,512]{4,3,2,1,0:T(8,128)(2,1)S(1)}, bf16[2,1,5,32,512]{4,3,2,1,0:T(8,128)(2,1)S(1)}, u32[]{:S(2)}, u32[]{:S(2)}) collective-permute-start(bf16[2,1,5,32,512]{4,3,2,1,0:T(8,128)(2,1)S(1)} %get-tuple-element.90.refs_1_), channel_id=1, source_target_pairs={{0,6},{2,4},{4,2},{6,0},{1,7},{3,5},{5,3},{7,1},{8,14},{10,12},{12... | collective-permute-start | bytes 983048 | tf_op jit(solution)/shard_map/ppermute | solution.py:25
  38.4 8.3 %collective-permute-start.13 = (bf16[1,2,5,32,512]{4,3,2,1,0:T(8,128)(2,1)S(1)}, bf16[1,2,5,32,512]{4,3,2,1,0:T(8,128)(2,1)S(1)}, u32[]{:S(2)}, u32[]{:S(2)}) collective-permute-start(bf16[1,2,5,32,512]{4,3,2,1,0:T(8,128)(2,1)S(1)} %get-tuple-element.91.refs_2_), channel_id=1, source_target_pairs={{0,24},{8,16},{16,8},{24,0},{1,25},{9,17},{17,9},{25,1},{2,26},{10... | collective-permute-start | bytes 983048 | tf_op jit(solution)/shard_map/ppermute | solution.py:25
  40.8 6.2 %collective-permute-start.14 = (bf16[2,1,5,32,512]{4,3,2,1,0:T(8,128)(2,1)S(1)}, bf16[2,1,5,32,512]{4,3,2,1,0:T(8,128)(2,1)S(1)}, u32[]{:S(2)}, u32[]{:S(2)}) collective-permute-start(bf16[2,1,5,32,512]{4,3,2,1,0:T(8,128)(2,1)S(1)} %get-tuple-element.92.refs_3_), channel_id=1, source_target_pairs={{0,2},{2,0},{4,6},{6,4},{1,3},{3,1},{5,7},{7,5},{8,10},{10,8},{12,... | collective-permute-start | bytes 983048 | tf_op jit(solution)/shard_map/ppermute | solution.py:25
  48.5 16.0 %collective-permute-start.15 = (bf16[2,2,5,32,512]{4,3,2,1,0:T(8,128)(2,1)S(1)}, bf16[2,2,5,32,512]{4,3,2,1,0:T(8,128)(2,1)S(1)}, u32[]{:S(2)}, u32[]{:S(2)}) collective-permute-start(bf16[2,2,5,32,512]{4,3,2,1,0:T(8,128)(2,1)S(1)} %get-tuple-element.97.refs_0_), channel_id=1, source_target_pairs={{0,6},{2,4},{4,2},{6,0},{1,7},{3,5},{5,3},{7,1},{8,14},{10,12},{12... | collective-permute-start | bytes 1966088 | tf_op jit(solution)/shard_map/ppermute | solution.py:25
  50.0 14.5 %collective-permute-start.16 = (bf16[2,2,5,32,512]{4,3,2,1,0:T(8,128)(2,1)S(1)}, bf16[2,2,5,32,512]{4,3,2,1,0:T(8,128)(2,1)S(1)}, u32[]{:S(2)}, u32[]{:S(2)}) collective-permute-start(bf16[2,2,5,32,512]{4,3,2,1,0:T(8,128)(2,1)S(1)} %get-tuple-element.98.refs_1_), channel_id=1, source_target_pairs={{0,24},{8,16},{16,8},{24,0},{1,25},{9,17},{17,9},{25,1},{2,26},{10... | collective-permute-start | bytes 1966088 | tf_op jit(solution)/shard_map/ppermute | solution.py:25
  51.2 13.3 %collective-permute-start.17 = (bf16[2,2,5,32,512]{4,3,2,1,0:T(8,128)(2,1)S(1)}, bf16[2,2,5,32,512]{4,3,2,1,0:T(8,128)(2,1)S(1)}, u32[]{:S(2)}, u32[]{:S(2)}) collective-permute-start(bf16[2,2,5,32,512]{4,3,2,1,0:T(8,128)(2,1)S(1)} %get-tuple-element.99.refs_2_), channel_id=1, source_target_pairs={{0,2},{2,0},{4,6},{6,4},{1,3},{3,1},{5,7},{7,5},{8,10},{10,8},{12,... | collective-permute-start | bytes 1966088 | tf_op jit(solution)/shard_map/ppermute | solution.py:25
  51.2 13.3 %collective-permute-start.18 = (bf16[2,2,5,32,512]{4,3,2,1,0:T(8,128)(2,1)S(1)}, bf16[2,2,5,32,512]{4,3,2,1,0:T(8,128)(2,1)S(1)}, u32[]{:S(2)}, u32[]{:S(2)}) collective-permute-start(bf16[2,2,5,32,512]{4,3,2,1,0:T(8,128)(2,1)S(1)} %get-tuple-element.100.refs_3_), channel_id=1, source_target_pairs={{0,8},{8,0},{16,24},{24,16},{1,9},{9,1},{17,25},{25,17},{2,10},{10... | collective-permute-start | bytes 1966088 | tf_op jit(solution)/shard_map/ppermute | solution.py:25
  51.3 22.7 %collective-permute-start.2 = (bf16[1152,512]{1,0:T(8,128)(2,1)S(1)}, bf16[1152,512]{1,0:T(8,128)(2,1)S(1)}, u32[]{:S(2)}, u32[]{:S(2)}) collective-permute-start(bf16[1152,512]{1,0:T(8,128)(2,1)S(1)} %collective-permute-done.1.refs_0_), channel_id=1, source_target_pairs={{0,32},{32,0},{64,96},{96,64},{1,33},{33,1},{65,97},{97,65},{2,34}... | collective-permute-start | bytes 3538952 | tf_op jit(solution)/shard_map/ppermute | solution.py:25
  68.6 16.3 %collective-permute-start.19 = (bf16[2,4,3,32,512]{4,3,2,1,0:T(8,128)(2,1)S(1)}, bf16[2,4,3,32,512]{4,3,2,1,0:T(8,128)(2,1)S(1)}, u32[]{:S(2)}, u32[]{:S(2)}) collective-permute-start(bf16[2,4,3,32,512]{4,3,2,1,0:T(8,128)(2,1)S(1)} %get-tuple-element.105.refs_0_), channel_id=1, source_target_pairs={{0,24},{8,16},{16,8},{24,0},{1,25},{9,17},{17,9},{25,1},{2,26},{10... | collective-permute-start | bytes 2359304 | tf_op jit(solution)/shard_map/ppermute | solution.py:25
  71.1 16.2 %collective-permute-start.20 = (bf16[4,2,3,32,512]{4,3,2,1,0:T(8,128)(2,1)S(1)}, bf16[4,2,3,32,512]{4,3,2,1,0:T(8,128)(2,1)S(1)}, u32[]{:S(2)}, u32[]{:S(2)}) collective-permute-start(bf16[4,2,3,32,512]{4,3,2,1,0:T(8,128)(2,1)S(1)} %get-tuple-element.106.refs_1_), channel_id=1, source_target_pairs={{0,2},{2,0},{4,6},{6,4},{1,3},{3,1},{5,7},{7,5},{8,10},{10,8},{12,... | collective-permute-start | bytes 2359304 | tf_op jit(solution)/shard_map/ppermute | solution.py:25
  72.8 15.6 %collective-permute-start.21 = (bf16[2,4,3,32,512]{4,3,2,1,0:T(8,128)(2,1)S(1)}, bf16[2,4,3,32,512]{4,3,2,1,0:T(8,128)(2,1)S(1)}, u32[]{:S(2)}, u32[]{:S(2)}) collective-permute-start(bf16[2,4,3,32,512]{4,3,2,1,0:T(8,128)(2,1)S(1)} %get-tuple-element.107.refs_2_), channel_id=1, source_target_pairs={{0,8},{8,0},{16,24},{24,16},{1,9},{9,1},{17,25},{25,17},{2,10},{10... | collective-permute-start | bytes 2359304 | tf_op jit(solution)/shard_map/ppermute | solution.py:25
  72.8 16.3 %collective-permute-start.22 = (bf16[4,2,3,32,512]{4,3,2,1,0:T(8,128)(2,1)S(1)}, bf16[4,2,3,32,512]{4,3,2,1,0:T(8,128)(2,1)S(1)}, u32[]{:S(2)}, u32[]{:S(2)}) collective-permute-start(bf16[4,2,3,32,512]{4,3,2,1,0:T(8,128)(2,1)S(1)} %get-tuple-element.108.refs_3_), channel_id=1, source_target_pairs={{0,6},{2,4},{4,2},{6,0},{1,7},{3,5},{5,3},{7,1},{8,14},{10,12},{12... | collective-permute-start | bytes 2359304 | tf_op jit(solution)/shard_map/ppermute | solution.py:25
  89.1 16.2 %collective-permute-start.23 = (bf16[2,4,2,32,512]{4,3,2,1,0:T(8,128)(2,1)S(1)}, bf16[2,4,2,32,512]{4,3,2,1,0:T(8,128)(2,1)S(1)}, u32[]{:S(2)}, u32[]{:S(2)}) collective-permute-start(bf16[2,4,2,32,512]{4,3,2,1,0:T(8,128)(2,1)S(1)} %get-tuple-element.122.refs_0_.refs_4_.refs_8_), channel_id=1, source_target_pairs={{0,24},{8,16},{16,8},{24,0},{1,25},{9,17},{17,9},{25,1},{2,26},{10... | collective-permute-start | bytes 1572872 | tf_op jit(solution)/shard_map/ppermute | solution.py:25
  90.6 14.7 %collective-permute-start.24 = (bf16[4,2,2,32,512]{4,3,2,1,0:T(8,128)(2,1)S(1)}, bf16[4,2,2,32,512]{4,3,2,1,0:T(8,128)(2,1)S(1)}, u32[]{:S(2)}, u32[]{:S(2)}) collective-permute-start(bf16[4,2,2,32,512]{4,3,2,1,0:T(8,128)(2,1)S(1)} %get-tuple-element.123.refs_1_.refs_5_.refs_9_), channel_id=1, source_target_pairs={{0,2},{2,0},{4,6},{6,4},{1,3},{3,1},{5,7},{7,5},{8,10},{10,8},{12,... | collective-permute-start | bytes 1572872 | tf_op jit(solution)/shard_map/ppermute | solution.py:25
  90.6 14.7 %collective-permute-start.25 = (bf16[2,4,2,32,512]{4,3,2,1,0:T(8,128)(2,1)S(1)}, bf16[2,4,2,32,512]{4,3,2,1,0:T(8,128)(2,1)S(1)}, u32[]{:S(2)}, u32[]{:S(2)}) collective-permute-start(bf16[2,4,2,32,512]{4,3,2,1,0:T(8,128)(2,1)S(1)} %get-tuple-element.124.refs_2_.refs_6_.refs_10_), channel_id=1, source_target_pairs={{0,8},{8,0},{16,24},{24,16},{1,9},{9,1},{17,25},{25,17},{2,10},{10... | collective-permute-start | bytes 1572872 | tf_op jit(solution)/shard_map/ppermute | solution.py:25
  90.9 14.4 %collective-permute-start.26 = (bf16[4,2,2,32,512]{4,3,2,1,0:T(8,128)(2,1)S(1)}, bf16[4,2,2,32,512]{4,3,2,1,0:T(8,128)(2,1)S(1)}, u32[]{:S(2)}, u32[]{:S(2)}) collective-permute-start(bf16[4,2,2,32,512]{4,3,2,1,0:T(8,128)(2,1)S(1)} %get-tuple-element.125.refs_3_.refs_7_.refs_11_), channel_id=1, source_target_pairs={{0,6},{2,4},{4,2},{6,0},{1,7},{3,5},{5,3},{7,1},{8,14},{10,12},{12... | collective-permute-start | bytes 1572872 | tf_op jit(solution)/shard_map/ppermute | solution.py:25
  129.0 22.6 %collective-permute-start.33 = (bf16[544,512]{1,0:T(8,128)(2,1)S(1)}, bf16[544,512]{1,0:T(8,128)(2,1)S(1)}, u32[]{:S(2)}, u32[]{:S(2)}) collective-permute-start(bf16[544,512]{1,0:T(8,128)(2,1)S(1)} %get-tuple-element.133.refs_0_), channel_id=1, source_target_pairs={{0,64},{32,96},{64,0},{96,32},{1,65},{33,97},{65,1},{97,33},{2,66}... | collective-permute-start | bytes 1671176 | tf_op jit(solution)/shard_map/ppermute | solution.py:25
  145.0 28.0 %collective-permute-start.27 = (bf16[408,512]{1,0:T(8,128)(2,1)S(1)}, bf16[408,512]{1,0:T(8,128)(2,1)S(1)}, u32[]{:S(2)}, u32[]{:S(2)}) collective-permute-start(bf16[408,512]{1,0:T(8,128)(2,1)S(1)} %get-tuple-element.128.refs_0_), channel_id=1, source_target_pairs={{0,32},{32,0},{64,96},{96,64},{1,33},{33,1},{65,97},{97,65},{2,34}... | collective-permute-start | bytes 1253384 | tf_op jit(solution)/shard_map/ppermute | solution.py:25
  150.4 12.7 %collective-permute-start.28 = (bf16[408,512]{1,0:T(8,128)(2,1)S(1)}, bf16[408,512]{1,0:T(8,128)(2,1)S(1)}, u32[]{:S(2)}, u32[]{:S(2)}) collective-permute-start(bf16[408,512]{1,0:T(8,128)(2,1)S(1)} %get-tuple-element.128.refs_0_), channel_id=1, source_target_pairs={{0,64},{32,96},{64,0},{96,32},{1,65},{33,97},{65,1},{97,33},{2,66}... | collective-permute-start | bytes 1253384 | tf_op jit(solution)/shard_map/ppermute | solution.py:25
  151.2 13.6 %collective-permute-start.32 = (bf16[544,512]{1,0:T(8,128)(2,1)S(1)}, bf16[544,512]{1,0:T(8,128)(2,1)S(1)}, u32[]{:S(2)}, u32[]{:S(2)}) collective-permute-start(bf16[544,512]{1,0:T(8,128)(2,1)S(1)} %get-tuple-element.133.refs_0_), channel_id=1, source_target_pairs={{0,32},{32,0},{64,96},{96,64},{1,33},{33,1},{65,97},{97,65},{2,34}... | collective-permute-start | bytes 1671176 | tf_op jit(solution)/shard_map/ppermute | solution.py:25
  151.6 13.5 %collective-permute-start.34 = (bf16[544,512]{1,0:T(8,128)(2,1)S(1)}, bf16[544,512]{1,0:T(8,128)(2,1)S(1)}, u32[]{:S(2)}, u32[]{:S(2)}) collective-permute-start(bf16[544,512]{1,0:T(8,128)(2,1)S(1)} %collective-permute-done.33.refs_2_), channel_id=1, source_target_pairs={{0,32},{32,0},{64,96},{96,64},{1,33},{33,1},{65,97},{97,65},{2,34}... | collective-permute-start | bytes 1671176 | tf_op jit(solution)/shard_map/ppermute | solution.py:25
  163.1 10.0 %collective-permute-start.29 = (bf16[408,512]{1,0:T(8,128)(2,1)S(1)}, bf16[408,512]{1,0:T(8,128)(2,1)S(1)}, u32[]{:S(2)}, u32[]{:S(2)}) collective-permute-start(bf16[408,512]{1,0:T(8,128)(2,1)S(1)} %collective-permute-done.28.refs_2_), channel_id=1, source_target_pairs={{0,32},{32,0},{64,96},{96,64},{1,33},{33,1},{65,97},{97,65},{2,34}... | collective-permute-start | bytes 1253384 | tf_op jit(solution)/shard_map/ppermute | solution.py:25
  163.9 6.8 %collective-permute-start.31 = (bf16[136,512]{1,0:T(8,128)(2,1)S(1)}, bf16[136,512]{1,0:T(8,128)(2,1)S(1)}, u32[]{:S(2)}, u32[]{:S(2)}) collective-permute-start(bf16[136,512]{1,0:T(8,128)(2,1)S(1)} %get-tuple-element.131.refs_4_), channel_id=1, source_target_pairs={{0,64},{32,96},{64,0},{96,32},{1,65},{33,97},{65,1},{97,33},{2,66}... | collective-permute-start | bytes 417800 | tf_op jit(solution)/shard_map/ppermute | solution.py:25
  164.8 8.2 %collective-permute-start.30 = (bf16[136,512]{1,0:T(8,128)(2,1)S(1)}, bf16[136,512]{1,0:T(8,128)(2,1)S(1)}, u32[]{:S(2)}, u32[]{:S(2)}) collective-permute-start(bf16[136,512]{1,0:T(8,128)(2,1)S(1)} %get-tuple-element.131.refs_4_), channel_id=1, source_target_pairs={{0,32},{32,0},{64,96},{96,64},{1,33},{33,1},{65,97},{97,65},{2,34}... | collective-permute-start | bytes 417800 | tf_op jit(solution)/shard_map/ppermute | solution.py:25
  (29 other events, 401.3 us)

commit v6 on v5

--- a/solution.py
+++ b/solution.py
@@ -874,12 +874,11 @@
         n_side = swap(normed, "head", 1)
         n_far = swap(normed, "head", 2)
         if t1 == length:
-            sent[1][2] = after(sent[1][2], normed)
-            sent[1].append(swap(sent[1][2], "head", 1))
             result = project_result(
                 place, counts, spots, sent[0], late, (256,), 0, None, length, slots
             )
-            n_far = after(n_far, result[1])
+            sent[1][2] = after(sent[1][2], (normed, result[1]))
+            sent[1].append(swap(sent[1][2], "head", 1))
         sent.append([normed, n_side, n_far])
         if t0 == 0 or t1 == length:
             sent[-1].append(swap(n_far, "head", 1))

time: 178 us -> 188 us (1.056)
  starting transfers between devices: 48.5 us -> 55.9 us
  waiting for transfers between devices: 20.2 us -> 22.4 us
    ppermute x36, starting transfers between devices: 48.5 us -> 55.9 us  [swap(): return lax.ppermute(a, names, [(i, i ^ bits) for i in range(sizes[axes])])]
    ppermute x36, waiting for transfers between devices: 20.2 us -> 22.4 us  [swap(): return lax.ppermute(a, names, [(i, i ^ bits) for i in range(sizes[axes])])]
  transfers between devices with their start and end apart: 36 -> 36, of which waited for: 11 -> 11; matrix products, arithmetic and copies ran while one was open for 1% -> 1% of each run, Pallas kernels for 41% -> 39%
where the time goes in v6:
time: 188 us; the launch traced here: 187 us
  Pallas kernels  104 us (55%)
  starting transfers between devices  55.9 us (30%)
  waiting for transfers between devices  22.4 us (12%)
  other arithmetic  2.14 us (1%)
    ppermute x36, starting transfers between devices, swap(): return lax.ppermute(a, names, [(i, i ^ bits) for i in range(sizes[axes])])  55.9 us
    pallas_call x3, Pallas kernels, wkv(): pl.pallas_call(functools.partial(wkv_kernel, t0=t0, span=span, slot0=c0 *...  38.2 us
    pallas_call x4, Pallas kernels, mix(): pl.pallas_call(functools.partial(mix_kernel, d=d, length=length), out_sha...  24.1 us
    ppermute x36, waiting for transfers between devices, swap(): return lax.ppermute(a, names, [(i, i ^ bits) for i in range(sizes[axes])])  22.4 us
    pallas_call x1, Pallas kernels, project_rkv(): pl.pallas_call(rkv_kernel, out_shape=jax.ShapeDtypeStruct((3, rows, 512),...  13.7 us
    pallas_call x2, Pallas kernels, project_result(): pl.pallas_call(functools.partial(result_kernel, spans=spans, t0=t0, slot0...  8.87 us
    pallas_call x4, Pallas kernels, pack(): pl.pallas_call(functools.partial(pack_kernel, n=n, lot=lot), out_shape=sh...  8.62 us
    pallas_call x1, Pallas kernels, project_gate(): pl.pallas_call(gate_kernel, out_shape=jax.ShapeDtypeStruct((rows, 512), B...  5.97 us
  transfers between devices with their start and end apart: 36, of which 11 were waited for; matrix products, arithmetic and copies ran while one was open for 1% of the time, Pallas kernels for 39%

profile of v6, /device:TPU:1, one launch (start us, length us, event | category | flops | bytes accessed | tf_op | source)
XLA Modules:
  0.0 187.3 jit_solution(1955233927850846880)
XLA Ops:
  0.7 3.0 %split.1 = (bf16[5,16,512]{2,1,0:T(8,128)(2,1)S(1)}, bf16[5,16,512]{2,1,0:T(8,128)(2,1)S(1)}, bf16[5,16,512]{2,1,0:T(8,128)(2,1)S(1)}, bf16[5,16,512]{2,1,0:T(8,...) custom-call(s32[4]{0:T(128)S(1)} %pad_add_fusion.place_ref, s32[64]{0:T(128)} %keep_ref.7, ...), custom_call_target="tpu_custom_call" | custom-call | tf_op jit(solution)/shard_map/split/pallas_call | solution.py:105
  5.2 3.0 %collective-permute-start = (bf16[5,16,512]{2,1,0:T(8,128)(2,1)S(1)}, bf16[5,16,512]{2,1,0:T(8,128)(2,1)S(1)}, u32[]{:S(2)}, u32[]{:S(2)}) collective-permute-start(bf16[5,16,512]{2,1,0:T(8,128)(2,1)S(1)} %get-tuple-element.73), channel_id=1, source_target_pairs={{0,96},{32,64},{64,32},{96,0},{1,97},{33,65},{65,33},{97,1},{2,98}... | collective-permute-start | bytes 245768 | tf_op jit(solution)/shard_map/ppermute | solution.py:25
  8.9 2.0 %collective-permute-done = bf16[5,16,512]{2,1,0:T(8,128)(2,1)S(1)} collective-permute-done((bf16[5,16,512]{2,1,0:T(8,128)(2,1)S(1)}, bf16[5,16,512]{2,1,0:T(8,128)(2,1)S(1)}, u32[]{:S(2)}, u32[]{:S(2)}) %collective-permute-start) | collective-permute-done | bytes 81952 | tf_op jit(solution)/shard_map/ppermute | solution.py:25
  10.9 2.1 %collective-permute-done.4 = bf16[5,16,512]{2,1,0:T(8,128)(2,1)S(1)} collective-permute-done((bf16[5,16,512]{2,1,0:T(8,128)(2,1)S(1)}, bf16[5,16,512]{2,1,0:T(8,128)(2,1)S(1)}, u32[]{:S(2)}, u32[]{:S(2)}) %collective-permute-start.4) | collective-permute-done | bytes 81952 | tf_op jit(solution)/shard_map/ppermute | solution.py:25
  14.2 3.0 %collective-permute-start.1 = (bf16[1152,512]{1,0:T(8,128)(2,1)S(1)}, bf16[1152,512]{1,0:T(8,128)(2,1)S(1)}, u32[]{:S(2)}, u32[]{:S(2)}) collective-permute-start(bf16[1152,512]{1,0:T(8,128)(2,1)S(1)} %get-tuple-element.74.refs_0_), channel_id=1, source_target_pairs={{0,64},{32,96},{64,0},{96,32},{1,65},{33,97},{65,1},{97,33},{2,66}... | collective-permute-start | bytes 3538952 | tf_op jit(solution)/shard_map/ppermute | solution.py:25
  17.2 5.9 %mix.4 = (bf16[5,1088,2048]{2,1,0:T(8,128)(2,1)}, f32[1088,64]{1,0:T(8,128)S(1)}) custom-call(s32[4]{0:T(128)S(1)} %pad_add_fusion.place_ref, s32[2]{0:T(128)} %count_ref.19, bf16[1152,512]{1,0:T(8,128)(2,1)S(1)} %get-tuple-element.74.refs_0_, f32[5,2048]{1,0:T(8,128)} %refs_1_.9, bf16[64,2048]{1,0:T(8,128)(2,1)} %bitcast.24), custom_call_target="tpu_custom_call" | custom-call | flops 11141120 | bytes 6684672 | tf_op jit(solution)/shard_map/mix/pallas_call | solution.py:280
  27.3 1.8 collective-permute-start.9
  29.1 2.2 %collective-permute-start.10 = (bf16[1,1,5,32,512]{4,3,2,1,0:T(8,128)(2,1)S(1)}, bf16[1,1,5,32,512]{4,3,2,1,0:T(8,128)(2,1)S(1)}, u32[]{:S(2)}, u32[]{:S(2)}) collective-permute-start(bf16[1,1,5,32,512]{4,3,2,1,0:T(8,128)(2,1)S(1)} %get-tuple-element.140.refs_3_), channel_id=1, source_target_pairs={{0,24},{8,16},{16,8},{24,0},{1,25},{9,17},{17,9},{25,1},{2,26},{10... | collective-permute-start | bytes 491528 | tf_op jit(solution)/shard_map/ppermute | solution.py:25
  34.8 2.4 %pack.4 = (bf16[1,2,5,32,512]{4,3,2,1,0:T(8,128)(2,1)S(1)}, bf16[2,1,5,32,512]{4,3,2,1,0:T(8,128)(2,1)S(1)}, bf16[1,2,5,32,512]{4,3,2,1,0:T(8,128)(2,1)S(1)}, bf16[2,1,5,32,512]{4,3,2,1,0:T(8,128)(2,1)S(1)}) custom-call(s32[4]{0:T(128)S(1)} %pad_add_fusion.place_ref, bf16[1,1,5,32,512]{4,3,2,1,0:T(8,128)(2,1)S(1)} %get-tuple-element.141.refs_0_, ...), custom_call_target="tpu_custom_call" | custom-call | bytes 8388608 | tf_op jit(solution)/shard_map/pack/pallas_call | solution.py:179
  38.4 2.4 %collective-permute-start.13 = (bf16[1,2,5,32,512]{4,3,2,1,0:T(8,128)(2,1)S(1)}, bf16[1,2,5,32,512]{4,3,2,1,0:T(8,128)(2,1)S(1)}, u32[]{:S(2)}, u32[]{:S(2)}) collective-permute-start(bf16[1,2,5,32,512]{4,3,2,1,0:T(8,128)(2,1)S(1)} %get-tuple-element.90.refs_2_), channel_id=1, source_target_pairs={{0,24},{8,16},{16,8},{24,0},{1,25},{9,17},{17,9},{25,1},{2,26},{10... | collective-permute-start | bytes 983048 | tf_op jit(solution)/shard_map/ppermute | solution.py:25
  40.8 5.8 %mix.5 = (bf16[5,1088,2048]{2,1,0:T(8,128)(2,1)}, f32[1088,64]{1,0:T(8,128)S(1)}) custom-call(s32[4]{0:T(128)S(1)} %pad_add_fusion.place_ref, s32[2]{0:T(128)} %count_ref.19, bf16[1152,512]{1,0:T(8,128)(2,1)S(1)} %collective-permute-done.6.refs_0_, f32[5,2048]{1,0:T(8,128)} %refs_1_.9, bf16[64,2048]{1,0:T(8,128)(2,1)} %bitcast.25, ...), custom_call_target="tpu_custom_call", output_to_operand_aliasing={{0}: (6, {})} | custom-call | flops 11141120 | bytes 6684672 | tf_op jit(solution)/shard_map/mix/pallas_call | solution.py:280
  51.3 7.4 %collective-permute-start.2 = (bf16[1152,512]{1,0:T(8,128)(2,1)S(1)}, bf16[1152,512]{1,0:T(8,128)(2,1)S(1)}, u32[]{:S(2)}, u32[]{:S(2)}) collective-permute-start(bf16[1152,512]{1,0:T(8,128)(2,1)S(1)} %collective-permute-done.1.refs_0_), channel_id=1, source_target_pairs={{0,32},{32,0},{64,96},{96,64},{1,33},{33,1},{65,97},{97,65},{2,34}... | collective-permute-start | bytes 3538952 | tf_op jit(solution)/shard_map/ppermute | solution.py:25
  58.6 5.8 %mix.6 = (bf16[5,1088,2048]{2,1,0:T(8,128)(2,1)}, f32[1088,64]{1,0:T(8,128)S(1)}) custom-call(s32[4]{0:T(128)S(1)} %pad_add_fusion.place_ref, s32[2]{0:T(128)} %count_ref.19, bf16[1152,512]{1,0:T(8,128)(2,1)S(1)} %collective-permute-done.1.refs_0_, f32[5,2048]{1,0:T(8,128)} %refs_1_.9, bf16[64,2048]{1,0:T(8,128)(2,1)} %bitcast.26, ...), custom_call_target="tpu_custom_call", output_to_operand_aliasing={{0}: (6, {})} | custom-call | flops 11141120 | bytes 6684672 | tf_op jit(solution)/shard_map/mix/pallas_call | solution.py:280
  66.0 2.6 %pack.6 = (bf16[2,4,3,32,512]{4,3,2,1,0:T(8,128)(2,1)S(1)}, bf16[4,2,3,32,512]{4,3,2,1,0:T(8,128)(2,1)S(1)}, bf16[2,4,3,32,512]{4,3,2,1,0:T(8,128)(2,1)S(1)}, bf16[4,2,3,32,512]{4,3,2,1,0:T(8,128)(2,1)S(1)}) custom-call(s32[4]{0:T(128)S(1)} %pad_add_fusion.place_ref, bf16[2,2,5,32,512]{4,3,2,1,0:T(8,128)(2,1)} %copy-done.8, ...), custom_call_target="tpu_custom_call" | custom-call | bytes 8388608 | tf_op jit(solution)/shard_map/pack/pallas_call | solution.py:179
  68.6 2.4 %collective-permute-start.19 = (bf16[2,4,3,32,512]{4,3,2,1,0:T(8,128)(2,1)S(1)}, bf16[2,4,3,32,512]{4,3,2,1,0:T(8,128)(2,1)S(1)}, u32[]{:S(2)}, u32[]{:S(2)}) collective-permute-start(bf16[2,4,3,32,512]{4,3,2,1,0:T(8,128)(2,1)S(1)} %get-tuple-element.104.refs_0_), channel_id=1, source_target_pairs={{0,24},{8,16},{16,8},{24,0},{1,25},{9,17},{17,9},{25,1},{2,26},{10... | collective-permute-start | bytes 2359304 | tf_op jit(solution)/shard_map/ppermute | solution.py:25
  73.9 6.6 %mix.7 = (bf16[5,1088,2048]{2,1,0:T(8,128)(2,1)}, f32[1088,512]{1,0:T(8,128)S(1)}) custom-call(s32[4]{0:T(128)S(1)} %pad_add_fusion.place_ref, s32[2]{0:T(128)} %count_ref.19, bf16[1152,512]{1,0:T(8,128)(2,1)S(1)} %collective-permute-done.2.refs_0_, f32[5,2048]{1,0:T(8,128)} %refs_1_.9, bf16[64,2048]{1,0:T(8,128)(2,1)} %bitcast.27, ...), custom_call_target="tpu_custom_call", output_to_operand_aliasing={{0}: (6, {})} | custom-call | flops 11141120 | bytes 6684672 | tf_op jit(solution)/shard_map/mix/pallas_call | solution.py:280
  80.5 2.3 %pack.7 = (bf16[2,4,2,32,512]{4,3,2,1,0:T(8,128)(2,1)S(1)}, bf16[4,2,2,32,512]{4,3,2,1,0:T(8,128)(2,1)S(1)}, bf16[2,4,2,32,512]{4,3,2,1,0:T(8,128)(2,1)S(1)}, bf16[4,2,2,32,512]{4,3,2,1,0:T(8,128)(2,1)S(1)}) custom-call(s32[4]{0:T(128)S(1)} %pad_add_fusion.place_ref, bf16[2,2,5,32,512]{4,3,2,1,0:T(8,128)(2,1)} %copy-done.8, ...), custom_call_target="tpu_custom_call" | custom-call | bytes 8388608 | tf_op jit(solution)/shard_map/pack/pallas_call | solution.py:179
  82.8 2.2 %collective-permute-done.19.refs_4_ = bf16[2,4,3,32,512]{4,3,2,1,0:T(8,128)(2,1)S(1)} collective-permute-done((bf16[2,4,3,32,512]{4,3,2,1,0:T(8,128)(2,1)S(1)}, bf16[2,4,3,32,512]{4,3,2,1,0:T(8,128)(2,1)S(1)}, u32[]{:S(2)}, u32[]{:S(2)}) %collective-permute-start.19) | collective-permute-done | bytes 786464 | tf_op jit(solution)/shard_map/ppermute | solution.py:25
  85.0 2.3 %collective-permute-done.20.refs_5_ = bf16[4,2,3,32,512]{4,3,2,1,0:T(8,128)(2,1)S(1)} collective-permute-done((bf16[4,2,3,32,512]{4,3,2,1,0:T(8,128)(2,1)S(1)}, bf16[4,2,3,32,512]{4,3,2,1,0:T(8,128)(2,1)S(1)}, u32[]{:S(2)}, u32[]{:S(2)}) %collective-permute-start.20) | collective-permute-done | bytes 786464 | tf_op jit(solution)/shard_map/ppermute | solution.py:25
  91.5 13.7 %project_rkv.1.refs_0_.refs_1_.refs_2_.refs_5_.refs_6_.refs_7_.refs_13_.refs_14_.refs_15_ = bf16[3,1088,512]{2,1,0:T(8,128)(2,1)} custom-call(s32[4]{0:T(128)S(1)} %pad_add_fusion.place_ref, bf16[5,1088,2048]{2,1,0:T(8,128)(2,1)} %get-tuple-element.86.x_ref, bf16[2,4,3,32,512]{4,3,2,1,0:T(8,128)(2,1)S(1)} %get-tuple-element.104.refs_0_, ...), custom_call_target="tpu_custom_call" | custom-call | flops 6845104128 | bytes 25165824 | tf_op jit(solution)/shard_map/project_rkv/pallas_call | solution.py:327
  105.3 6.0 %project_gate.1.refs_4_.refs_9_.refs_17_ = bf16[1088,512]{1,0:T(8,128)(2,1)S(1)} custom-call(s32[4]{0:T(128)S(1)} %pad_add_fusion.place_ref, bf16[5,1088,2048]{2,1,0:T(8,128)(2,1)} %get-tuple-element.86.x_ref, bf16[2,4,2,32,512]{4,3,2,1,0:T(8,128)(2,1)S(1)} %get-tuple-element.121.refs_0_.refs_4_.refs_8_, ...), custom_call_target="tpu_custom_call" | custom-call | flops 2281701376 | bytes 8388608 | tf_op jit(solution)/shard_map/project_gate/pallas_call | solution.py:361
  111.4 17.5 %wkv.3 = (bf16[544,512]{1,0:T(8,128)(2,1)S(1)}, f32[2,4,128,128]{3,2,1,0:T(8,128)S(1)}, f32[64,8,64,64]{3,2,1,0:T(8,128)}) custom-call(s32[2]{0:T(128)} %count_ref.19, s32[64]{0:T(128)} %keep_ref.7, bf16[456,128]{1,0:T(8,128)(2,1)S(1)} %copy-done.12, ...), custom_call_target="tpu_custom_call" | custom-call | flops 20480000000 | bytes 33554432 | tf_op jit(solution)/shard_map/wkv/pallas_call | solution.py:727
  129.0 2.1 %collective-permute-start.30 = (bf16[544,512]{1,0:T(8,128)(2,1)S(1)}, bf16[544,512]{1,0:T(8,128)(2,1)S(1)}, u32[]{:S(2)}, u32[]{:S(2)}) collective-permute-start(bf16[544,512]{1,0:T(8,128)(2,1)S(1)} %get-tuple-element.131.refs_0_), channel_id=1, source_target_pairs={{0,64},{32,96},{64,0},{96,32},{1,65},{33,97},{65,1},{97,33},{2,66}... | collective-permute-start | bytes 1671176 | tf_op jit(solution)/shard_map/ppermute | solution.py:25
  131.0 5.3 %collective-permute-start.29 = (bf16[544,512]{1,0:T(8,128)(2,1)S(1)}, bf16[544,512]{1,0:T(8,128)(2,1)S(1)}, u32[]{:S(2)}, u32[]{:S(2)}) collective-permute-start(bf16[544,512]{1,0:T(8,128)(2,1)S(1)} %get-tuple-element.131.refs_0_), channel_id=1, source_target_pairs={{0,32},{32,0},{64,96},{96,64},{1,33},{33,1},{65,97},{97,65},{2,34}... | collective-permute-start | bytes 1671176 | tf_op jit(solution)/shard_map/ppermute | solution.py:25
  136.4 3.3 %collective-permute-done.30.refs_2_ = bf16[544,512]{1,0:T(8,128)(2,1)S(1)} collective-permute-done((bf16[544,512]{1,0:T(8,128)(2,1)S(1)}, bf16[544,512]{1,0:T(8,128)(2,1)S(1)}, u32[]{:S(2)}, u32[]{:S(2)}) %collective-permute-start.30) | collective-permute-done | bytes 557088 | tf_op jit(solution)/shard_map/ppermute | solution.py:25
  139.7 5.9 %collective-permute-start.31 = (bf16[544,512]{1,0:T(8,128)(2,1)S(1)}, bf16[544,512]{1,0:T(8,128)(2,1)S(1)}, u32[]{:S(2)}, u32[]{:S(2)}) collective-permute-start(bf16[544,512]{1,0:T(8,128)(2,1)S(1)} %collective-permute-done.30.refs_2_), channel_id=1, source_target_pairs={{0,32},{32,0},{64,96},{96,64},{1,33},{33,1},{65,97},{97,65},{2,34}... | collective-permute-start | bytes 1671176 | tf_op jit(solution)/shard_map/ppermute | solution.py:25
  145.6 14.0 %wkv.4 = (bf16[408,512]{1,0:T(8,128)(2,1)S(1)}, f32[2,4,128,128]{3,2,1,0:T(8,128)S(1)}, f32[64,8,64,64]{3,2,1,0:T(8,128)}) custom-call(s32[2]{0:T(128)} %count_ref.19, s32[64]{0:T(128)} %keep_ref.7, bf16[456,128]{1,0:T(8,128)(2,1)S(1)} %copy-done.12, ...), custom_call_target="tpu_custom_call", output_to_operand_aliasing={{2}: (21, {})} | custom-call | flops 15360000000 | bytes 25165824 | tf_op jit(solution)/shard_map/wkv/pallas_call | solution.py:727
  159.6 2.1 %collective-permute-start.28 = (bf16[408,512]{1,0:T(8,128)(2,1)S(1)}, bf16[408,512]{1,0:T(8,128)(2,1)S(1)}, u32[]{:S(2)}, u32[]{:S(2)}) collective-permute-start(bf16[408,512]{1,0:T(8,128)(2,1)S(1)} %get-tuple-element.127.refs_0_), channel_id=1, source_target_pairs={{0,64},{32,96},{64,0},{96,32},{1,65},{33,97},{65,1},{97,33},{2,66}... | collective-permute-start | bytes 1253384 | tf_op jit(solution)/shard_map/ppermute | solution.py:25
  161.6 6.7 %wkv.5 = (bf16[136,512]{1,0:T(8,128)(2,1)S(1)}, f32[2,4,128,128]{3,2,1,0:T(8,128)}, f32[64,8,64,64]{3,2,1,0:T(8,128)}, f32[2,8,64,64]{3,2,1,0:T(8,128)S(1)}) custom-call(s32[2]{0:T(128)} %count_ref.19, s32[64]{0:T(128)} %keep_ref.7, bf16[456,128]{1,0:T(8,128)(2,1)S(1)} %copy-done.12, ...), custom_call_target="tpu_custom_call", output_to_operand_aliasing={{2}: (21, {})} | custom-call | flops 5120000000 | bytes 8388608 | tf_op jit(solution)/shard_map/wkv/pallas_call | solution.py:727
  168.3 4.4 %project_result.2 = (bf16[2,512,512]{2,1,0:T(8,128)(2,1)}, bf16[64,512]{1,0:T(8,128)(2,1)}) custom-call(s32[4]{0:T(128)S(1)} %pad_add_fusion.place_ref, s32[2]{0:T(128)} %count_ref.19, s32[2]{0:T(128)} %spot_ref.7, bf16[544,512]{1,0:T(8,128)(2,1)S(1)} %get-tuple-element.131.refs_0_, bf16[544,512]{1,0:T(8,128)(2,1)S(1)} %collective-permute-done.29.refs_1_, ...), custom_call_target="tpu_custom_call" | custom-call | flops 1073741824 | bytes 8388608 | tf_op jit(solution)/shard_map/project_result/pallas_call | solution.py:412
  175.5 4.8 %collective-permute-done.34.refs_6_ = bf16[136,512]{1,0:T(8,128)(2,1)S(1)} collective-permute-done((bf16[136,512]{1,0:T(8,128)(2,1)S(1)}, bf16[136,512]{1,0:T(8,128)(2,1)S(1)}, u32[]{:S(2)}, u32[]{:S(2)}) %collective-permute-start.34) | collective-permute-done | bytes 139296 | tf_op jit(solution)/shard_map/ppermute | solution.py:25
  182.7 4.5 %project_result.3 = (bf16[2,512,512]{2,1,0:T(8,128)(2,1)}, bf16[64,512]{1,0:T(8,128)(2,1)}) custom-call(s32[4]{0:T(128)S(1)} %pad_add_fusion.place_ref, s32[2]{0:T(128)} %count_ref.19, s32[2]{0:T(128)} %spot_ref.7, bf16[408,512]{1,0:T(8,128)(2,1)S(1)} %get-tuple-element.127.refs_0_, ...), custom_call_target="tpu_custom_call", output_to_operand_aliasing={{0}: (19, {}), {1}: (20, {})} | custom-call | flops 1073741824 | bytes 8388608 | tf_op jit(solution)/shard_map/project_result/pallas_call | solution.py:412
  (115 shorter events, 30.6 us)
Async XLA Ops:
  3.7 19.4 %collective-permute-start.6 = (bf16[1152,512]{1,0:T(8,128)(2,1)S(1)}, bf16[1152,512]{1,0:T(8,128)(2,1)S(1)}, u32[]{:S(2)}, u32[]{:S(2)}) collective-permute-start(bf16[1152,512]{1,0:T(8,128)(2,1)S(1)} %get-tuple-element.74.refs_0_), channel_id=1, source_target_pairs={{0,32},{32,0},{64,96},{96,64},{1,33},{33,1},{65,97},{97,65},{2,34}... | collective-permute-start | bytes 3538952 | tf_op jit(solution)/shard_map/ppermute | solution.py:25
  5.2 5.7 %collective-permute-start = (bf16[5,16,512]{2,1,0:T(8,128)(2,1)S(1)}, bf16[5,16,512]{2,1,0:T(8,128)(2,1)S(1)}, u32[]{:S(2)}, u32[]{:S(2)}) collective-permute-start(bf16[5,16,512]{2,1,0:T(8,128)(2,1)S(1)} %get-tuple-element.73), channel_id=1, source_target_pairs={{0,96},{32,64},{64,32},{96,0},{1,97},{33,65},{65,33},{97,1},{2,98}... | collective-permute-start | bytes 245768 | tf_op jit(solution)/shard_map/ppermute | solution.py:25
  13.8 9.3 %collective-permute-start.5 = (bf16[4,5,16,512]{3,2,1,0:T(8,128)(2,1)}, bf16[4,5,16,512]{3,2,1,0:T(8,128)(2,1)}, u32[]{:S(2)}, u32[]{:S(2)}) collective-permute-start(bf16[4,5,16,512]{3,2,1,0:T(8,128)(2,1)} %pad_maximum_fusion), channel_id=1, source_target_pairs={{0,1},{1,0},{2,3},{3,2},{4,5},{5,4},{6,7},{7,6},{8,9},{9,8},{10,11... | collective-permute-start | bytes 983048 | tf_op jit(solution)/shard_map/ppermute | solution.py:25
  14.2 37.1 %collective-permute-start.1 = (bf16[1152,512]{1,0:T(8,128)(2,1)S(1)}, bf16[1152,512]{1,0:T(8,128)(2,1)S(1)}, u32[]{:S(2)}, u32[]{:S(2)}) collective-permute-start(bf16[1152,512]{1,0:T(8,128)(2,1)S(1)} %get-tuple-element.74.refs_0_), channel_id=1, source_target_pairs={{0,64},{32,96},{64,0},{96,32},{1,65},{33,97},{65,1},{97,33},{2,66}... | collective-permute-start | bytes 3538952 | tf_op jit(solution)/shard_map/ppermute | solution.py:25
  24.4 7.0 %collective-permute-start.7 = (bf16[1,1,5,32,512]{4,3,2,1,0:T(8,128)(2,1)S(1)}, bf16[1,1,5,32,512]{4,3,2,1,0:T(8,128)(2,1)S(1)}, u32[]{:S(2)}, u32[]{:S(2)}) collective-permute-start(bf16[1,1,5,32,512]{4,3,2,1,0:T(8,128)(2,1)S(1)} %get-tuple-element.141.refs_0_), channel_id=1, source_target_pairs={{0,2},{2,0},{4,6},{6,4},{1,3},{3,1},{5,7},{7,5},{8,10},{10,8},{12,... | collective-permute-start | bytes 491528 | tf_op jit(solution)/shard_map/ppermute | solution.py:25
  25.7 5.7 %collective-permute-start.8 = (bf16[1,1,5,32,512]{4,3,2,1,0:T(8,128)(2,1)S(1)}, bf16[1,1,5,32,512]{4,3,2,1,0:T(8,128)(2,1)S(1)}, u32[]{:S(2)}, u32[]{:S(2)}) collective-permute-start(bf16[1,1,5,32,512]{4,3,2,1,0:T(8,128)(2,1)S(1)} %get-tuple-element.142.refs_1_), channel_id=1, source_target_pairs={{0,8},{8,0},{16,24},{24,16},{1,9},{9,1},{17,25},{25,17},{2,10},{10... | collective-permute-start | bytes 491528 | tf_op jit(solution)/shard_map/ppermute | solution.py:25
  27.3 5.7 %collective-permute-start.9 = (bf16[1,1,5,32,512]{4,3,2,1,0:T(8,128)(2,1)S(1)}, bf16[1,1,5,32,512]{4,3,2,1,0:T(8,128)(2,1)S(1)}, u32[]{:S(2)}, u32[]{:S(2)}) collective-permute-start(bf16[1,1,5,32,512]{4,3,2,1,0:T(8,128)(2,1)S(1)} %get-tuple-element.143.refs_2_), channel_id=1, source_target_pairs={{0,6},{2,4},{4,2},{6,0},{1,7},{3,5},{5,3},{7,1},{8,14},{10,12},{12... | collective-permute-start | bytes 491528 | tf_op jit(solution)/shard_map/ppermute | solution.py:25
  37.2 9.5 %collective-permute-start.11 = (bf16[1,2,5,32,512]{4,3,2,1,0:T(8,128)(2,1)S(1)}, bf16[1,2,5,32,512]{4,3,2,1,0:T(8,128)(2,1)S(1)}, u32[]{:S(2)}, u32[]{:S(2)}) collective-permute-start(bf16[1,2,5,32,512]{4,3,2,1,0:T(8,128)(2,1)S(1)} %get-tuple-element.88.refs_0_), channel_id=1, source_target_pairs={{0,8},{8,0},{16,24},{24,16},{1,9},{9,1},{17,25},{25,17},{2,10},{10... | collective-permute-start | bytes 983048 | tf_op jit(solution)/shard_map/ppermute | solution.py:25
  37.6 9.1 %collective-permute-start.12 = (bf16[2,1,5,32,512]{4,3,2,1,0:T(8,128)(2,1)S(1)}, bf16[2,1,5,32,512]{4,3,2,1,0:T(8,128)(2,1)S(1)}, u32[]{:S(2)}, u32[]{:S(2)}) collective-permute-start(bf16[2,1,5,32,512]{4,3,2,1,0:T(8,128)(2,1)S(1)} %get-tuple-element.89.refs_1_), channel_id=1, source_target_pairs={{0,6},{2,4},{4,2},{6,0},{1,7},{3,5},{5,3},{7,1},{8,14},{10,12},{12... | collective-permute-start | bytes 983048 | tf_op jit(solution)/shard_map/ppermute | solution.py:25
  38.4 8.3 %collective-permute-start.13 = (bf16[1,2,5,32,512]{4,3,2,1,0:T(8,128)(2,1)S(1)}, bf16[1,2,5,32,512]{4,3,2,1,0:T(8,128)(2,1)S(1)}, u32[]{:S(2)}, u32[]{:S(2)}) collective-permute-start(bf16[1,2,5,32,512]{4,3,2,1,0:T(8,128)(2,1)S(1)} %get-tuple-element.90.refs_2_), channel_id=1, source_target_pairs={{0,24},{8,16},{16,8},{24,0},{1,25},{9,17},{17,9},{25,1},{2,26},{10... | collective-permute-start | bytes 983048 | tf_op jit(solution)/shard_map/ppermute | solution.py:25
  40.8 6.2 %collective-permute-start.14 = (bf16[2,1,5,32,512]{4,3,2,1,0:T(8,128)(2,1)S(1)}, bf16[2,1,5,32,512]{4,3,2,1,0:T(8,128)(2,1)S(1)}, u32[]{:S(2)}, u32[]{:S(2)}) collective-permute-start(bf16[2,1,5,32,512]{4,3,2,1,0:T(8,128)(2,1)S(1)} %get-tuple-element.91.refs_3_), channel_id=1, source_target_pairs={{0,2},{2,0},{4,6},{6,4},{1,3},{3,1},{5,7},{7,5},{8,10},{10,8},{12,... | collective-permute-start | bytes 983048 | tf_op jit(solution)/shard_map/ppermute | solution.py:25
  48.5 16.0 %collective-permute-start.15 = (bf16[2,2,5,32,512]{4,3,2,1,0:T(8,128)(2,1)S(1)}, bf16[2,2,5,32,512]{4,3,2,1,0:T(8,128)(2,1)S(1)}, u32[]{:S(2)}, u32[]{:S(2)}) collective-permute-start(bf16[2,2,5,32,512]{4,3,2,1,0:T(8,128)(2,1)S(1)} %get-tuple-element.96.refs_0_), channel_id=1, source_target_pairs={{0,6},{2,4},{4,2},{6,0},{1,7},{3,5},{5,3},{7,1},{8,14},{10,12},{12... | collective-permute-start | bytes 1966088 | tf_op jit(solution)/shard_map/ppermute | solution.py:25
  50.0 14.5 %collective-permute-start.16 = (bf16[2,2,5,32,512]{4,3,2,1,0:T(8,128)(2,1)S(1)}, bf16[2,2,5,32,512]{4,3,2,1,0:T(8,128)(2,1)S(1)}, u32[]{:S(2)}, u32[]{:S(2)}) collective-permute-start(bf16[2,2,5,32,512]{4,3,2,1,0:T(8,128)(2,1)S(1)} %get-tuple-element.97.refs_1_), channel_id=1, source_target_pairs={{0,24},{8,16},{16,8},{24,0},{1,25},{9,17},{17,9},{25,1},{2,26},{10... | collective-permute-start | bytes 1966088 | tf_op jit(solution)/shard_map/ppermute | solution.py:25
  51.2 13.3 %collective-permute-start.17 = (bf16[2,2,5,32,512]{4,3,2,1,0:T(8,128)(2,1)S(1)}, bf16[2,2,5,32,512]{4,3,2,1,0:T(8,128)(2,1)S(1)}, u32[]{:S(2)}, u32[]{:S(2)}) collective-permute-start(bf16[2,2,5,32,512]{4,3,2,1,0:T(8,128)(2,1)S(1)} %get-tuple-element.98.refs_2_), channel_id=1, source_target_pairs={{0,2},{2,0},{4,6},{6,4},{1,3},{3,1},{5,7},{7,5},{8,10},{10,8},{12,... | collective-permute-start | bytes 1966088 | tf_op jit(solution)/shard_map/ppermute | solution.py:25
  51.2 13.3 %collective-permute-start.18 = (bf16[2,2,5,32,512]{4,3,2,1,0:T(8,128)(2,1)S(1)}, bf16[2,2,5,32,512]{4,3,2,1,0:T(8,128)(2,1)S(1)}, u32[]{:S(2)}, u32[]{:S(2)}) collective-permute-start(bf16[2,2,5,32,512]{4,3,2,1,0:T(8,128)(2,1)S(1)} %get-tuple-element.99.refs_3_), channel_id=1, source_target_pairs={{0,8},{8,0},{16,24},{24,16},{1,9},{9,1},{17,25},{25,17},{2,10},{10... | collective-permute-start | bytes 1966088 | tf_op jit(solution)/shard_map/ppermute | solution.py:25
  51.3 22.7 %collective-permute-start.2 = (bf16[1152,512]{1,0:T(8,128)(2,1)S(1)}, bf16[1152,512]{1,0:T(8,128)(2,1)S(1)}, u32[]{:S(2)}, u32[]{:S(2)}) collective-permute-start(bf16[1152,512]{1,0:T(8,128)(2,1)S(1)} %collective-permute-done.1.refs_0_), channel_id=1, source_target_pairs={{0,32},{32,0},{64,96},{96,64},{1,33},{33,1},{65,97},{97,65},{2,34}... | collective-permute-start | bytes 3538952 | tf_op jit(solution)/shard_map/ppermute | solution.py:25
  68.6 16.3 %collective-permute-start.19 = (bf16[2,4,3,32,512]{4,3,2,1,0:T(8,128)(2,1)S(1)}, bf16[2,4,3,32,512]{4,3,2,1,0:T(8,128)(2,1)S(1)}, u32[]{:S(2)}, u32[]{:S(2)}) collective-permute-start(bf16[2,4,3,32,512]{4,3,2,1,0:T(8,128)(2,1)S(1)} %get-tuple-element.104.refs_0_), channel_id=1, source_target_pairs={{0,24},{8,16},{16,8},{24,0},{1,25},{9,17},{17,9},{25,1},{2,26},{10... | collective-permute-start | bytes 2359304 | tf_op jit(solution)/shard_map/ppermute | solution.py:25
  71.1 16.2 %collective-permute-start.20 = (bf16[4,2,3,32,512]{4,3,2,1,0:T(8,128)(2,1)S(1)}, bf16[4,2,3,32,512]{4,3,2,1,0:T(8,128)(2,1)S(1)}, u32[]{:S(2)}, u32[]{:S(2)}) collective-permute-start(bf16[4,2,3,32,512]{4,3,2,1,0:T(8,128)(2,1)S(1)} %get-tuple-element.105.refs_1_), channel_id=1, source_target_pairs={{0,2},{2,0},{4,6},{6,4},{1,3},{3,1},{5,7},{7,5},{8,10},{10,8},{12,... | collective-permute-start | bytes 2359304 | tf_op jit(solution)/shard_map/ppermute | solution.py:25
  72.8 15.6 %collective-permute-start.21 = (bf16[2,4,3,32,512]{4,3,2,1,0:T(8,128)(2,1)S(1)}, bf16[2,4,3,32,512]{4,3,2,1,0:T(8,128)(2,1)S(1)}, u32[]{:S(2)}, u32[]{:S(2)}) collective-permute-start(bf16[2,4,3,32,512]{4,3,2,1,0:T(8,128)(2,1)S(1)} %get-tuple-element.106.refs_2_), channel_id=1, source_target_pairs={{0,8},{8,0},{16,24},{24,16},{1,9},{9,1},{17,25},{25,17},{2,10},{10... | collective-permute-start | bytes 2359304 | tf_op jit(solution)/shard_map/ppermute | solution.py:25
  72.8 16.3 %collective-permute-start.22 = (bf16[4,2,3,32,512]{4,3,2,1,0:T(8,128)(2,1)S(1)}, bf16[4,2,3,32,512]{4,3,2,1,0:T(8,128)(2,1)S(1)}, u32[]{:S(2)}, u32[]{:S(2)}) collective-permute-start(bf16[4,2,3,32,512]{4,3,2,1,0:T(8,128)(2,1)S(1)} %get-tuple-element.107.refs_3_), channel_id=1, source_target_pairs={{0,6},{2,4},{4,2},{6,0},{1,7},{3,5},{5,3},{7,1},{8,14},{10,12},{12... | collective-permute-start | bytes 2359304 | tf_op jit(solution)/shard_map/ppermute | solution.py:25
  89.1 16.2 %collective-permute-start.23 = (bf16[2,4,2,32,512]{4,3,2,1,0:T(8,128)(2,1)S(1)}, bf16[2,4,2,32,512]{4,3,2,1,0:T(8,128)(2,1)S(1)}, u32[]{:S(2)}, u32[]{:S(2)}) collective-permute-start(bf16[2,4,2,32,512]{4,3,2,1,0:T(8,128)(2,1)S(1)} %get-tuple-element.121.refs_0_.refs_4_.refs_8_), channel_id=1, source_target_pairs={{0,24},{8,16},{16,8},{24,0},{1,25},{9,17},{17,9},{25,1},{2,26},{10... | collective-permute-start | bytes 1572872 | tf_op jit(solution)/shard_map/ppermute | solution.py:25
  90.6 14.7 %collective-permute-start.24 = (bf16[4,2,2,32,512]{4,3,2,1,0:T(8,128)(2,1)S(1)}, bf16[4,2,2,32,512]{4,3,2,1,0:T(8,128)(2,1)S(1)}, u32[]{:S(2)}, u32[]{:S(2)}) collective-permute-start(bf16[4,2,2,32,512]{4,3,2,1,0:T(8,128)(2,1)S(1)} %get-tuple-element.122.refs_1_.refs_5_.refs_9_), channel_id=1, source_target_pairs={{0,2},{2,0},{4,6},{6,4},{1,3},{3,1},{5,7},{7,5},{8,10},{10,8},{12,... | collective-permute-start | bytes 1572872 | tf_op jit(solution)/shard_map/ppermute | solution.py:25
  90.6 14.7 %collective-permute-start.25 = (bf16[2,4,2,32,512]{4,3,2,1,0:T(8,128)(2,1)S(1)}, bf16[2,4,2,32,512]{4,3,2,1,0:T(8,128)(2,1)S(1)}, u32[]{:S(2)}, u32[]{:S(2)}) collective-permute-start(bf16[2,4,2,32,512]{4,3,2,1,0:T(8,128)(2,1)S(1)} %get-tuple-element.123.refs_2_.refs_6_.refs_10_), channel_id=1, source_target_pairs={{0,8},{8,0},{16,24},{24,16},{1,9},{9,1},{17,25},{25,17},{2,10},{10... | collective-permute-start | bytes 1572872 | tf_op jit(solution)/shard_map/ppermute | solution.py:25
  90.9 14.4 %collective-permute-start.26 = (bf16[4,2,2,32,512]{4,3,2,1,0:T(8,128)(2,1)S(1)}, bf16[4,2,2,32,512]{4,3,2,1,0:T(8,128)(2,1)S(1)}, u32[]{:S(2)}, u32[]{:S(2)}) collective-permute-start(bf16[4,2,2,32,512]{4,3,2,1,0:T(8,128)(2,1)S(1)} %get-tuple-element.124.refs_3_.refs_7_.refs_11_), channel_id=1, source_target_pairs={{0,6},{2,4},{4,2},{6,0},{1,7},{3,5},{5,3},{7,1},{8,14},{10,12},{12... | collective-permute-start | bytes 1572872 | tf_op jit(solution)/shard_map/ppermute | solution.py:25
  129.0 10.8 %collective-permute-start.30 = (bf16[544,512]{1,0:T(8,128)(2,1)S(1)}, bf16[544,512]{1,0:T(8,128)(2,1)S(1)}, u32[]{:S(2)}, u32[]{:S(2)}) collective-permute-start(bf16[544,512]{1,0:T(8,128)(2,1)S(1)} %get-tuple-element.131.refs_0_), channel_id=1, source_target_pairs={{0,64},{32,96},{64,0},{96,32},{1,65},{33,97},{65,1},{97,33},{2,66}... | collective-permute-start | bytes 1671176 | tf_op jit(solution)/shard_map/ppermute | solution.py:25
  131.0 37.3 %collective-permute-start.29 = (bf16[544,512]{1,0:T(8,128)(2,1)S(1)}, bf16[544,512]{1,0:T(8,128)(2,1)S(1)}, u32[]{:S(2)}, u32[]{:S(2)}) collective-permute-start(bf16[544,512]{1,0:T(8,128)(2,1)S(1)} %get-tuple-element.131.refs_0_), channel_id=1, source_target_pairs={{0,32},{32,0},{64,96},{96,64},{1,33},{33,1},{65,97},{97,65},{2,34}... | collective-permute-start | bytes 1671176 | tf_op jit(solution)/shard_map/ppermute | solution.py:25
  139.7 28.6 %collective-permute-start.31 = (bf16[544,512]{1,0:T(8,128)(2,1)S(1)}, bf16[544,512]{1,0:T(8,128)(2,1)S(1)}, u32[]{:S(2)}, u32[]{:S(2)}) collective-permute-start(bf16[544,512]{1,0:T(8,128)(2,1)S(1)} %collective-permute-done.30.refs_2_), channel_id=1, source_target_pairs={{0,32},{32,0},{64,96},{96,64},{1,33},{33,1},{65,97},{97,65},{2,34}... | collective-permute-start | bytes 1671176 | tf_op jit(solution)/shard_map/ppermute | solution.py:25
  159.6 23.1 %collective-permute-start.27 = (bf16[408,512]{1,0:T(8,128)(2,1)S(1)}, bf16[408,512]{1,0:T(8,128)(2,1)S(1)}, u32[]{:S(2)}, u32[]{:S(2)}) collective-permute-start(bf16[408,512]{1,0:T(8,128)(2,1)S(1)} %get-tuple-element.127.refs_0_), channel_id=1, source_target_pairs={{0,32},{32,0},{64,96},{96,64},{1,33},{33,1},{65,97},{97,65},{2,34}... | collective-permute-start | bytes 1253384 | tf_op jit(solution)/shard_map/ppermute | solution.py:25
  159.6 13.2 %collective-permute-start.28 = (bf16[408,512]{1,0:T(8,128)(2,1)S(1)}, bf16[408,512]{1,0:T(8,128)(2,1)S(1)}, u32[]{:S(2)}, u32[]{:S(2)}) collective-permute-start(bf16[408,512]{1,0:T(8,128)(2,1)S(1)} %get-tuple-element.127.refs_0_), channel_id=1, source_target_pairs={{0,64},{32,96},{64,0},{96,32},{1,65},{33,97},{65,1},{97,33},{2,66}... | collective-permute-start | bytes 1253384 | tf_op jit(solution)/shard_map/ppermute | solution.py:25
  172.8 9.9 %collective-permute-start.32 = (bf16[408,512]{1,0:T(8,128)(2,1)S(1)}, bf16[408,512]{1,0:T(8,128)(2,1)S(1)}, u32[]{:S(2)}, u32[]{:S(2)}) collective-permute-start(bf16[408,512]{1,0:T(8,128)(2,1)S(1)} %collective-permute-done.28.refs_2_), channel_id=1, source_target_pairs={{0,32},{32,0},{64,96},{96,64},{1,33},{33,1},{65,97},{97,65},{2,34}... | collective-permute-start | bytes 1253384 | tf_op jit(solution)/shard_map/ppermute | solution.py:25
  173.6 6.7 %collective-permute-start.34 = (bf16[136,512]{1,0:T(8,128)(2,1)S(1)}, bf16[136,512]{1,0:T(8,128)(2,1)S(1)}, u32[]{:S(2)}, u32[]{:S(2)}) collective-permute-start(bf16[136,512]{1,0:T(8,128)(2,1)S(1)} %get-tuple-element.130.refs_4_), channel_id=1, source_target_pairs={{0,64},{32,96},{64,0},{96,32},{1,65},{33,97},{65,1},{97,33},{2,66}... | collective-permute-start | bytes 417800 | tf_op jit(solution)/shard_map/ppermute | solution.py:25
  175.2 7.5 %collective-permute-start.33 = (bf16[136,512]{1,0:T(8,128)(2,1)S(1)}, bf16[136,512]{1,0:T(8,128)(2,1)S(1)}, u32[]{:S(2)}, u32[]{:S(2)}) collective-permute-start(bf16[136,512]{1,0:T(8,128)(2,1)S(1)} %get-tuple-element.130.refs_4_), channel_id=1, source_target_pairs={{0,32},{32,0},{64,96},{96,64},{1,33},{33,1},{65,97},{97,65},{2,34}... | collective-permute-start | bytes 417800 | tf_op jit(solution)/shard_map/ppermute | solution.py:25
  (29 other events, 401.3 us)
